TPU v7x, 32 devices: a whole 2x2x4 slice. The times are simulated.
32 devices in a mesh: gx: 8 (over z, x), gy: 4 (over y, core).
Axes of the slice: x: 2, y: 2, z: 4, core: 2. Of those that a mesh axis runs over, the one named last changes fastest.
Arguments:
- state: float32 [9, 56, 8192], P(None, None, ('gx', 'gy')), may hold values from -6 to 6
- star: float32 [3, 9, 9, 8192], P(None, None, None, ('gx', 'gy')), may hold values from -1.5 to 1.5
- deriv: float32 [3, 56, 56], replicated, may hold values from -0.75 to 0.75
- trace_ops: float32 [4, 56, 21], replicated, may hold values from -0.75 to 0.75
- lift: float32 [4, 21, 56], replicated, may hold values from -1.25 to 1.25
- face_flux: float32 [4, 9, 9, 8192], P(None, None, None, ('gx', 'gy')), may hold values from -0.3 to 0.3
- orient: int32 [4, 8192], P(None, ('gx', 'gy')), may hold values from 0 to 2
- neighbours: int32 [4, 8192], P(None, ('gx', 'gy')), may hold values from 0 to 1536, as said below
- send_faces: int32 [8, 4, 4, 128], P('gx', 'gy'), may hold values from 0 to 1023, as said below
- sea_faces: int32 [4096], P(('gx', 'gy')), may hold values from 0 to 1023
- sea_owner: int32 [4096, 1], P(('gx', 'gy')), may hold values from 0 to 31; in each aligned block of 128 rows (0 to 127, 128 to 255, ...) at most 4 rows name the same one
- sea_blocks: int32 [4096], P(('gx', 'gy')), may hold values from 0 to 255
- sea_weights: float32 [21, 4096, 256], P(None, ('gx', 'gy')), may hold values from -0.6 to 0.6
- depth: float32 [2048, 1024], P('gx', 'gy'), may hold values from 1 to 3
- wet: int32 [2048, 1024], P('gx', 'gy'), may hold values 0 or 1
- sea_state: float32 [3, 2048, 1024], P(None, 'gx', 'gy'), may hold values from -0.6 to 0.6
Outputs:
- elastic: float32 [9, 56, 8192], P(None, None, ('gx', 'gy'))
- ocean: float32 [3, 2048, 1024], P(None, 'gx', 'gy')
Inputs may be any that keep to these rules, and one draw needn't show every extreme that they name: `neighbours`: A code below 1024 names a face of the same device, paired both ways; 1024 + k * 128 + s names the face in slot s of the back-pointing list of the grid neighbour in direction k, which lists this face in its slot s; 1536 marks a face at the edge of the device grid. `send_faces`: local face codes; each face of a device stands in at most one of its lists, once. `sea_faces`: local face codes. `sea_owner`: the flat index of a device, gx index times the gy axis's length plus gy index; among the 128 rows of one device at most 4 name the same owner, and some owner is named 4 times.
All inputs are finite; a program needn't handle non-finite values. No bound on the sum of `wet` on one device may be relied on, other than what follows from the above.
Results may differ from a plain program's by a relative error of at most 0.0001.
Values sent between devices are 32-bit elements; how exact they have to be, the bound alone decides.
No kernel may reach another device: no remote copies, remote signals or barrier semaphores. Data moves between devices by JAX's collectives and lax.ppermute only.
A program may use at most 128 MiB of HBM per device.

v0:
```python
import math

import jax
import jax.numpy as jnp
import numpy as np
from jax import lax
from jax.experimental import pallas as pl
from jax.experimental.pallas import tpu as pltpu
from jax.sharding import PartitionSpec as P


ORDER = 6
STEPS = 2
BS = 16
HALF = 32
SPREAD = 8.0
COURANT = 0.25
LANES = 128
HALO_X = 40
HALO_Y = 34
EDGE = 8
SEA_ROWS = 16
F32 = jnp.float32
BF16 = jnp.bfloat16


def node_turns():
    upper = ORDER - 1
    nodes = [(i, j) for i in range(upper + 1) for j in range(upper + 1 - i)]
    once = [nodes.index((pair[1], upper - pair[0] - pair[1])) for pair in nodes]
    twice = [once[once[number]] for number in range(len(nodes))]
    return [list(range(len(nodes))), once, twice]


def pad8(n):
    return -(-n // 8) * 8


def band(out_at, in_at):
    k = np.arange(-HALF, HALF + 1)
    raw = 1.0 / np.cosh(math.pi * k / (2.0 * SPREAD))
    raw = raw / raw.sum()
    diff = in_at[None, :] - out_at[:, None]
    w = np.where(np.abs(diff) <= HALF, raw[np.clip(diff + HALF, 0, 2 * HALF)], 0.0)
    w = w.astype(np.float32)
    hi = w.astype(jnp.bfloat16)
    lo = (w - hi.astype(np.float32)).astype(jnp.bfloat16)
    return hi, lo


def split(x):
    hi = x.astype(BF16)
    lo = (x - hi.astype(F32)).astype(BF16)
    return hi, lo


def mm(a, b):
    return lax.dot_general(a, b, (((1,), (0,)), ((), ())), preferred_element_type=F32)


def mm_tn(a, b):
    return lax.dot_general(a, b, (((0,), (0,)), ((), ())), preferred_element_type=F32)


def mm_nt(a, b):
    return lax.dot_general(a, b, (((1,), (1,)), ((), ())), preferred_element_type=F32)


def iota(shape, dim):
    return lax.broadcasted_iota(jnp.int32, shape, dim)


def hot(mask):
    return jnp.where(mask, 1.0, 0.0).astype(BF16)


HBM = "hbm"


def call(body, outs, scratch, *args, micros, limit=20, held=()):
    def spec(in_hbm):
        return pl.BlockSpec(memory_space=pltpu.HBM if in_hbm else pltpu.VMEM)

    args = [
        pltpu.with_memory_space_constraint(a, pltpu.HBM) if i in held else a
        for i, a in enumerate(args)
    ]
    return pl.pallas_call(
        body,
        in_specs=[spec(i in held) for i in range(len(args))],
        out_specs=[spec(len(o) == 3) for o in outs],
        out_shape=[(pltpu.HBM if len(o) == 3 else jax.ShapeDtypeStruct)(o[0], o[1]) for o in outs],
        scratch_shapes=[pltpu.VMEM(*x) if isinstance(x, tuple) else x for x in scratch],
        compiler_params=pltpu.CompilerParams(vmem_limit_bytes=limit * 2**20),
        cost_estimate=pl.CostEstimate(
            flops=micros * 10**8, bytes_accessed=micros * 3 * 10**6, transcendentals=0
        ),
    )(*args)


def sems(count):
    return pltpu.SemaphoreType.DMA((count,))


def start(pairs, sem_ref, first=0):
    copies = [
        pltpu.make_async_copy(src, dst, sem_ref.at[first + i])
        for i, (src, dst) in enumerate(pairs)
    ]
    for copy in copies:
        copy.start()
    return copies


def finish(copies):
    for copy in copies:
        copy.wait()


def slots_of(basis):
    kb = -(-basis // 16) * 16
    row, col = iota((basis, 3 * kb), 0), iota((basis, 3 * kb), 1)
    return hot((col == row) | (col == kb + row)), hot(col == 2 * kb + row)


def prep_deriv(deriv_ref, w_ref):
    basis = deriv_ref.shape[1]
    sel_hi, sel_lo = slots_of(basis)
    parts = []
    for d in range(3):
        hi, lo = split(deriv_ref[d])
        parts.append(mm_tn(hi, sel_hi) + mm_tn(lo, sel_lo))
    w_ref[...] = jnp.concatenate(parts, axis=0).astype(BF16)


def staged(ref, stage_ref):
    for n in range(ref.shape[0]):
        stage_ref[n * 4 : (n + 1) * 4, :] = ref[n]
    return split(stage_ref[...])


def prep_trace(trace_ref, place_ref, stage_ref, wt_ref):
    sel_hi, sel_lo = slots_of(trace_ref.shape[2])
    hi, lo = staged(trace_ref, stage_ref)
    hi = mm(place_ref[...], hi).astype(BF16)
    lo = mm(place_ref[...], lo).astype(BF16)
    wt_ref[...] = (mm(hi, sel_hi) + mm(lo, sel_lo)).astype(BF16)


def prep_lift(lift_ref, stage_ref, wl_ref):
    nodes = lift_ref.shape[0]
    np_ = pad8(nodes)
    row, col = iota((4 * nodes, 8 * np_), 0), iota((4 * nodes, 8 * np_), 1)
    at = (row % 4) * np_ + row // 4
    sel = hot((col == at) | (col == 4 * np_ + at))
    hi, lo = staged(lift_ref, stage_ref)
    wl_ref[...] = jnp.concatenate([mm_tn(hi, sel), mm_tn(lo, sel)], axis=0).astype(BF16)


def stacked(x):
    rows = x.shape[0]
    pad = -(-rows // 16) * 16 - rows
    if pad:
        x = jnp.concatenate([x, jnp.zeros((pad, x.shape[1]), F32)], axis=0)
    hi, lo = split(x)
    return jnp.concatenate([hi, lo, hi], axis=0)


def derive(src_ref, star_ref, w_ref, moved_ref, emit):
    variables, basis, elems = src_ref.shape
    for v in range(variables):
        moved_ref[v] = mm(w_ref[...], stacked(src_ref[v]))
    group = 3

    def body(g, carry):
        for h in range(elems // LANES):
            at = slice(h * LANES, (h + 1) * LANES)
            acc = [jnp.zeros((basis, LANES), F32) for _ in range(group)]
            for v in range(variables):
                for d in range(3):
                    m = moved_ref[v, d * basis : (d + 1) * basis, at]
                    for i in range(group):
                        acc[i] = acc[i] + star_ref[g * group + i, v, d : d + 1, at] * m
            for i in range(group):
                emit(g * group + i, at, acc[i])
        return carry

    lax.fori_loop(0, variables // group, body, 0)


def predict(field_ref, star_ref, w_ref, moved_ref, term_ref, integ_ref):
    if field_ref is not term_ref:
        term_ref[...] = field_ref[...]
    integ_ref[...] = term_ref[...]

    def body(k, carry):
        scale = F32(-1.0 / ORDER)
        for o in range(1, ORDER - 1):
            scale = jnp.where(k == o, F32(-1.0 / (o + 1)), scale)

        def emit(u, at, acc):
            value = acc * scale
            term_ref[u, :, at] = value
            integ_ref[u, :, at] = integ_ref[u, :, at] + value

        derive(term_ref, star_ref, w_ref, moved_ref, emit)
        return carry

    lax.fori_loop(1, ORDER, body, 0)


def traces(integ_ref, wt_ref, own_refs):
    variables, _, elems = integ_ref.shape
    np_ = wt_ref.shape[0] // 12
    count = len(own_refs)
    for v in range(variables):
        t = mm(wt_ref[0 : count * 4 * np_, :], stacked(integ_ref[v]))
        for r in range(count):
            for f in range(4):
                own_refs[r][v * np_ : (v + 1) * np_, f * elems : (f + 1) * elems] = t[
                    (r * 4 + f) * np_ : (r * 4 + f + 1) * np_
                ]
    rows = own_refs[0].shape[0]
    for r in range(count):
        if rows > variables * np_:
            own_refs[r][variables * np_ :, :] = jnp.zeros(
                (rows - variables * np_, 4 * elems), F32
            )


def send_gather(own_ref, send_ref, left_ref, outs):
    rows, faces = own_ref.shape
    hi, lo = split(own_ref[...])
    left_ref[0:rows] = hi
    left_ref[rows : 2 * rows] = lo
    slots = send_ref.shape[3]
    for k in range(0, 4, 2):
        picks = jnp.concatenate([send_ref[0, 0, k : k + 1], send_ref[0, 0, k + 1 : k + 2]], axis=1)
        res = mm(left_ref[...], hot(iota((faces, 2 * slots), 0) == picks))
        res = res[:rows] + res[rows:]
        outs[k][0:rows] = res[:, :slots]
        outs[k + 1][0:rows] = res[:, slots:]


def row_of(ref):
    return jnp.concatenate([ref[f : f + 1, :] for f in range(ref.shape[0])], axis=1)


def local_jump(own_refs, source_turn, codes, left_ref, jump_ref):
    rows, faces = own_refs[0].shape
    width = faces // 4
    value = jnp.where(
        source_turn == 1.0,
        own_refs[1][...],
        jnp.where(source_turn == 2.0, own_refs[2][...], own_refs[0][...]),
    )
    hi, lo = split(value)
    left_ref[0:rows] = hi
    left_ref[rows : 2 * rows] = lo
    for q in range(4):
        at = slice(q * width, (q + 1) * width)
        res = mm(left_ref[...], hot(iota((faces, width), 0) == codes[:, at]))
        jump_ref[:, at] = own_refs[0][:, at] - (res[:rows] + res[rows:])


def surface(arrived, slot_turn, codes, jump_ref, flux_m_ref, perm_ref, wl_ref, base_ref, scratch, out_ref):
    left_ref, part_ref, flux_ref = scratch
    rows, faces = jump_ref.shape
    variables, basis, elems = base_ref.shape
    value = jnp.concatenate(arrived, axis=1)
    slots = value.shape[1]
    hi, lo = split(value)
    both = jnp.concatenate([hi, lo], axis=1)
    turned = mm(perm_ref[...], both)
    turn = jnp.concatenate([slot_turn, slot_turn], axis=1)
    chosen = jnp.where(
        turn == 1.0, turned[:rows], jnp.where(turn == 2.0, turned[rows:], both.astype(F32))
    ).astype(BF16)
    left_ref[0:rows] = chosen[:, :slots]
    left_ref[rows : 2 * rows] = chosen[:, slots:]
    for q in range(4):
        at = slice(q * elems, (q + 1) * elems)
        res = mm(left_ref[...], hot(iota((slots, elems), 0) + faces == codes[:, at]))
        part_ref[:, at] = jump_ref[:, at] - (res[:rows] + res[rows:])
    np_ = flux_ref.shape[1] // 4

    group = 3

    def body(g, carry):
        for f in range(4):
            for h in range(elems // LANES):
                here = slice(h * LANES, (h + 1) * LANES)
                wide = slice(f * elems + h * LANES, f * elems + (h + 1) * LANES)
                acc = [jnp.zeros((np_, LANES), F32) for _ in range(group)]
                for v in range(variables):
                    jump = part_ref[v * np_ : (v + 1) * np_, wide]
                    for i in range(group):
                        acc[i] = acc[i] + flux_m_ref[g * group + i, v, f : f + 1, here] * jump
                for i in range(group):
                    flux_ref[g * group + i, f * np_ : (f + 1) * np_, here] = acc[i]
        return carry

    lax.fori_loop(0, variables // group, body, 0)
    for u in range(variables):
        hi, lo = split(flux_ref[u])
        res = mm(wl_ref[...], jnp.concatenate([hi, lo], axis=0))
        out_ref[u] = base_ref[u] - (res[:basis] + res[basis:])


def first_kernel(
    state_hbm, star_hbm, deriv_hbm, trace_hbm, place_hbm, send_hbm, sea_hbm, depth_hbm, wet_hbm,
    w_ref, wt_ref, integ_ref, lifted_ref, o0, o1, o2, o3,
    star_ref, deriv_ref, trace_ref, place_ref, send_ref, own_ref,
    moved_ref, term_ref, left_ref, stage_ref, sea_edge, depth_edge, wet_edge, sem_ref,
):
    urgent = start(
        [(deriv_hbm, deriv_ref), (state_hbm, term_ref), (star_hbm, star_ref)], sem_ref
    )
    later = start(
        [(trace_hbm, trace_ref), (place_hbm, place_ref), (send_hbm, send_ref)], sem_ref, 3
    )
    tall = depth_hbm.shape[0]
    pairs = []
    for side, at in enumerate((pl.ds(0, EDGE), pl.ds(tall - EDGE, EDGE))):
        for j in range(3):
            pairs.append((sea_hbm.at[j, at], sea_edge.at[side, j]))
        pairs.append((depth_hbm.at[at], depth_edge.at[side]))
        pairs.append((wet_hbm.at[at], wet_edge.at[side]))
    later = later + start(pairs, sem_ref, 6)
    finish(urgent[:1])
    prep_deriv(deriv_ref, w_ref)
    finish(urgent[1:])
    predict(term_ref, star_ref, w_ref, moved_ref, term_ref, integ_ref)
    finish(later)
    prep_trace(trace_ref, place_ref, stage_ref, wt_ref)
    traces(integ_ref, wt_ref, (own_ref,))
    send_gather(own_ref, send_ref, left_ref, (o0, o1, o2, o3))
    rows = own_ref.shape[0]
    np_ = lifted_ref.shape[0]
    lifted_ref[...] = own_ref[2 * np_ : 3 * np_, :]
    for side, (out, at) in enumerate(((o0, 0), (o1, EDGE - STEPS))):
        for j in range(5):
            if j < 3:
                edge = sea_edge[side, j]
            else:
                edge = depth_edge[side] if j == 3 else wet_edge[side].astype(F32)
            for h in range(edge.shape[1] // LANES):
                begin = rows + h * SEA_ROWS + j * STEPS
                out[begin : begin + STEPS] = edge[
                    at : at + STEPS, h * LANES : (h + 1) * LANES
                ]


def local_work(
    integ_ref, field_ref, star_ref, w_ref, wt_ref, turn, codes, jump_ref, base_ref,
    own_refs, left_ref, moved_ref,
):
    traces(integ_ref, wt_ref, own_refs)
    local_jump(own_refs, turn, codes, left_ref, jump_ref)

    def emit(u, at, acc):
        base_ref[u, :, at] = field_ref[u, :, at] - acc

    derive(integ_ref, star_ref, w_ref, moved_ref, emit)


def local_first_kernel(
    integ_ref, field_ref, star_ref, w_ref, wt_ref, codes_ref, orient_ref, lift_ref,
    jump_ref, base_ref, slot_ref, wl_ref, turn_out, slot_out, wl_out, w_out, wt_out,
    turn_ref, own0, own1, own2, left_ref, moved_ref, stage_ref, sem_ref,
):
    prep_lift(lift_ref, stage_ref, wl_ref)
    codes = row_of(codes_ref)
    faces = codes.shape[1]
    slots = slot_ref.shape[1]
    turns = jnp.broadcast_to(row_of(orient_ref).astype(F32), (16, faces)).astype(BF16)
    width = faces // 4
    for q in range(4):
        at = slice(q * width, (q + 1) * width)
        turn_ref[:, at] = mm(turns, hot(iota((faces, width), 0) == codes[:, at]))[0:8]
    for q in range(slots // LANES):
        at = slice(q * LANES, (q + 1) * LANES)
        wanted = iota((LANES, faces), 0) + (faces + q * LANES)
        slot_ref[:, at] = mm_nt(turns, hot(wanted == codes))[0:8]
    copies = start(
        [(turn_ref, turn_out), (slot_ref, slot_out), (wl_ref, wl_out), (w_ref, w_out),
         (wt_ref, wt_out)], sem_ref,
    )
    local_work(
        integ_ref, field_ref, star_ref, w_ref, wt_ref, turn_ref[0:1, :], codes, jump_ref, base_ref,
        (own0, own1, own2), left_ref, moved_ref,
    )
    finish(copies)


def second_kernel(
    a0, a1, a2, a3, slot_ref, codes_ref, jump_ref, flux_m_ref, perm_ref, wl_ref, base_ref,
    star_ref, w_ref, wt_ref, send_ref,
    lifted_ref, field_out, integ_out, edge_low, edge_high, s0, s1, s2, s3,
    field_ref, integ_ref, own_ref, o0, o1, o2, o3,
    arr_left_ref, part_ref, flux_ref, moved_ref, term_ref, left_ref, sem_ref,
):
    rows = jump_ref.shape[0]
    tail = pl.ds(rows, a0.shape[0] - rows)
    copies = start([(a0.at[tail], edge_low), (a1.at[tail], edge_high)], sem_ref)
    surface(
        [a[0:rows] for a in (a0, a1, a2, a3)], slot_ref[0:1, :], row_of(codes_ref), jump_ref,
        flux_m_ref, perm_ref, wl_ref, base_ref, (arr_left_ref, part_ref, flux_ref), field_ref,
    )
    copies += start([(field_ref, field_out)], sem_ref, 2)
    predict(field_ref, star_ref, w_ref, moved_ref, term_ref, integ_ref)
    copies += start([(integ_ref, integ_out)], sem_ref, 3)
    traces(integ_ref, wt_ref, (own_ref,))
    np_ = lifted_ref.shape[0]
    lifted_ref[...] = own_ref[2 * np_ : 3 * np_, :]
    send_gather(own_ref, send_ref, left_ref, (o0, o1, o2, o3))
    copies += start([(o0, s0), (o1, s1), (o2, s2), (o3, s3)], sem_ref, 4)
    finish(copies)


def local_second_kernel(
    integ_hbm, field_hbm, star_hbm, w_hbm, wt_hbm, turn_hbm, codes_hbm,
    jump_out, base_out,
    integ_ref, field_ref, star_ref, w_ref, wt_ref, turn_ref, codes_ref, jump_ref, base_ref,
    own0, own1, own2, left_ref, moved_ref, sem_ref,
):
    copies = start(
        [(integ_hbm, integ_ref), (wt_hbm, wt_ref), (turn_hbm, turn_ref), (codes_hbm, codes_ref),
         (star_hbm, star_ref), (w_hbm, w_ref), (field_hbm, field_ref)], sem_ref,
    )
    finish(copies)
    local_work(
        integ_ref, field_ref, star_ref, w_ref, wt_ref, turn_ref[0:1, :], row_of(codes_ref),
        jump_ref, base_ref, (own0, own1, own2), left_ref, moved_ref,
    )
    finish(start([(jump_ref, jump_out), (base_ref, base_out)], sem_ref, 7))


def last_kernel(
    a0, a1, a2, a3, slot_hbm, codes_hbm, jump_hbm, flux_m_hbm, perm_hbm, wl_hbm, base_hbm,
    field_out,
    b0, b1, b2, b3, slot_ref, codes_ref, jump_ref, flux_m_ref, perm_ref, wl_ref, base_ref,
    field_ref, arr_left_ref, part_ref, flux_ref, sem_ref,
):
    copies = start(
        [(a0, b0), (a1, b1), (a2, b2), (a3, b3), (slot_hbm, slot_ref), (perm_hbm, perm_ref),
         (codes_hbm, codes_ref), (jump_hbm, jump_ref), (flux_m_hbm, flux_m_ref),
         (wl_hbm, wl_ref), (base_hbm, base_ref)], sem_ref,
    )
    finish(copies)
    surface(
        [b0[...], b1[...], b2[...], b3[...]], slot_ref[0:1, :], row_of(codes_ref), jump_ref,
        flux_m_ref, perm_ref, wl_ref, base_ref, (arr_left_ref, part_ref, flux_ref), field_ref,
    )
    finish(start([(field_ref, field_out)], sem_ref))


def project_kernel(capacity, nodes, own_a, own_b, faces_ref, owner_ref, blocks_ref, weights_ref, pay_ref, disp_ref, rows_ref):
    np_ = pad8(nodes)
    faces = own_a.shape[1]
    sea_rows, _ = weights_ref.shape[1:]
    both = jnp.concatenate([own_a[...], own_b[...]], axis=0)
    hi, lo = split(both)
    picks = hot(iota((faces, sea_rows), 0) == faces_ref[...])
    disp = mm(jnp.concatenate([hi, lo], axis=0), picks)
    disp = disp[: 2 * np_] + disp[2 * np_ :]
    disp = jnp.concatenate([disp, jnp.zeros((LANES - 2 * np_, sea_rows), F32)], axis=0)
    disp_ref[...] = disp.T
    across = jnp.broadcast_to(owner_ref[...].astype(F32), (sea_rows, sea_rows))
    owner = across.T
    earlier = iota((sea_rows, sea_rows), 0) < iota((sea_rows, sea_rows), 1)
    rank = jnp.sum(jnp.where((owner == across) & earlier, 1.0, 0.0), axis=0, keepdims=True)
    place = (across[0:1, :] * float(capacity) + rank).astype(jnp.int32)
    devs = pay_ref.shape[0]
    total = devs * capacity
    put = hot(iota((total, sea_rows), 0) == place)
    chunk = 32

    def body(c, carry):
        here = pl.ds(pl.multiple_of(c * chunk, chunk), chunk)
        cols = disp_ref[here, :]
        for t in range(STEPS):
            acc = cols[:, t * np_ : t * np_ + 1] * weights_ref[0, here, :]
            for n in range(1, nodes):
                acc = acc + cols[:, t * np_ + n : t * np_ + n + 1] * weights_ref[n, here, :]
            rows_ref[t, here, :] = acc
        return carry

    lax.fori_loop(0, sea_rows // chunk, body, 0)
    twice = jnp.concatenate([put, put], axis=1)
    parts = []
    for t in range(STEPS):
        hi, lo = split(rows_ref[t])
        parts.append(mm(twice, jnp.concatenate([hi, lo], axis=0)))
    labels = jnp.broadcast_to(blocks_ref[...].astype(F32), (LANES, sea_rows)).astype(BF16)
    parts.append(mm_nt(put, labels))
    value = jnp.concatenate(parts, axis=1)
    for d in range(devs):
        pay_ref[d] = value[d * capacity : (d + 1) * capacity]


def raster_kernel(
    pay_hbm, bx_hi_hbm, bx_lo_hbm, by_hi_hbm, by_lo_hbm, ext_hbm, right_hbm, left_hbm,
    uplift_ref, up_ref, down_ref, bx_hi, bx_lo, by_hi, by_lo, ext_ref, right_ref, left_ref,
    pay_ref, got_ref, sem_ref,
):
    urgent = start([(pay_hbm, pay_ref)], sem_ref)
    later = start(
        [(bx_hi_hbm, bx_hi), (bx_lo_hbm, bx_lo), (right_hbm, right_ref), (left_hbm, left_ref),
         (by_hi_hbm, by_hi), (by_lo_hbm, by_lo), (ext_hbm, ext_ref)], sem_ref, 1,
    )
    finish(urgent)
    devs, capacity, _ = pay_ref.shape
    total = devs * capacity
    for d in range(devs):
        got_ref[d * capacity : (d + 1) * capacity] = pay_ref[d]
    tile_x, tile_y = uplift_ref.shape[1:]
    across = tile_y // BS
    cells = BS * BS
    blocks = (tile_x // BS) * across
    labels = got_ref[:, STEPS * cells :].T
    pick = hot(iota((blocks, total), 0) == labels[0:1, :].astype(jnp.int32))
    pick = jnp.concatenate([pick, pick], axis=1)
    by = iota((blocks, cells), 0) % across
    cx = iota((blocks, cells), 1) // BS
    for t in range(STEPS):
        hi, lo = split(got_ref[:, t * cells : (t + 1) * cells])
        x = mm(pick, jnp.concatenate([hi, lo], axis=0))
        step = 1
        while step < BS:
            from_above = pltpu.roll(pltpu.roll(x, blocks - step, 0), BS * step, 1)
            from_below = pltpu.roll(pltpu.roll(x, step, 0), cells - BS * step, 1)
            low_row = (by & step) == 0
            low_col = (cx & step) == 0
            x = jnp.where(low_row == low_col, x, jnp.where(low_row, from_above, from_below))
            step *= 2
        uplift_ref[t] = x
        up_ref[t * HALO_X : (t + 1) * HALO_X] = x[tile_x - HALO_X :, :]
        down_ref[t * HALO_X : (t + 1) * HALO_X] = x[:HALO_X, :]
    finish(later)


def shore_kernel(
    axes, sea_hbm, depth_hbm, wet_hbm, low_hbm, high_hbm,
    ext_out, right_out, left_out,
    ext_ref, wet_ref, low_ref, high_ref, right_ref, left_ref, sem_ref,
):
    tile_x, tile_y = depth_hbm.shape
    body = pl.ds(0, tile_x)
    finish(
        start(
            [(sea_hbm.at[j], ext_ref.at[j, body]) for j in range(3)]
            + [(depth_hbm, ext_ref.at[3, body]), (wet_hbm, wet_ref), (low_hbm, low_ref),
               (high_hbm, high_ref)], sem_ref,
        )
    )
    ext_ref[4, 0:tile_x, :] = wet_ref[...].astype(F32)
    at_x = lax.axis_index(axes[0])
    has_low = at_x > 0
    has_high = at_x < lax.axis_size(axes[0]) - 1

    def edge_of(ref, present, j, before):
        halves = []
        for h in range(tile_y // LANES):
            begin = h * SEA_ROWS + j * STEPS
            halves.append(ref[begin : begin + STEPS, :])
        value = jnp.where(present, jnp.concatenate(halves, axis=1), 0.0)
        blank = jnp.zeros((EDGE - STEPS, tile_y), F32)
        return jnp.concatenate([blank, value] if before else [value, blank], axis=0)

    for j in range(5):
        ext_ref[j, tile_x : tile_x + EDGE, :] = edge_of(high_ref, has_high, j, False)
        ext_ref[j, tile_x + EDGE : tile_x + 2 * EDGE, :] = edge_of(low_ref, has_low, j, True)
    copies = start([(ext_ref, ext_out)], sem_ref)
    lane = iota(right_ref.shape, 1)
    right = jnp.zeros(right_ref.shape, F32)
    left = right
    for j in range(5):
        moved = 2 * HALO_Y + 2 * j
        last = ext_ref[j, :, tile_y - LANES :]
        first = ext_ref[j, :, :LANES]
        right = jnp.where(
            lane >= LANES - moved, right, pltpu.roll(last, LANES - moved, 1)
        )
        left = jnp.where(lane < moved, left, pltpu.roll(first, moved, 1))
    right_ref[...] = right
    left_ref[...] = left
    finish(copies + start([(right_ref, right_out), (left_ref, left_out)], sem_ref, 1))


def along_x_kernel(
    axes, uplift_ref, low_ref, high_ref, b_hi, b_lo, sea_right, sea_left,
    along_ref, right_ref, left_ref,
):
    _, tile_y = uplift_ref.shape[1:]
    at_x = lax.axis_index(axes[0])
    has_low = at_x > 0
    has_high = at_x < lax.axis_size(axes[0]) - 1
    for t in range(STEPS):
        at = slice(t * HALO_X, (t + 1) * HALO_X)
        value = jnp.concatenate(
            [
                uplift_ref[t],
                jnp.where(has_high, high_ref[at, :], 0.0),
                jnp.where(has_low, low_ref[at, :], 0.0),
            ],
            axis=0,
        )
        hi, lo = split(value)
        along_ref[t] = mm(b_hi[...], hi) + mm(b_hi[...], lo) + mm(b_lo[...], hi)
    tall = along_ref.shape[1]
    lane = iota((tall, LANES), 1)
    last = slice(tile_y - LANES, tile_y)
    first = slice(0, LANES)
    right, left = sea_right[...], sea_left[...]
    for t in reversed(range(STEPS)):
        moved = t * HALO_Y
        tail = along_ref[t, :, last]
        head = along_ref[t, :, first]
        if t:
            tail, head = pltpu.roll(tail, LANES - moved, 1), pltpu.roll(head, moved, 1)
        right = jnp.where(lane >= LANES - moved - HALO_Y, tail, right)
        left = jnp.where(lane < moved + HALO_Y, head, left)
    right_ref[...] = right
    left_ref[...] = left


def ocean_kernel(axes, along_ref, ext_ref, low_ref, high_ref, b_hi, b_lo, out_ref):
    tall, tile_y = along_ref.shape[1:]
    tile_x = out_ref.shape[1]
    at_y = lax.axis_index(axes[1])
    low = jnp.where(at_y > 0, low_ref[...], 0.0)
    high = jnp.where(at_y < lax.axis_size(axes[1]) - 1, high_ref[...], 0.0)
    lane = iota((tall, LANES), 1)
    forces = []
    for t in range(STEPS):
        right = pltpu.roll(high, LANES - HALO_Y, 1) if t else high
        left = pltpu.roll(low, HALO_Y, 1) if t else low
        value = jnp.concatenate([along_ref[t], right, left], axis=1)
        hi, lo = split(value)
        forces.append(mm(hi, b_hi[...]) + mm(lo, b_hi[...]) + mm(hi, b_lo[...]))
    fields = []
    for j in range(5):
        moved = 2 * HALO_Y + 2 * j
        edge = jnp.where(
            lane < LANES // 2, pltpu.roll(high, LANES - moved, 1), pltpu.roll(low, moved, 1)
        )
        fields.append(jnp.concatenate([ext_ref[j], edge], axis=1))
    eta, east, north, depth, wet = fields
    rows, cols = eta.shape

    def px(x):
        return pltpu.roll(x, rows - 1, 0)

    def mx(x):
        return pltpu.roll(x, 1, 0)

    def py(x):
        return pltpu.roll(x, cols - 1, 1)

    def my(x):
        return pltpu.roll(x, 1, 1)

    factor = 0.5 * COURANT
    for t in range(STEPS):
        eta = eta + wet * forces[t]
        column = depth + eta
        qx, qy = column * east, column * north
        near = [(px(a), mx(a), py(a), my(a)) for a in (eta, east, north)]
        mean = [0.25 * (a + b + c + d) for a, b, c, d in near]
        eta_x, eta_y = near[0][0] - near[0][1], near[0][2] - near[0][3]
        east_x, east_y = near[1][0] - near[1][1], near[1][2] - near[1][3]
        north_x, north_y = near[2][0] - near[2][1], near[2][2] - near[2][3]
        eta_new = mean[0] - factor * ((px(qx) - mx(qx)) + (py(qy) - my(qy)))
        east_new = mean[1] - factor * (east * east_x + north * east_y + eta_x)
        north_new = mean[2] - factor * (east * north_x + north * north_y + eta_y)
        eta, east, north = eta_new * wet, east_new * wet, north_new * wet
    out_ref[0] = eta[:tile_x, :tile_y]
    out_ref[1] = east[:tile_x, :tile_y]
    out_ref[2] = north[:tile_x, :tile_y]


def shift(value, axis, step):
    count = lax.axis_size(axis)
    return lax.ppermute(value, axis, [(i, (i + step) % count) for i in range(count)])


def on_device(
    state, star, deriv, trace_ops, lift, face_flux, orient, neighbours, send_faces,
    sea_faces, sea_owner, sea_blocks, sea_weights, depth, wet, sea_state,
):
    variables, basis, elems = state.shape
    nodes = trace_ops.shape[2]
    np_ = pad8(nodes)
    faces = 4 * elems
    slots = send_faces.shape[-1]
    rows = -(-variables * np_ // 16) * 16
    kb = -(-basis // 16) * 16
    turns = node_turns()
    place = np.zeros((12 * np_, 4 * nodes), np.float32)
    perm = np.zeros((2 * rows, rows), np.float32)
    for r in range(3):
        for n in range(nodes):
            for f in range(4):
                place[(r * 4 + f) * np_ + n, turns[r][n] * 4 + f] = 1.0
            for v in range(variables):
                if r:
                    perm[(r - 1) * rows + v * np_ + n, v * np_ + turns[r][n]] = 1.0
    place = jnp.asarray(place, BF16)
    perm = jnp.asarray(perm, BF16)
    star = star.transpose(1, 2, 0, 3)
    face_flux = face_flux.transpose(1, 2, 0, 3)
    trace_ops = trace_ops.transpose(2, 0, 1)
    lift = lift.transpose(1, 0, 2)

    wide = (rows, faces)
    out = (rows, slots)
    tile_x, tile_y = depth.shape
    out_x = (rows + (tile_y // LANES) * SEA_ROWS, slots)
    field_shape = (variables, basis, elems)
    moved = ((variables, 3 * basis, elems), F32)
    left = ((2 * rows, faces), BF16)
    arr_left = ((2 * rows, 4 * slots), BF16)
    flux = ((variables, 4 * np_, elems), F32)
    stage = ((4 * nodes, basis), F32)

    def sent(outgoing):
        return [
            shift(outgoing[1], "gx", 1), shift(outgoing[0], "gx", -1),
            shift(outgoing[3], "gy", 1), shift(outgoing[2], "gy", -1),
        ]

    w_of = ((3 * basis, 3 * kb), BF16)
    wt_of = ((12 * np_, 3 * kb), BF16)
    wl_of = ((2 * basis, 8 * np_), BF16)
    turn_of = ((8, faces), F32)
    slot_of = ((8, 4 * slots), F32)
    field_of, wide_of, out_of = (field_shape, F32), (wide, F32), (out, F32)
    star_of, flux_m_of = (star.shape, F32), (face_flux.shape, F32)
    lifted_of = ((np_, faces), F32)
    codes_of = (neighbours.shape, neighbours.dtype)
    perm_of = (perm.shape, BF16)

    def hbm(array):
        return (*array, HBM)

    w, wt, integ, lifted_a, *outgoing = call(
        first_kernel,
        [w_of, wt_of, field_of, lifted_of] + [(out_x, F32)] * 2 + [out_of] * 2,
        [star_of, (deriv.shape, F32), (trace_ops.shape, F32), (place.shape, BF16),
         (send_faces.shape, send_faces.dtype), wide_of, moved, field_of, left, stage,
         ((2, 3, EDGE, tile_y), F32), ((2, EDGE, tile_y), F32), ((2, EDGE, tile_y), wet.dtype),
         sems(16)],
        state, star, deriv, trace_ops, place, send_faces, sea_state, depth, wet,
        micros=10, held=range(9),
    )
    arrived = sent(outgoing)
    jump, base, slot_turn, wl, turn_h, slot_h, wl_h, w_h, wt_h = call(
        local_first_kernel,
        [wide_of, field_of, slot_of, wl_of, hbm(turn_of), hbm(slot_of), hbm(wl_of), hbm(w_of),
         hbm(wt_of)],
        [turn_of, wide_of, wide_of, wide_of, left, moved, stage, sems(5)],
        integ, state, star, w, wt, neighbours, orient, lift,
        micros=4,
    )
    lifted_b, field_h, integ_h, edge_low, edge_high, *outgoing = call(
        second_kernel,
        [lifted_of, hbm(field_of), hbm(field_of)]
        + [((out_x[0] - rows, slots), F32, HBM)] * 2 + [hbm(out_of)] * 4,
        [field_of, field_of, wide_of] + [out_of] * 4
        + [arr_left, wide_of, flux, moved, field_of, left, sems(8)],
        *arrived, slot_turn, neighbours, jump, face_flux, perm, wl, base, star, w, wt,
        send_faces, micros=10,
    )

    sea_rows, cells = sea_weights.shape[1:]
    devs = lax.axis_size("gx") * lax.axis_size("gy")
    capacity = max(2, (sea_rows + devs - 1) // devs)
    message = (devs, capacity, STEPS * cells + LANES)
    payload, = call(
        lambda *refs: project_kernel(capacity, nodes, *refs),
        [(message, F32)],
        [((sea_rows, LANES), F32), ((STEPS, sea_rows, cells), F32)],
        lifted_a, lifted_b, sea_faces.reshape(1, -1), sea_owner.reshape(1, -1),
        sea_blocks.reshape(1, -1), sea_weights, micros=3,
    )
    got = lax.all_to_all(payload, ("gx", "gy"), split_axis=0, concat_axis=0, tiled=True)
    arrived = sent(outgoing)
    tall = tile_x + 2 * EDGE
    axes = ("gx", "gy")
    ext_of = ((5, tall, tile_y), F32)
    strip_of = ((tall, LANES), F32)
    edge_of = (edge_low.shape, F32)
    ext_h, right_h, left_h = call(
        lambda *refs: shore_kernel(axes, *refs),
        [hbm(ext_of), hbm(strip_of), hbm(strip_of)],
        [ext_of, (wet.shape, wet.dtype), edge_of, edge_of, strip_of, strip_of, sems(7)],
        sea_state, depth, wet, edge_low, edge_high, micros=2, held=range(5),
    )
    jump_h, base_h = call(
        local_second_kernel, [hbm(wide_of), hbm(field_of)],
        [field_of, field_of, star_of, w_of, wt_of, turn_of, codes_of, wide_of, field_of,
         wide_of, wide_of, wide_of, left, moved, sems(9)],
        integ_h, field_h, star, w_h, wt_h, turn_h, neighbours,
        micros=5, held=range(7),
    )
    elastic, = call(
        last_kernel, [hbm(field_of)],
        [out_of] * 4 + [slot_of, codes_of, wide_of, flux_m_of, perm_of, wl_of, field_of, field_of,
         arr_left, wide_of, flux, sems(11)],
        *arrived, slot_h, neighbours, jump_h, face_flux, perm, wl_h, base_h,
        micros=4, held=range(11),
    )

    halo = ((STEPS * HALO_X, tile_y), F32)
    cell_x = np.concatenate([np.arange(tile_x + EDGE), np.arange(-EDGE, 0)])
    read_x = np.concatenate([np.arange(tile_x + HALO_X), np.arange(-HALO_X, 0)])
    cell_y = np.concatenate([np.arange(tile_y + LANES // 2), np.arange(-LANES // 2, 0)])
    read_y = np.concatenate([np.arange(tile_y + LANES), np.arange(-LANES, 0)])
    bands = [jnp.asarray(b) for b in band(cell_x, read_x)]
    bands += [jnp.asarray(b.T) for b in band(cell_y, read_y)]
    uplift, up, down, bx_hi, bx_lo, by_hi, by_lo, ext, sea_right, sea_left = call(
        raster_kernel,
        [((STEPS, tile_x, tile_y), F32), halo, halo]
        + [(b.shape, BF16) for b in bands] + [ext_of, strip_of, strip_of],
        [(message, F32), ((devs * capacity, message[2]), F32), sems(8)],
        got, *bands, ext_h, right_h, left_h, micros=3, held=range(8),
    )
    x_low, x_high = shift(up, "gx", 1), shift(down, "gx", -1)
    along, right, left_going = call(
        lambda *refs: along_x_kernel(axes, *refs),
        [((STEPS, tall, tile_y), F32), strip_of, strip_of], [],
        uplift, x_low, x_high, bx_hi, bx_lo, sea_right, sea_left, micros=1,
    )
    y_low, y_high = shift(right, "gy", 1), shift(left_going, "gy", -1)
    ocean, = call(
        lambda *refs: ocean_kernel(axes, *refs), [((3, tile_x, tile_y), F32)], [],
        along, ext, y_low, y_high, by_hi, by_lo, micros=4,
    )
    return elastic, ocean


def solution(mesh):
    both = ("gx", "gy")
    placed = (
        P(None, None, both),
        P(None, None, None, both),
        P(),
        P(),
        P(),
        P(None, None, None, both),
        P(None, both),
        P(None, both),
        P("gx", "gy", None, None),
        P(both),
        P(both, None),
        P(both),
        P(None, both, None),
        P("gx", "gy"),
        P("gx", "gy"),
        P(None, "gx", "gy"),
    )

    return jax.shard_map(
        on_device,
        mesh=mesh,
        in_specs=placed,
        out_specs=(P(None, None, both), P(None, "gx", "gy")),
        check_vma=False,
    )
```

profile of v0, /device:TPU:1, one launch (start us, length us, event | category | flops | bytes accessed | tf_op | source)
XLA Modules:
  0.0 81.1 jit_solution(6654476775053069686)
XLA Ops:
  0.7 0.0 copy-start.6
  0.7 10.4 %shard_map.221 = (bf16[168,192]{1,0:T(8,128)(2,1)S(1)}, bf16[288,192]{1,0:T(8,128)(2,1)S(1)}, f32[9,56,256]{2,1,0:T(8,128)S(1)}, f32[24,1024]{1,0:T(8,128)S(1)},...) custom-call(f32[9,56,256]{2,1,0:T(8,128)} %field_ref.1, ...), custom_call_target="tpu_custom_call" | custom-call | flops 1000000000 | bytes 30000000 | tf_op jit(solution)/shard_map/pallas_call | solution.py:88
  11.1 0.0 copy-start.2
  11.1 0.0 copy-start.4
  11.1 2.1 %collective-permute-start = (f32[256,128]{1,0:T(8,128)S(1)}, f32[256,128]{1,0:T(8,128)S(1)}, u32[]{:S(2)}, u32[]{:S(2)}) collective-permute-start(f32[256,128]{1,0:T(8,128)S(1)} %get-tuple-element.46), channel_id=1, source_target_pairs={{0,4},{4,8},{8,12},{12,16},{16,20},{20,24},{24,28},{28,0},{1,5},{5... | collective-permute-start | bytes 393224 | tf_op jit(solution)/shard_map/ppermute | solution.py:685
  13.2 3.1 %collective-permute-start.1 = (f32[256,128]{1,0:T(8,128)S(1)}, f32[256,128]{1,0:T(8,128)S(1)}, u32[]{:S(2)}, u32[]{:S(2)}) collective-permute-start(f32[256,128]{1,0:T(8,128)S(1)} %get-tuple-element.47), channel_id=1, source_target_pairs={{0,28},{4,0},{8,4},{12,8},{16,12},{20,16},{24,20},{28,24},{1,29},{... | collective-permute-start | bytes 393224 | tf_op jit(solution)/shard_map/ppermute | solution.py:685
  16.3 2.2 %collective-permute-start.2 = (f32[224,128]{1,0:T(8,128)S(1)}, f32[224,128]{1,0:T(8,128)S(1)}, u32[]{:S(2)}, u32[]{:S(2)}) collective-permute-start(f32[224,128]{1,0:T(8,128)S(1)} %get-tuple-element.48), channel_id=1, source_target_pairs={{0,1},{1,2},{2,3},{3,0},{4,5},{5,6},{6,7},{7,4},{8,9},{9,10},{10,1... | collective-permute-start | bytes 344072 | tf_op jit(solution)/shard_map/ppermute | solution.py:685
  18.5 3.8 %shard_map.222 = (f32[224,1024]{1,0:T(8,128)S(1)}, f32[9,56,256]{2,1,0:T(8,128)S(1)}, f32[8,512]{1,0:T(8,128)S(1)}, bf16[112,192]{1,0:T(8,128)(2,1)S(1)}, f32[8,...) custom-call(f32[9,56,256]{2,1,0:T(8,128)S(1)} %get-tuple-element.50., ...), custom_call_target="tpu_custom_call" | custom-call | flops 400000000 | bytes 12000000 | tf_op jit(solution)/shard_map/pallas_call | solution.py:88
  22.4 0.3 collective-permute-done.3.a3
  22.8 11.1 %shard_map.223 = (f32[24,1024]{1,0:T(8,128)S(1)}, f32[9,56,256]{2,1,0:T(8,128)}, f32[9,56,256]{2,1,0:T(8,128)}, f32[32,128]{1,0:T(8,128)}, f32[32,128]{1,0:T(8,1...) custom-call(f32[256,128]{1,0:T(8,128)S(1)} %collective-permute-done.a0, ...), custom_call_target="tpu_custom_call" | custom-call | flops 1000000000 | bytes 30000000 | tf_op jit(solution)/shard_map/pallas_call | solution.py:88
  34.0 2.5 %shard_map.226 = f32[32,4,640]{2,1,0:T(4,128)} custom-call(f32[24,1024]{1,0:T(8,128)S(1)} %get-tuple-element.70.refs_0_, f32[24,1024]{1,0:T(8,128)S(1)} %get-tuple-element.71.refs_1_, s32[1,128]{1,0:T(1,128)S(1)} %bitcast.14, s32[1,128]{1,0:T(1,128)S(1)} %bitcast.15, s32[1,128]{1,0:T(1,128)S(1)} %bitcast.16, f32[21,128,256]{2,1,0:T(8,128)S(1)} %copy-done), custom_call_target="tpu_custom_call" | custom-call | flops 300000000 | bytes 9000000 | tf_op jit(solution)/shard_map/pallas_call | solution.py:88
  36.5 3.5 %all-to-all-start = ((f32[32,4,640]{2,1,0:T(4,128)}), f32[32,4,640]{2,1,0:T(4,128)S(1)}, u32[]{:S(2)}, u32[]{:S(2)}) async-start(f32[32,4,640]{2,1,0:T(4,128)} %shard_map.226), calls=%async_computation | async-start | bytes 655360 | tf_op jit(solution)/shard_map/all_to_all | solution.py:787
  40.1 1.4 %collective-permute-start.4 = (f32[224,128]{1,0:T(8,128)S(1)}, f32[224,128]{1,0:T(8,128)S(1)}, u32[]{:S(2)}, u32[]{:S(2)}) collective-permute-start(f32[224,128]{1,0:T(8,128)S(1)} %copy-done.20), channel_id=1, source_target_pairs={{0,4},{4,8},{8,12},{12,16},{16,20},{20,24},{24,28},{28,0},{1,5},{5... | collective-permute-start | bytes 344072 | tf_op jit(solution)/shard_map/ppermute | solution.py:685
  41.5 2.8 %shard_map.227 = (f32[5,272,256]{2,1,0:T(8,128)}, f32[272,128]{1,0:T(8,128)}, f32[272,128]{1,0:T(8,128)}) custom-call(f32[3,256,256]{2,1,0:T(8,128)} %refs_0_.1, f32[256,256]{1,0:T(8,128)} %refs_1_.1, s32[256,256]{1,0:T(8,128)} %refs_2_.1, f32[32,128]{1,0:T(8,128)} %get-tuple-element.72.refs_3_, f32[32,128]{1,0:T(8,128)} %get-tuple-element.73.refs_4_), custom_call_target="tpu_custom_call" | custom-call | flops 200000000 | bytes 6000000 | tf_op jit(solution)/shard_map/pallas_call | solution.py:88
  44.3 9.1 %all-to-all-done.pay_hbm = f32[32,4,640]{2,1,0:T(4,128)S(1)} async-done(((f32[32,4,640]{2,1,0:T(4,128)}), f32[32,4,640]{2,1,0:T(4,128)S(1)}, u32[]{:S(2)}, u32[]{:S(2)}) %all-to-all-start) | async-done | bytes 327712 | tf_op jit(solution)/shard_map/all_to_all | solution.py:787
  53.4 0.7 copy-done.12
  54.1 2.3 %shard_map.228 = (f32[2,256,256]{2,1,0:T(8,128)S(1)}, f32[80,256]{1,0:T(8,128)S(1)}, f32[80,256]{1,0:T(8,128)S(1)}, bf16[272,336]{1,0:T(8,128)(2,1)S(1)}, bf16[2...) custom-call(f32[32,4,640]{2,1,0:T(4,128)} %copy-done.12, ...), custom_call_target="tpu_custom_call" | custom-call | flops 300000000 | bytes 9000000 | tf_op jit(solution)/shard_map/pallas_call | solution.py:88
  56.5 0.8 %collective-permute-start.8 = (f32[80,256]{1,0:T(8,128)S(1)}, f32[80,256]{1,0:T(8,128)S(1)}, u32[]{:S(2)}, u32[]{:S(2)}) collective-permute-start(f32[80,256]{1,0:T(8,128)S(1)} %get-tuple-element.78), channel_id=1, source_target_pairs={{0,4},{4,8},{8,12},{12,16},{16,20},{20,24},{24,28},{28,0},{1,5},{5... | collective-permute-start | bytes 245768 | tf_op jit(solution)/shard_map/ppermute | solution.py:685
  57.3 3.4 %collective-permute-start.9 = (f32[80,256]{1,0:T(8,128)S(1)}, f32[80,256]{1,0:T(8,128)S(1)}, u32[]{:S(2)}, u32[]{:S(2)}) collective-permute-start(f32[80,256]{1,0:T(8,128)S(1)} %get-tuple-element.79), channel_id=1, source_target_pairs={{0,28},{4,0},{8,4},{12,8},{16,12},{20,16},{24,20},{28,24},{1,29},{... | collective-permute-start | bytes 245768 | tf_op jit(solution)/shard_map/ppermute | solution.py:685
  60.7 0.0 collective-permute-start.5
  60.7 0.0 collective-permute-start.6
  60.8 1.8 %collective-permute-done.8.refs_1_ = f32[80,256]{1,0:T(8,128)S(1)} collective-permute-done((f32[80,256]{1,0:T(8,128)S(1)}, f32[80,256]{1,0:T(8,128)S(1)}, u32[]{:S(2)}, u32[]{:S(2)}) %collective-permute-start.8) | collective-permute-done | bytes 81952 | tf_op jit(solution)/shard_map/ppermute | solution.py:685
  62.6 2.6 %collective-permute-start.7 = (f32[224,128]{1,0:T(8,128)S(1)}, f32[224,128]{1,0:T(8,128)S(1)}, u32[]{:S(2)}, u32[]{:S(2)}) collective-permute-start(f32[224,128]{1,0:T(8,128)S(1)} %copy-done.17), channel_id=1, source_target_pairs={{0,3},{1,0},{2,1},{3,2},{4,7},{5,4},{6,5},{7,6},{8,11},{9,8},{10,9... | collective-permute-start | bytes 344072 | tf_op jit(solution)/shard_map/ppermute | solution.py:685
  65.2 0.7 shard_map.229
  65.9 0.1 collective-permute-start.10
  65.9 0.5 collective-permute-start.11
  66.4 5.2 %shard_map.224 = (f32[224,1024]{1,0:T(8,128)}, f32[9,56,256]{2,1,0:T(8,128)}) custom-call(f32[9,56,256]{2,1,0:T(8,128)} %get-tuple-element.62.integ_hbm, f32[9,56,256]{2,1,0:T(8,128)} %get-tuple-element.63.field_hbm, f32[9,9,3,256]{3,2,1,0:T(4,128)} %bitcast.10, bf16[168,192]{1,0:T(8,128)(2,1)} %get-tuple-element.64.w_hbm, ...), custom_call_target="tpu_custom_call" | custom-call | flops 500000000 | bytes 15000000 | tf_op jit(solution)/shard_map/pallas_call | solution.py:88
  71.7 0.6 copy-done.14
  72.3 0.0 copy-done.15
  72.4 0.0 copy-done.16
  72.4 4.4 %shard_map.225 = f32[9,56,256]{2,1,0:T(8,128)} custom-call(f32[224,128]{1,0:T(8,128)} %copy-done.13, f32[224,128]{1,0:T(8,128)} %copy-done.14, f32[224,128]{1,0:T(8,128)} %copy-done.15, f32[224,128]{1,0:T(8,128)} %copy-done.16, f32[8,512]{1,0:T(8,128)} %get-tuple-element.61.slot_hbm, s32[4,256]{1,0:T(4,128)} %codes_hbm.3, ...), custom_call_target="tpu_custom_call" | custom-call | flops 400000000 | bytes 12000000 | tf_op jit(solution)/shard_map/pallas_call | solution.py:88
  76.9 4.2 %shard_map.230 = f32[3,256,256]{2,1,0:T(8,128)} custom-call(f32[2,272,256]{2,1,0:T(8,128)S(1)} %get-tuple-element.84.refs_0_, f32[5,272,256]{2,1,0:T(8,128)S(1)} %get-tuple-element.85.refs_1_, f32[272,128]{1,0:T(8,128)S(1)} %collective-permute-done.10.refs_2_, f32[272,128]{1,0:T(8,128)S(1)} %collective-permute-done.11.refs_3_, ...), custom_call_target="tpu_custom_call" | custom-call | flops 400000000 | bytes 12000000 | tf_op jit(solution)/shard_map/pallas_call | solution.py:88
  (46 shorter events, 0.1 us)
Async XLA Ops:
  0.6 17.9 %copy-start.1 = (f32[9,56,256]{2,1,0:T(8,128)S(1)}, f32[9,56,256]{2,1,0:T(8,128)}, u32[]{:S(2)}) copy-start(f32[9,56,256]{2,1,0:T(8,128)} %field_ref.1) | copy-start | bytes 1548292
  0.6 17.9 %copy-start.3 = (f32[3,9,9,256]{3,0,2,1:T(4,128)S(1)}, f32[3,9,9,256]{3,0,2,1:T(4,128)}, u32[]{:S(2)}) copy-start(f32[3,9,9,256]{3,0,2,1:T(4,128)} %param.23) | copy-start | bytes 746500
  0.7 17.8 %copy-start.5 = (f32[4,21,56]{2,0,1:T(4,128)S(1)}, f32[4,21,56]{2,0,1:T(4,128)}, u32[]{:S(2)}) copy-start(f32[4,21,56]{2,0,1:T(4,128)} %param.26) | copy-start | bytes 56452
  0.7 17.8 %copy-start.6 = (s32[4,256]{1,0:T(4,128)S(1)}, s32[4,256]{1,0:T(4,128)}, u32[]{:S(2)}) copy-start(s32[4,256]{1,0:T(4,128)} %codes_hbm.3) | copy-start | bytes 12292
  0.7 17.8 %copy-start.7 = (s32[4,256]{1,0:T(4,128)S(1)}, s32[4,256]{1,0:T(4,128)}, u32[]{:S(2)}) copy-start(s32[4,256]{1,0:T(4,128)} %orient_ref.1) | copy-start | bytes 12292
  11.1 11.7 %copy-start.2 = (f32[4,9,9,256]{3,0,2,1:T(4,128)S(1)}, f32[4,9,9,256]{3,0,2,1:T(4,128)}, u32[]{:S(2)}) copy-start(f32[4,9,9,256]{3,0,2,1:T(4,128)} %param.27) | copy-start | bytes 995332
  11.1 11.7 %copy-start.4 = (bf16[448,224]{1,0:T(8,128)(2,1)S(1)}, bf16[448,224]{1,0:T(8,128)(2,1)}, u32[]{:S(2)}) copy-start(bf16[448,224]{1,0:T(8,128)(2,1)} %constant.13.clone.perm_ref.perm_hbm) | copy-start | bytes 602116
  11.1 11.7 %copy-start.11 = (s32[1,1,4,128]{3,2,1,0:T(4,128)S(1)}, s32[1,1,4,128]{3,2,1,0:T(4,128)}, u32[]{:S(2)}) copy-start(s32[1,1,4,128]{3,2,1,0:T(4,128)} %send_ref.1) | copy-start | bytes 6148
  11.1 11.6 %collective-permute-start = (f32[256,128]{1,0:T(8,128)S(1)}, f32[256,128]{1,0:T(8,128)S(1)}, u32[]{:S(2)}, u32[]{:S(2)}) collective-permute-start(f32[256,128]{1,0:T(8,128)S(1)} %get-tuple-element.46), channel_id=1, source_target_pairs={{0,4},{4,8},{8,12},{12,16},{16,20},{20,24},{24,28},{28,0},{1,5},{5... | collective-permute-start | bytes 393224 | tf_op jit(solution)/shard_map/ppermute | solution.py:685
  13.2 9.5 %collective-permute-start.1 = (f32[256,128]{1,0:T(8,128)S(1)}, f32[256,128]{1,0:T(8,128)S(1)}, u32[]{:S(2)}, u32[]{:S(2)}) collective-permute-start(f32[256,128]{1,0:T(8,128)S(1)} %get-tuple-element.47), channel_id=1, source_target_pairs={{0,28},{4,0},{8,4},{12,8},{16,12},{20,16},{24,20},{28,24},{1,29},{... | collective-permute-start | bytes 393224 | tf_op jit(solution)/shard_map/ppermute | solution.py:685
  16.3 6.1 %collective-permute-start.2 = (f32[224,128]{1,0:T(8,128)S(1)}, f32[224,128]{1,0:T(8,128)S(1)}, u32[]{:S(2)}, u32[]{:S(2)}) collective-permute-start(f32[224,128]{1,0:T(8,128)S(1)} %get-tuple-element.48), channel_id=1, source_target_pairs={{0,1},{1,2},{2,3},{3,0},{4,5},{5,6},{6,7},{7,4},{8,9},{9,10},{10,1... | collective-permute-start | bytes 344072 | tf_op jit(solution)/shard_map/ppermute | solution.py:685
  18.5 4.2 %collective-permute-start.3 = (f32[224,128]{1,0:T(8,128)S(1)}, f32[224,128]{1,0:T(8,128)S(1)}, u32[]{:S(2)}, u32[]{:S(2)}) collective-permute-start(f32[224,128]{1,0:T(8,128)S(1)} %get-tuple-element.49), channel_id=1, source_target_pairs={{0,3},{1,0},{2,1},{3,2},{4,7},{5,4},{6,5},{7,6},{8,11},{9,8},{10,9... | collective-permute-start | bytes 344072 | tf_op jit(solution)/shard_map/ppermute | solution.py:685
  22.7 11.2 %copy-start = (f32[21,128,256]{2,1,0:T(8,128)S(1)}, f32[21,128,256]{2,1,0:T(8,128)}, u32[]{:S(2)}) copy-start(f32[21,128,256]{2,1,0:T(8,128)} %refs_5_.1) | copy-start | bytes 8257540
  22.7 11.2 %copy-start.8 = (s32[128]{0:T(128)S(1)}, s32[128]{0:T(128)}, u32[]{:S(2)}) copy-start(s32[128]{0:T(128)} %param.31) | copy-start | bytes 1540
  22.8 11.2 %copy-start.9 = (s32[128,1]{0,1:T(1,128)S(1)}, s32[128,1]{0,1:T(1,128)}, u32[]{:S(2)}) copy-start(s32[128,1]{0,1:T(1,128)} %param.32) | copy-start | bytes 1540
  22.8 11.2 %copy-start.10 = (s32[128]{0:T(128)S(1)}, s32[128]{0:T(128)}, u32[]{:S(2)}) copy-start(s32[128]{0:T(128)} %param.33) | copy-start | bytes 1540
  34.0 6.1 %copy-start.20 = (f32[224,128]{1,0:T(8,128)S(1)}, f32[224,128]{1,0:T(8,128)}, u32[]{:S(2)}) copy-start(f32[224,128]{1,0:T(8,128)} %get-tuple-element.57) | copy-start | bytes 344068
  36.5 16.9 %all-to-all-start = ((f32[32,4,640]{2,1,0:T(4,128)}), f32[32,4,640]{2,1,0:T(4,128)S(1)}, u32[]{:S(2)}, u32[]{:S(2)}) async-start(f32[32,4,640]{2,1,0:T(4,128)} %shard_map.226), calls=%async_computation | async-start | bytes 655360 | tf_op jit(solution)/shard_map/all_to_all | solution.py:787
  40.1 25.9 %collective-permute-start.4 = (f32[224,128]{1,0:T(8,128)S(1)}, f32[224,128]{1,0:T(8,128)S(1)}, u32[]{:S(2)}, u32[]{:S(2)}) collective-permute-start(f32[224,128]{1,0:T(8,128)S(1)} %copy-done.20), channel_id=1, source_target_pairs={{0,4},{4,8},{8,12},{12,16},{16,20},{20,24},{24,28},{28,0},{1,5},{5... | collective-permute-start | bytes 344072 | tf_op jit(solution)/shard_map/ppermute | solution.py:685
  53.4 0.7 copy-start.12
  54.1 6.5 %copy-start.19 = (f32[224,128]{1,0:T(8,128)S(1)}, f32[224,128]{1,0:T(8,128)}, u32[]{:S(2)}) copy-start(f32[224,128]{1,0:T(8,128)} %get-tuple-element.58) | copy-start | bytes 344068
  54.1 6.6 %copy-start.18 = (f32[224,128]{1,0:T(8,128)S(1)}, f32[224,128]{1,0:T(8,128)}, u32[]{:S(2)}) copy-start(f32[224,128]{1,0:T(8,128)} %get-tuple-element.59) | copy-start | bytes 344068
  54.1 8.5 %copy-start.17 = (f32[224,128]{1,0:T(8,128)S(1)}, f32[224,128]{1,0:T(8,128)}, u32[]{:S(2)}) copy-start(f32[224,128]{1,0:T(8,128)} %get-tuple-element.60) | copy-start | bytes 344068
  56.5 6.1 %collective-permute-start.8 = (f32[80,256]{1,0:T(8,128)S(1)}, f32[80,256]{1,0:T(8,128)S(1)}, u32[]{:S(2)}, u32[]{:S(2)}) collective-permute-start(f32[80,256]{1,0:T(8,128)S(1)} %get-tuple-element.78), channel_id=1, source_target_pairs={{0,4},{4,8},{8,12},{12,16},{16,20},{20,24},{24,28},{28,0},{1,5},{5... | collective-permute-start | bytes 245768 | tf_op jit(solution)/shard_map/ppermute | solution.py:685
  57.3 7.9 %collective-permute-start.9 = (f32[80,256]{1,0:T(8,128)S(1)}, f32[80,256]{1,0:T(8,128)S(1)}, u32[]{:S(2)}, u32[]{:S(2)}) collective-permute-start(f32[80,256]{1,0:T(8,128)S(1)} %get-tuple-element.79), channel_id=1, source_target_pairs={{0,28},{4,0},{8,4},{12,8},{16,12},{20,16},{24,20},{28,24},{1,29},{... | collective-permute-start | bytes 245768 | tf_op jit(solution)/shard_map/ppermute | solution.py:685
  60.7 11.0 %collective-permute-start.5 = (f32[224,128]{1,0:T(8,128)S(1)}, f32[224,128]{1,0:T(8,128)S(1)}, u32[]{:S(2)}, u32[]{:S(2)}) collective-permute-start(f32[224,128]{1,0:T(8,128)S(1)} %copy-done.19), channel_id=1, source_target_pairs={{0,28},{4,0},{8,4},{12,8},{16,12},{20,16},{24,20},{28,24},{1,29},{... | collective-permute-start | bytes 344072 | tf_op jit(solution)/shard_map/ppermute | solution.py:685
  60.7 11.0 %collective-permute-start.6 = (f32[224,128]{1,0:T(8,128)S(1)}, f32[224,128]{1,0:T(8,128)S(1)}, u32[]{:S(2)}, u32[]{:S(2)}) collective-permute-start(f32[224,128]{1,0:T(8,128)S(1)} %copy-done.18), channel_id=1, source_target_pairs={{0,1},{1,2},{2,3},{3,0},{4,5},{5,6},{6,7},{7,4},{8,9},{9,10},{10,1... | collective-permute-start | bytes 344072 | tf_op jit(solution)/shard_map/ppermute | solution.py:685
  62.6 9.1 %collective-permute-start.7 = (f32[224,128]{1,0:T(8,128)S(1)}, f32[224,128]{1,0:T(8,128)S(1)}, u32[]{:S(2)}, u32[]{:S(2)}) collective-permute-start(f32[224,128]{1,0:T(8,128)S(1)} %copy-done.17), channel_id=1, source_target_pairs={{0,3},{1,0},{2,1},{3,2},{4,7},{5,4},{6,5},{7,6},{8,11},{9,8},{10,9... | collective-permute-start | bytes 344072 | tf_op jit(solution)/shard_map/ppermute | solution.py:685
  65.9 11.0 %collective-permute-start.10 = (f32[272,128]{1,0:T(8,128)S(1)}, f32[272,128]{1,0:T(8,128)S(1)}, u32[]{:S(2)}, u32[]{:S(2)}) collective-permute-start(f32[272,128]{1,0:T(8,128)S(1)} %get-tuple-element.86), channel_id=1, source_target_pairs={{0,1},{1,2},{2,3},{3,0},{4,5},{5,6},{6,7},{7,4},{8,9},{9,10},{10,1... | collective-permute-start | bytes 417800 | tf_op jit(solution)/shard_map/ppermute | solution.py:685
  65.9 5.8 %copy-start.13 = (f32[224,128]{1,0:T(8,128)}, f32[224,128]{1,0:T(8,128)S(1)}, u32[]{:S(2)}) copy-start(f32[224,128]{1,0:T(8,128)S(1)} %collective-permute-done.4.a0) | copy-start | bytes 344068
  65.9 10.9 %collective-permute-start.11 = (f32[272,128]{1,0:T(8,128)S(1)}, f32[272,128]{1,0:T(8,128)S(1)}, u32[]{:S(2)}, u32[]{:S(2)}) collective-permute-start(f32[272,128]{1,0:T(8,128)S(1)} %get-tuple-element.87), channel_id=1, source_target_pairs={{0,3},{1,0},{2,1},{3,2},{4,7},{5,4},{6,5},{7,6},{8,11},{9,8},{10,9... | collective-permute-start | bytes 417800 | tf_op jit(solution)/shard_map/ppermute | solution.py:685
  71.7 0.7 copy-start.16
  (2 other events, 1.3 us)
where the time goes:
time: 82.6 us; the launch traced here: 81.1 us
  Pallas kernels  47.5 us (58%)
  starting transfers between devices  19.7 us (24%)
  waiting for transfers between devices  11.4 us (14%)
  local copies, waits for them, and re-layouts  1.49 us (2%)
  between operations  1.02 us (1%)
    pallas_call x10, Pallas kernels, call(): pl.pallas_call(body, in_specs=[spec(i in held) for i in range(len(args))]...  47.5 us
    ppermute x12, starting transfers between devices, shift(): lax.ppermute(value, axis, [(i, (i + step) % count) for i in range(count)])  16.2 us
    all_to_all x1, waiting for transfers between devices, on_device(): lax.all_to_all(payload, ('gx', 'gy'), split_axis=0, concat_axis=0, tiled=...  9.14 us
    all_to_all x1, starting transfers between devices, on_device(): lax.all_to_all(payload, ('gx', 'gy'), split_axis=0, concat_axis=0, tiled=...  3.54 us
    ppermute x12, waiting for transfers between devices, shift(): lax.ppermute(value, axis, [(i, (i + step) % count) for i in range(count)])  2.21 us
  transfers between devices with their start and end apart: 13, of which 3 were waited for; matrix products, arithmetic and copies ran while one was open for 0% of the time, Pallas kernels for 24%

commit v1 on v0

--- a/solution.py
+++ b/solution.py
@@ -166,32 +166,44 @@
     return jnp.concatenate([hi, lo, hi], axis=0)
 
 
-def derive(src_ref, star_ref, w_ref, moved_ref, emit):
-    variables, basis, elems = src_ref.shape
-    for v in range(variables):
+GROUP = 3
+
+
+def mix(src_ref, first, w_ref, moved_ref):
+    for v in range(first, first + GROUP):
         moved_ref[v] = mm(w_ref[...], stacked(src_ref[v]))
-    group = 3
-
-    def body(g, carry):
+
+
+def combine(first, star_ref, moved_ref, total_ref, emit):
+    variables, basis, elems = total_ref.shape
+    for u0 in range(0, variables, GROUP):
         for h in range(elems // LANES):
             at = slice(h * LANES, (h + 1) * LANES)
-            acc = [jnp.zeros((basis, LANES), F32) for _ in range(group)]
-            for v in range(variables):
+            acc = [total_ref[u0 + i, :, at] if first else None for i in range(GROUP)]
+            for v in range(first, first + GROUP):
                 for d in range(3):
                     m = moved_ref[v, d * basis : (d + 1) * basis, at]
-                    for i in range(group):
-                        acc[i] = acc[i] + star_ref[g * group + i, v, d : d + 1, at] * m
-            for i in range(group):
-                emit(g * group + i, at, acc[i])
-        return carry
-
-    lax.fori_loop(0, variables // group, body, 0)
-
-
-def predict(field_ref, star_ref, w_ref, moved_ref, term_ref, integ_ref):
-    if field_ref is not term_ref:
-        term_ref[...] = field_ref[...]
+                    for i in range(GROUP):
+                        part = star_ref[u0 + i, v, d : d + 1, at] * m
+                        acc[i] = part if acc[i] is None else acc[i] + part
+            for i in range(GROUP):
+                if first + GROUP < variables:
+                    total_ref[u0 + i, :, at] = acc[i]
+                else:
+                    emit(u0 + i, at, acc[i])
+
+
+def derive(src_ref, star_ref, w_ref, moved_ref, total_ref, emit):
+    variables = src_ref.shape[0]
+    for first in range(0, variables, GROUP):
+        if first + GROUP < variables:
+            mix(src_ref, first + GROUP, w_ref, moved_ref)
+        combine(first, star_ref, moved_ref, total_ref, emit)
+
+
+def predict(star_ref, w_ref, moved_ref, term_ref, integ_ref, total_ref):
     integ_ref[...] = term_ref[...]
+    mix(term_ref, 0, w_ref, moved_ref)
 
     def body(k, carry):
         scale = F32(-1.0 / ORDER)
@@ -203,7 +215,8 @@
             term_ref[u, :, at] = value
             integ_ref[u, :, at] = integ_ref[u, :, at] + value
 
-        derive(term_ref, star_ref, w_ref, moved_ref, emit)
+        derive(term_ref, star_ref, w_ref, moved_ref, total_ref, emit)
+        mix(term_ref, 0, w_ref, moved_ref)
         return carry
 
     lax.fori_loop(1, ORDER, body, 0)
@@ -311,7 +324,7 @@
     state_hbm, star_hbm, deriv_hbm, trace_hbm, place_hbm, send_hbm, sea_hbm, depth_hbm, wet_hbm,
     w_ref, wt_ref, integ_ref, lifted_ref, o0, o1, o2, o3,
     star_ref, deriv_ref, trace_ref, place_ref, send_ref, own_ref,
-    moved_ref, term_ref, left_ref, stage_ref, sea_edge, depth_edge, wet_edge, sem_ref,
+    moved_ref, term_ref, total_ref, left_ref, stage_ref, sea_edge, depth_edge, wet_edge, sem_ref,
 ):
     urgent = start(
         [(deriv_hbm, deriv_ref), (state_hbm, term_ref), (star_hbm, star_ref)], sem_ref
@@ -330,7 +343,7 @@
     finish(urgent[:1])
     prep_deriv(deriv_ref, w_ref)
     finish(urgent[1:])
-    predict(term_ref, star_ref, w_ref, moved_ref, term_ref, integ_ref)
+    predict(star_ref, w_ref, moved_ref, term_ref, integ_ref, total_ref)
     finish(later)
     prep_trace(trace_ref, place_ref, stage_ref, wt_ref)
     traces(integ_ref, wt_ref, (own_ref,))
@@ -353,7 +366,7 @@
 
 def local_work(
     integ_ref, field_ref, star_ref, w_ref, wt_ref, turn, codes, jump_ref, base_ref,
-    own_refs, left_ref, moved_ref,
+    own_refs, left_ref, moved_ref, total_ref,
 ):
     traces(integ_ref, wt_ref, own_refs)
     local_jump(own_refs, turn, codes, left_ref, jump_ref)
@@ -361,13 +374,14 @@
     def emit(u, at, acc):
         base_ref[u, :, at] = field_ref[u, :, at] - acc
 
-    derive(integ_ref, star_ref, w_ref, moved_ref, emit)
+    mix(integ_ref, 0, w_ref, moved_ref)
+    derive(integ_ref, star_ref, w_ref, moved_ref, total_ref, emit)
 
 
 def local_first_kernel(
     integ_ref, field_ref, star_ref, w_ref, wt_ref, codes_ref, orient_ref, lift_ref,
     jump_ref, base_ref, slot_ref, wl_ref, turn_out, slot_out, wl_out, w_out, wt_out,
-    turn_ref, own0, own1, own2, left_ref, moved_ref, stage_ref, sem_ref,
+    turn_ref, own0, own1, own2, left_ref, moved_ref, total_ref, stage_ref, sem_ref,
 ):
     prep_lift(lift_ref, stage_ref, wl_ref)
     codes = row_of(codes_ref)
@@ -388,17 +402,19 @@
     )
     local_work(
         integ_ref, field_ref, star_ref, w_ref, wt_ref, turn_ref[0:1, :], codes, jump_ref, base_ref,
-        (own0, own1, own2), left_ref, moved_ref,
+        (own0, own1, own2), left_ref, moved_ref, total_ref,
     )
     finish(copies)
 
 
 def second_kernel(
+    capacity, nodes,
     a0, a1, a2, a3, slot_ref, codes_ref, jump_ref, flux_m_ref, perm_ref, wl_ref, base_ref,
-    star_ref, w_ref, wt_ref, send_ref,
-    lifted_ref, field_out, integ_out, edge_low, edge_high, s0, s1, s2, s3,
+    star_ref, w_ref, wt_ref, send_ref, lifted_ref, faces_ref, owner_ref, blocks_ref, weights_ref,
+    pay_ref, field_out, integ_out, edge_low, edge_high, s0, s1, s2, s3,
     field_ref, integ_ref, own_ref, o0, o1, o2, o3,
-    arr_left_ref, part_ref, flux_ref, moved_ref, term_ref, left_ref, sem_ref,
+    arr_left_ref, part_ref, flux_ref, moved_ref, term_ref, total_ref, left_ref,
+    disp_ref, rows_ref, sem_ref,
 ):
     rows = jump_ref.shape[0]
     tail = pl.ds(rows, a0.shape[0] - rows)
@@ -408,13 +424,17 @@
         flux_m_ref, perm_ref, wl_ref, base_ref, (arr_left_ref, part_ref, flux_ref), field_ref,
     )
     copies += start([(field_ref, field_out)], sem_ref, 2)
-    predict(field_ref, star_ref, w_ref, moved_ref, term_ref, integ_ref)
+    term_ref[...] = field_ref[...]
+    predict(star_ref, w_ref, moved_ref, term_ref, integ_ref, total_ref)
     copies += start([(integ_ref, integ_out)], sem_ref, 3)
     traces(integ_ref, wt_ref, (own_ref,))
-    np_ = lifted_ref.shape[0]
-    lifted_ref[...] = own_ref[2 * np_ : 3 * np_, :]
     send_gather(own_ref, send_ref, left_ref, (o0, o1, o2, o3))
     copies += start([(o0, s0), (o1, s1), (o2, s2), (o3, s3)], sem_ref, 4)
+    np_ = lifted_ref.shape[0]
+    project(
+        capacity, nodes, lifted_ref[...], own_ref[2 * np_ : 3 * np_, :], faces_ref, owner_ref,
+        blocks_ref, weights_ref, pay_ref, disp_ref, rows_ref,
+    )
     finish(copies)
 
 
@@ -422,7 +442,7 @@
     integ_hbm, field_hbm, star_hbm, w_hbm, wt_hbm, turn_hbm, codes_hbm,
     jump_out, base_out,
     integ_ref, field_ref, star_ref, w_ref, wt_ref, turn_ref, codes_ref, jump_ref, base_ref,
-    own0, own1, own2, left_ref, moved_ref, sem_ref,
+    own0, own1, own2, left_ref, moved_ref, total_ref, sem_ref,
 ):
     copies = start(
         [(integ_hbm, integ_ref), (wt_hbm, wt_ref), (turn_hbm, turn_ref), (codes_hbm, codes_ref),
@@ -431,7 +451,7 @@
     finish(copies)
     local_work(
         integ_ref, field_ref, star_ref, w_ref, wt_ref, turn_ref[0:1, :], row_of(codes_ref),
-        jump_ref, base_ref, (own0, own1, own2), left_ref, moved_ref,
+        jump_ref, base_ref, (own0, own1, own2), left_ref, moved_ref, total_ref,
     )
     finish(start([(jump_ref, jump_out), (base_ref, base_out)], sem_ref, 7))
 
@@ -455,11 +475,14 @@
     finish(start([(field_ref, field_out)], sem_ref))
 
 
-def project_kernel(capacity, nodes, own_a, own_b, faces_ref, owner_ref, blocks_ref, weights_ref, pay_ref, disp_ref, rows_ref):
+def project(
+    capacity, nodes, own_a, own_b, faces_ref, owner_ref, blocks_ref, weights_ref, pay_ref,
+    disp_ref, rows_ref,
+):
     np_ = pad8(nodes)
     faces = own_a.shape[1]
     sea_rows, _ = weights_ref.shape[1:]
-    both = jnp.concatenate([own_a[...], own_b[...]], axis=0)
+    both = jnp.concatenate([own_a, own_b], axis=0)
     hi, lo = split(both)
     picks = hot(iota((faces, sea_rows), 0) == faces_ref[...])
     disp = mm(jnp.concatenate([hi, lo], axis=0), picks)
@@ -500,16 +523,13 @@
 
 
 def raster_kernel(
-    pay_hbm, bx_hi_hbm, bx_lo_hbm, by_hi_hbm, by_lo_hbm, ext_hbm, right_hbm, left_hbm,
-    uplift_ref, up_ref, down_ref, bx_hi, bx_lo, by_hi, by_lo, ext_ref, right_ref, left_ref,
-    pay_ref, got_ref, sem_ref,
-):
-    urgent = start([(pay_hbm, pay_ref)], sem_ref)
+    pay_ref, b_hi_hbm, b_lo_hbm, right_hbm, left_hbm,
+    uplift_ref, up_ref, down_ref, b_hi, b_lo, right_ref, left_ref, got_ref, sem_ref,
+):
     later = start(
-        [(bx_hi_hbm, bx_hi), (bx_lo_hbm, bx_lo), (right_hbm, right_ref), (left_hbm, left_ref),
-         (by_hi_hbm, by_hi), (by_lo_hbm, by_lo), (ext_hbm, ext_ref)], sem_ref, 1,
-    )
-    finish(urgent)
+        [(b_hi_hbm, b_hi), (b_lo_hbm, b_lo), (right_hbm, right_ref), (left_hbm, left_ref)],
+        sem_ref,
+    )
     devs, capacity, _ = pay_ref.shape
     total = devs * capacity
     for d in range(devs):
@@ -748,7 +768,7 @@
         first_kernel,
         [w_of, wt_of, field_of, lifted_of] + [(out_x, F32)] * 2 + [out_of] * 2,
         [star_of, (deriv.shape, F32), (trace_ops.shape, F32), (place.shape, BF16),
-         (send_faces.shape, send_faces.dtype), wide_of, moved, field_of, left, stage,
+         (send_faces.shape, send_faces.dtype), wide_of, moved, field_of, field_of, left, stage,
          ((2, 3, EDGE, tile_y), F32), ((2, EDGE, tile_y), F32), ((2, EDGE, tile_y), wet.dtype),
          sems(16)],
         state, star, deriv, trace_ops, place, send_faces, sea_state, depth, wet,
@@ -759,30 +779,24 @@
         local_first_kernel,
         [wide_of, field_of, slot_of, wl_of, hbm(turn_of), hbm(slot_of), hbm(wl_of), hbm(w_of),
          hbm(wt_of)],
-        [turn_of, wide_of, wide_of, wide_of, left, moved, stage, sems(5)],
+        [turn_of, wide_of, wide_of, wide_of, left, moved, field_of, stage, sems(5)],
         integ, state, star, w, wt, neighbours, orient, lift,
         micros=4,
     )
-    lifted_b, field_h, integ_h, edge_low, edge_high, *outgoing = call(
-        second_kernel,
-        [lifted_of, hbm(field_of), hbm(field_of)]
-        + [((out_x[0] - rows, slots), F32, HBM)] * 2 + [hbm(out_of)] * 4,
-        [field_of, field_of, wide_of] + [out_of] * 4
-        + [arr_left, wide_of, flux, moved, field_of, left, sems(8)],
-        *arrived, slot_turn, neighbours, jump, face_flux, perm, wl, base, star, w, wt,
-        send_faces, micros=10,
-    )
-
     sea_rows, cells = sea_weights.shape[1:]
     devs = lax.axis_size("gx") * lax.axis_size("gy")
     capacity = max(2, (sea_rows + devs - 1) // devs)
     message = (devs, capacity, STEPS * cells + LANES)
-    payload, = call(
-        lambda *refs: project_kernel(capacity, nodes, *refs),
-        [(message, F32)],
-        [((sea_rows, LANES), F32), ((STEPS, sea_rows, cells), F32)],
-        lifted_a, lifted_b, sea_faces.reshape(1, -1), sea_owner.reshape(1, -1),
-        sea_blocks.reshape(1, -1), sea_weights, micros=3,
+    payload, field_h, integ_h, edge_low, edge_high, *outgoing = call(
+        lambda *refs: second_kernel(capacity, nodes, *refs),
+        [(message, F32), hbm(field_of), hbm(field_of)]
+        + [((out_x[0] - rows, slots), F32, HBM)] * 2 + [hbm(out_of)] * 4,
+        [field_of, field_of, wide_of] + [out_of] * 4
+        + [arr_left, wide_of, flux, moved, field_of, field_of, left,
+           ((sea_rows, LANES), F32), ((STEPS, sea_rows, cells), F32), sems(8)],
+        *arrived, slot_turn, neighbours, jump, face_flux, perm, wl, base, star, w, wt,
+        send_faces, lifted_a, sea_faces.reshape(1, -1), sea_owner.reshape(1, -1),
+        sea_blocks.reshape(1, -1), sea_weights, micros=12,
     )
     got = lax.all_to_all(payload, ("gx", "gy"), split_axis=0, concat_axis=0, tiled=True)
     arrived = sent(outgoing)
@@ -800,7 +814,7 @@
     jump_h, base_h = call(
         local_second_kernel, [hbm(wide_of), hbm(field_of)],
         [field_of, field_of, star_of, w_of, wt_of, turn_of, codes_of, wide_of, field_of,
-         wide_of, wide_of, wide_of, left, moved, sems(9)],
+         wide_of, wide_of, wide_of, left, moved, field_of, sems(9)],
         integ_h, field_h, star, w_h, wt_h, turn_h, neighbours,
         micros=5, held=range(7),
     )
@@ -817,14 +831,14 @@
     read_x = np.concatenate([np.arange(tile_x + HALO_X), np.arange(-HALO_X, 0)])
     cell_y = np.concatenate([np.arange(tile_y + LANES // 2), np.arange(-LANES // 2, 0)])
     read_y = np.concatenate([np.arange(tile_y + LANES), np.arange(-LANES, 0)])
-    bands = [jnp.asarray(b) for b in band(cell_x, read_x)]
-    bands += [jnp.asarray(b.T) for b in band(cell_y, read_y)]
-    uplift, up, down, bx_hi, bx_lo, by_hi, by_lo, ext, sea_right, sea_left = call(
+    bx = [jnp.asarray(b) for b in band(cell_x, read_x)]
+    by = [jnp.asarray(b.T) for b in band(cell_y, read_y)]
+    uplift, up, down, bx_hi, bx_lo, sea_right, sea_left = call(
         raster_kernel,
         [((STEPS, tile_x, tile_y), F32), halo, halo]
-        + [(b.shape, BF16) for b in bands] + [ext_of, strip_of, strip_of],
-        [(message, F32), ((devs * capacity, message[2]), F32), sems(8)],
-        got, *bands, ext_h, right_h, left_h, micros=3, held=range(8),
+        + [(b.shape, BF16) for b in bx] + [strip_of, strip_of],
+        [((devs * capacity, message[2]), F32), sems(4)],
+        got, *bx, right_h, left_h, micros=2, held=range(1, 5),
     )
     x_low, x_high = shift(up, "gx", 1), shift(down, "gx", -1)
     along, right, left_going = call(
@@ -835,7 +849,7 @@
     y_low, y_high = shift(right, "gy", 1), shift(left_going, "gy", -1)
     ocean, = call(
         lambda *refs: ocean_kernel(axes, *refs), [((3, tile_x, tile_y), F32)], [],
-        along, ext, y_low, y_high, by_hi, by_lo, micros=4,
+        along, ext_h, y_low, y_high, *by, micros=4,
     )
     return elastic, ocean
 

time: 82.6 us -> 79.1 us (0.958)
  Pallas kernels: 47.5 us -> 44.7 us
    pallas_call x10 -> x9, Pallas kernels: 47.5 us -> 44.7 us  [call(): pl.pallas_call(body, in_specs=[spec(i in held) for i in range(len(args))]...]
  transfers between devices with their start and end apart: 13 -> 13, of which waited for: 3 -> 3; matrix products, arithmetic and copies ran while one was open for 0% -> 0% of each run, Pallas kernels for 24% -> 25%
where the time goes in v1:
time: 79.1 us; the launch traced here: 77.7 us
  Pallas kernels  44.7 us (57%)
  starting transfers between devices  19.7 us (25%)
  waiting for transfers between devices  11.4 us (14%)
  between operations  1.07 us (1%)
    pallas_call x9, Pallas kernels, call(): pl.pallas_call(body, in_specs=[spec(i in held) for i in range(len(args))]...  44.7 us
    ppermute x12, starting transfers between devices, shift(): lax.ppermute(value, axis, [(i, (i + step) % count) for i in range(count)])  16.2 us
    all_to_all x1, waiting for transfers between devices, on_device(): lax.all_to_all(payload, ('gx', 'gy'), split_axis=0, concat_axis=0, tiled=...  9.14 us
    all_to_all x1, starting transfers between devices, on_device(): lax.all_to_all(payload, ('gx', 'gy'), split_axis=0, concat_axis=0, tiled=...  3.54 us
    ppermute x12, waiting for transfers between devices, shift(): lax.ppermute(value, axis, [(i, (i + step) % count) for i in range(count)])  2.25 us
  transfers between devices with their start and end apart: 13, of which 3 were waited for; matrix products, arithmetic and copies ran while one was open for 0% of the time, Pallas kernels for 25%

profile of v1, /device:TPU:1, one launch (start us, length us, event | category | flops | bytes accessed | tf_op | source)
XLA Modules:
  0.0 77.7 jit_solution(16457343268858005807)
XLA Ops:
  0.6 0.0 copy-start.4
  0.7 0.0 copy-start.9
  0.8 0.0 copy-start.2
  0.8 9.5 %shard_map.221 = (bf16[168,192]{1,0:T(8,128)(2,1)S(1)}, bf16[288,192]{1,0:T(8,128)(2,1)S(1)}, f32[9,56,256]{2,1,0:T(8,128)S(1)}, f32[24,1024]{1,0:T(8,128)S(1)},...) custom-call(f32[9,56,256]{2,1,0:T(8,128)} %field_ref.1, ...), custom_call_target="tpu_custom_call" | custom-call | flops 1000000000 | bytes 30000000 | tf_op jit(solution)/shard_map/pallas_call | solution.py:88
  10.3 2.1 %collective-permute-start = (f32[256,128]{1,0:T(8,128)S(1)}, f32[256,128]{1,0:T(8,128)S(1)}, u32[]{:S(2)}, u32[]{:S(2)}) collective-permute-start(f32[256,128]{1,0:T(8,128)S(1)} %get-tuple-element.43), channel_id=1, source_target_pairs={{0,4},{4,8},{8,12},{12,16},{16,20},{20,24},{24,28},{28,0},{1,5},{5... | collective-permute-start | bytes 393224 | tf_op jit(solution)/shard_map/ppermute | solution.py:705
  12.4 3.1 %collective-permute-start.1 = (f32[256,128]{1,0:T(8,128)S(1)}, f32[256,128]{1,0:T(8,128)S(1)}, u32[]{:S(2)}, u32[]{:S(2)}) collective-permute-start(f32[256,128]{1,0:T(8,128)S(1)} %get-tuple-element.44), channel_id=1, source_target_pairs={{0,28},{4,0},{8,4},{12,8},{16,12},{20,16},{24,20},{28,24},{1,29},{... | collective-permute-start | bytes 393224 | tf_op jit(solution)/shard_map/ppermute | solution.py:705
  15.5 2.2 %collective-permute-start.2 = (f32[224,128]{1,0:T(8,128)S(1)}, f32[224,128]{1,0:T(8,128)S(1)}, u32[]{:S(2)}, u32[]{:S(2)}) collective-permute-start(f32[224,128]{1,0:T(8,128)S(1)} %get-tuple-element.45), channel_id=1, source_target_pairs={{0,1},{1,2},{2,3},{3,0},{4,5},{5,6},{6,7},{7,4},{8,9},{9,10},{10,1... | collective-permute-start | bytes 344072 | tf_op jit(solution)/shard_map/ppermute | solution.py:705
  17.8 3.8 %shard_map.222 = (f32[224,1024]{1,0:T(8,128)S(1)}, f32[9,56,256]{2,1,0:T(8,128)S(1)}, f32[8,512]{1,0:T(8,128)S(1)}, bf16[112,192]{1,0:T(8,128)(2,1)S(1)}, f32[8,...) custom-call(f32[9,56,256]{2,1,0:T(8,128)S(1)} %get-tuple-element.47., ...), custom_call_target="tpu_custom_call" | custom-call | flops 400000000 | bytes 12000000 | tf_op jit(solution)/shard_map/pallas_call | solution.py:88
  21.6 0.4 collective-permute-done.3.refs_3_
  22.0 12.1 %shard_map.223 = (f32[32,4,640]{2,1,0:T(4,128)}, f32[9,56,256]{2,1,0:T(8,128)}, f32[9,56,256]{2,1,0:T(8,128)}, f32[32,128]{1,0:T(8,128)}, f32[32,128]{1,0:T(8,12...) custom-call(f32[256,128]{1,0:T(8,128)S(1)} %collective-permute-done.refs_0_, ...), custom_call_target="tpu_custom_call" | custom-call | flops 1200000000 | bytes 36000000 | tf_op jit(solution)/shard_map/pallas_call | solution.py:88
  34.1 3.5 %all-to-all-start = ((f32[32,4,640]{2,1,0:T(4,128)}), f32[32,4,640]{2,1,0:T(4,128)S(1)}, u32[]{:S(2)}, u32[]{:S(2)}) async-start(f32[32,4,640]{2,1,0:T(4,128)} %get-tuple-element.68), calls=%async_computation | async-start | bytes 655360 | tf_op jit(solution)/shard_map/all_to_all | solution.py:801
  37.7 1.4 %collective-permute-start.4 = (f32[224,128]{1,0:T(8,128)}, f32[224,128]{1,0:T(8,128)S(1)}, u32[]{:S(2)}, u32[]{:S(2)}) collective-permute-start(f32[224,128]{1,0:T(8,128)} %get-tuple-element.55), channel_id=1, source_target_pairs={{0,4},{4,8},{8,12},{12,16},{16,20},{20,24},{24,28},{28,0},{1,5},{5... | collective-permute-start | bytes 344072 | tf_op jit(solution)/shard_map/ppermute | solution.py:705
  39.1 2.8 %shard_map.226 = (f32[5,272,256]{2,1,0:T(8,128)}, f32[272,128]{1,0:T(8,128)}, f32[272,128]{1,0:T(8,128)}) custom-call(f32[3,256,256]{2,1,0:T(8,128)} %refs_0_.1, f32[256,256]{1,0:T(8,128)} %refs_1_.1, s32[256,256]{1,0:T(8,128)} %refs_2_.1, f32[32,128]{1,0:T(8,128)} %get-tuple-element.69.refs_3_, f32[32,128]{1,0:T(8,128)} %get-tuple-element.70.refs_4_), custom_call_target="tpu_custom_call" | custom-call | flops 200000000 | bytes 6000000 | tf_op jit(solution)/shard_map/pallas_call | solution.py:88
  41.9 9.1 %all-to-all-done.pay_ref = f32[32,4,640]{2,1,0:T(4,128)S(1)} async-done(((f32[32,4,640]{2,1,0:T(4,128)}), f32[32,4,640]{2,1,0:T(4,128)S(1)}, u32[]{:S(2)}, u32[]{:S(2)}) %all-to-all-start) | async-done | bytes 327712 | tf_op jit(solution)/shard_map/all_to_all | solution.py:801
  51.0 2.1 %shard_map.227 = (f32[2,256,256]{2,1,0:T(8,128)S(1)}, f32[80,256]{1,0:T(8,128)S(1)}, f32[80,256]{1,0:T(8,128)S(1)}, bf16[272,336]{1,0:T(8,128)(2,1)S(1)}, bf16[2...) custom-call(f32[32,4,640]{2,1,0:T(4,128)S(1)} %all-to-all-done.pay_ref, ...), custom_call_target="tpu_custom_call" | custom-call | flops 200000000 | bytes 6000000 | tf_op jit(solution)/shard_map/pallas_call | solution.py:88
  53.2 0.8 %collective-permute-start.8 = (f32[80,256]{1,0:T(8,128)S(1)}, f32[80,256]{1,0:T(8,128)S(1)}, u32[]{:S(2)}, u32[]{:S(2)}) collective-permute-start(f32[80,256]{1,0:T(8,128)S(1)} %get-tuple-element.74), channel_id=1, source_target_pairs={{0,4},{4,8},{8,12},{12,16},{16,20},{20,24},{24,28},{28,0},{1,5},{5... | collective-permute-start | bytes 245768 | tf_op jit(solution)/shard_map/ppermute | solution.py:705
  54.0 3.4 %collective-permute-start.9 = (f32[80,256]{1,0:T(8,128)S(1)}, f32[80,256]{1,0:T(8,128)S(1)}, u32[]{:S(2)}, u32[]{:S(2)}) collective-permute-start(f32[80,256]{1,0:T(8,128)S(1)} %get-tuple-element.75), channel_id=1, source_target_pairs={{0,28},{4,0},{8,4},{12,8},{16,12},{20,16},{24,20},{28,24},{1,29},{... | collective-permute-start | bytes 245768 | tf_op jit(solution)/shard_map/ppermute | solution.py:705
  57.4 0.0 collective-permute-start.5
  57.4 0.0 collective-permute-start.6
  57.5 1.8 %collective-permute-done.8.refs_1_ = f32[80,256]{1,0:T(8,128)S(1)} collective-permute-done((f32[80,256]{1,0:T(8,128)S(1)}, f32[80,256]{1,0:T(8,128)S(1)}, u32[]{:S(2)}, u32[]{:S(2)}) %collective-permute-start.8) | collective-permute-done | bytes 81952 | tf_op jit(solution)/shard_map/ppermute | solution.py:705
  59.3 2.6 %collective-permute-start.7 = (f32[224,128]{1,0:T(8,128)S(1)}, f32[224,128]{1,0:T(8,128)S(1)}, u32[]{:S(2)}, u32[]{:S(2)}) collective-permute-start(f32[224,128]{1,0:T(8,128)S(1)} %copy-done.19), channel_id=1, source_target_pairs={{0,3},{1,0},{2,1},{3,2},{4,7},{5,4},{6,5},{7,6},{8,11},{9,8},{10,9... | collective-permute-start | bytes 344072 | tf_op jit(solution)/shard_map/ppermute | solution.py:705
  61.9 0.7 shard_map.228
  62.6 0.0 copy-start.6
  62.6 0.0 copy-start.7
  62.6 0.1 collective-permute-start.10
  62.7 0.5 collective-permute-start.11
  63.2 5.3 %shard_map.224 = (f32[224,1024]{1,0:T(8,128)}, f32[9,56,256]{2,1,0:T(8,128)}) custom-call(f32[9,56,256]{2,1,0:T(8,128)} %get-tuple-element.60.integ_hbm, f32[9,56,256]{2,1,0:T(8,128)} %get-tuple-element.61.field_hbm, f32[9,9,3,256]{3,2,1,0:T(4,128)} %bitcast.10, bf16[168,192]{1,0:T(8,128)(2,1)} %get-tuple-element.62.w_hbm, ...), custom_call_target="tpu_custom_call" | custom-call | flops 500000000 | bytes 15000000 | tf_op jit(solution)/shard_map/pallas_call | solution.py:88
  68.6 0.6 copy-done.16
  69.2 0.0 copy-done.17
  69.2 0.0 copy-done.18
  69.3 4.4 %shard_map.225 = f32[9,56,256]{2,1,0:T(8,128)} custom-call(f32[224,128]{1,0:T(8,128)} %copy-done.15, f32[224,128]{1,0:T(8,128)} %copy-done.16, f32[224,128]{1,0:T(8,128)} %copy-done.17, f32[224,128]{1,0:T(8,128)} %copy-done.18, f32[8,512]{1,0:T(8,128)} %get-tuple-element.59.slot_hbm, s32[4,256]{1,0:T(4,128)} %codes_hbm.3, ...), custom_call_target="tpu_custom_call" | custom-call | flops 400000000 | bytes 12000000 | tf_op jit(solution)/shard_map/pallas_call | solution.py:88
  73.8 3.9 %shard_map.229 = f32[3,256,256]{2,1,0:T(8,128)} custom-call(f32[2,272,256]{2,1,0:T(8,128)S(1)} %get-tuple-element.80.refs_0_, f32[5,272,256]{2,1,0:T(8,128)S(1)} %copy-done.1, f32[272,128]{1,0:T(8,128)S(1)} %collective-permute-done.10.refs_2_, f32[272,128]{1,0:T(8,128)S(1)} %collective-permute-done.11.refs_3_, bf16[512,384]{1,0:T(8,128)(2,1)S(1)} %copy-done.7, ...), custom_call_target="tpu_custom_call" | custom-call | flops 400000000 | bytes 12000000 | tf_op jit(solution)/shard_map/pallas_call | solution.py:88
  (47 shorter events, 0.1 us)
Async XLA Ops:
  0.6 21.3 %copy-start.4 = (bf16[448,224]{1,0:T(8,128)(2,1)S(1)}, bf16[448,224]{1,0:T(8,128)(2,1)}, u32[]{:S(2)}) copy-start(bf16[448,224]{1,0:T(8,128)(2,1)} %constant.13.clone.refs_8_.perm_hbm) | copy-start | bytes 602116
  0.6 21.3 %copy-start.11 = (s32[1,1,4,128]{3,2,1,0:T(4,128)S(1)}, s32[1,1,4,128]{3,2,1,0:T(4,128)}, u32[]{:S(2)}) copy-start(s32[1,1,4,128]{3,2,1,0:T(4,128)} %refs_14_.1) | copy-start | bytes 6148
  0.7 17.1 %copy-start.5 = (f32[9,56,256]{2,1,0:T(8,128)S(1)}, f32[9,56,256]{2,1,0:T(8,128)}, u32[]{:S(2)}) copy-start(f32[9,56,256]{2,1,0:T(8,128)} %field_ref.1) | copy-start | bytes 1548292
  0.7 17.1 %copy-start.3 = (f32[3,9,9,256]{3,0,2,1:T(4,128)S(1)}, f32[3,9,9,256]{3,0,2,1:T(4,128)}, u32[]{:S(2)}) copy-start(f32[3,9,9,256]{3,0,2,1:T(4,128)} %param.23) | copy-start | bytes 746500
  0.7 17.1 %copy-start.9 = (s32[4,256]{1,0:T(4,128)S(1)}, s32[4,256]{1,0:T(4,128)}, u32[]{:S(2)}) copy-start(s32[4,256]{1,0:T(4,128)} %codes_hbm.3) | copy-start | bytes 12292
  0.7 17.1 %copy-start.10 = (s32[4,256]{1,0:T(4,128)S(1)}, s32[4,256]{1,0:T(4,128)}, u32[]{:S(2)}) copy-start(s32[4,256]{1,0:T(4,128)} %orient_ref.1) | copy-start | bytes 12292
  0.7 17.1 %copy-start.8 = (f32[4,21,56]{2,0,1:T(4,128)S(1)}, f32[4,21,56]{2,0,1:T(4,128)}, u32[]{:S(2)}) copy-start(f32[4,21,56]{2,0,1:T(4,128)} %param.26) | copy-start | bytes 56452
  0.7 21.3 %copy-start = (f32[21,128,256]{2,1,0:T(8,128)S(1)}, f32[21,128,256]{2,1,0:T(8,128)}, u32[]{:S(2)}) copy-start(f32[21,128,256]{2,1,0:T(8,128)} %refs_19_.1) | copy-start | bytes 8257540
  0.7 21.3 %copy-start.14 = (s32[128]{0:T(128)S(1)}, s32[128]{0:T(128)}, u32[]{:S(2)}) copy-start(s32[128]{0:T(128)} %param.33) | copy-start | bytes 1540
  0.7 21.3 %copy-start.13 = (s32[128,1]{0,1:T(1,128)S(1)}, s32[128,1]{0,1:T(1,128)}, u32[]{:S(2)}) copy-start(s32[128,1]{0,1:T(1,128)} %param.32) | copy-start | bytes 1540
  0.7 21.3 %copy-start.12 = (s32[128]{0:T(128)S(1)}, s32[128]{0:T(128)}, u32[]{:S(2)}) copy-start(s32[128]{0:T(128)} %param.31) | copy-start | bytes 1540
  0.8 21.3 %copy-start.2 = (f32[4,9,9,256]{3,0,2,1:T(4,128)S(1)}, f32[4,9,9,256]{3,0,2,1:T(4,128)}, u32[]{:S(2)}) copy-start(f32[4,9,9,256]{3,0,2,1:T(4,128)} %param.27) | copy-start | bytes 995332
  10.3 11.6 %collective-permute-start = (f32[256,128]{1,0:T(8,128)S(1)}, f32[256,128]{1,0:T(8,128)S(1)}, u32[]{:S(2)}, u32[]{:S(2)}) collective-permute-start(f32[256,128]{1,0:T(8,128)S(1)} %get-tuple-element.43), channel_id=1, source_target_pairs={{0,4},{4,8},{8,12},{12,16},{16,20},{20,24},{24,28},{28,0},{1,5},{5... | collective-permute-start | bytes 393224 | tf_op jit(solution)/shard_map/ppermute | solution.py:705
  12.4 9.5 %collective-permute-start.1 = (f32[256,128]{1,0:T(8,128)S(1)}, f32[256,128]{1,0:T(8,128)S(1)}, u32[]{:S(2)}, u32[]{:S(2)}) collective-permute-start(f32[256,128]{1,0:T(8,128)S(1)} %get-tuple-element.44), channel_id=1, source_target_pairs={{0,28},{4,0},{8,4},{12,8},{16,12},{20,16},{24,20},{28,24},{1,29},{... | collective-permute-start | bytes 393224 | tf_op jit(solution)/shard_map/ppermute | solution.py:705
  15.5 6.1 %collective-permute-start.2 = (f32[224,128]{1,0:T(8,128)S(1)}, f32[224,128]{1,0:T(8,128)S(1)}, u32[]{:S(2)}, u32[]{:S(2)}) collective-permute-start(f32[224,128]{1,0:T(8,128)S(1)} %get-tuple-element.45), channel_id=1, source_target_pairs={{0,1},{1,2},{2,3},{3,0},{4,5},{5,6},{6,7},{7,4},{8,9},{9,10},{10,1... | collective-permute-start | bytes 344072 | tf_op jit(solution)/shard_map/ppermute | solution.py:705
  17.7 4.2 %collective-permute-start.3 = (f32[224,128]{1,0:T(8,128)S(1)}, f32[224,128]{1,0:T(8,128)S(1)}, u32[]{:S(2)}, u32[]{:S(2)}) collective-permute-start(f32[224,128]{1,0:T(8,128)S(1)} %get-tuple-element.46), channel_id=1, source_target_pairs={{0,3},{1,0},{2,1},{3,2},{4,7},{5,4},{6,5},{7,6},{8,11},{9,8},{10,9... | collective-permute-start | bytes 344072 | tf_op jit(solution)/shard_map/ppermute | solution.py:705
  34.1 23.3 %copy-start.21 = (f32[224,128]{1,0:T(8,128)S(1)}, f32[224,128]{1,0:T(8,128)}, u32[]{:S(2)}) copy-start(f32[224,128]{1,0:T(8,128)} %get-tuple-element.56) | copy-start | bytes 344068
  34.1 23.3 %copy-start.20 = (f32[224,128]{1,0:T(8,128)S(1)}, f32[224,128]{1,0:T(8,128)}, u32[]{:S(2)}) copy-start(f32[224,128]{1,0:T(8,128)} %get-tuple-element.57) | copy-start | bytes 344068
  34.1 25.2 %copy-start.19 = (f32[224,128]{1,0:T(8,128)S(1)}, f32[224,128]{1,0:T(8,128)}, u32[]{:S(2)}) copy-start(f32[224,128]{1,0:T(8,128)} %get-tuple-element.58) | copy-start | bytes 344068
  34.1 16.9 %all-to-all-start = ((f32[32,4,640]{2,1,0:T(4,128)}), f32[32,4,640]{2,1,0:T(4,128)S(1)}, u32[]{:S(2)}, u32[]{:S(2)}) async-start(f32[32,4,640]{2,1,0:T(4,128)} %get-tuple-element.68), calls=%async_computation | async-start | bytes 655360 | tf_op jit(solution)/shard_map/all_to_all | solution.py:801
  37.7 25.0 %collective-permute-start.4 = (f32[224,128]{1,0:T(8,128)}, f32[224,128]{1,0:T(8,128)S(1)}, u32[]{:S(2)}, u32[]{:S(2)}) collective-permute-start(f32[224,128]{1,0:T(8,128)} %get-tuple-element.55), channel_id=1, source_target_pairs={{0,4},{4,8},{8,12},{12,16},{16,20},{20,24},{24,28},{28,0},{1,5},{5... | collective-permute-start | bytes 344072 | tf_op jit(solution)/shard_map/ppermute | solution.py:705
  53.2 6.1 %collective-permute-start.8 = (f32[80,256]{1,0:T(8,128)S(1)}, f32[80,256]{1,0:T(8,128)S(1)}, u32[]{:S(2)}, u32[]{:S(2)}) collective-permute-start(f32[80,256]{1,0:T(8,128)S(1)} %get-tuple-element.74), channel_id=1, source_target_pairs={{0,4},{4,8},{8,12},{12,16},{16,20},{20,24},{24,28},{28,0},{1,5},{5... | collective-permute-start | bytes 245768 | tf_op jit(solution)/shard_map/ppermute | solution.py:705
  54.0 7.9 %collective-permute-start.9 = (f32[80,256]{1,0:T(8,128)S(1)}, f32[80,256]{1,0:T(8,128)S(1)}, u32[]{:S(2)}, u32[]{:S(2)}) collective-permute-start(f32[80,256]{1,0:T(8,128)S(1)} %get-tuple-element.75), channel_id=1, source_target_pairs={{0,28},{4,0},{8,4},{12,8},{16,12},{20,16},{24,20},{28,24},{1,29},{... | collective-permute-start | bytes 245768 | tf_op jit(solution)/shard_map/ppermute | solution.py:705
  57.4 11.1 %collective-permute-start.5 = (f32[224,128]{1,0:T(8,128)S(1)}, f32[224,128]{1,0:T(8,128)S(1)}, u32[]{:S(2)}, u32[]{:S(2)}) collective-permute-start(f32[224,128]{1,0:T(8,128)S(1)} %copy-done.21), channel_id=1, source_target_pairs={{0,28},{4,0},{8,4},{12,8},{16,12},{20,16},{24,20},{28,24},{1,29},{... | collective-permute-start | bytes 344072 | tf_op jit(solution)/shard_map/ppermute | solution.py:705
  57.4 11.1 %collective-permute-start.6 = (f32[224,128]{1,0:T(8,128)S(1)}, f32[224,128]{1,0:T(8,128)S(1)}, u32[]{:S(2)}, u32[]{:S(2)}) collective-permute-start(f32[224,128]{1,0:T(8,128)S(1)} %copy-done.20), channel_id=1, source_target_pairs={{0,1},{1,2},{2,3},{3,0},{4,5},{5,6},{6,7},{7,4},{8,9},{9,10},{10,1... | collective-permute-start | bytes 344072 | tf_op jit(solution)/shard_map/ppermute | solution.py:705
  59.3 9.2 %collective-permute-start.7 = (f32[224,128]{1,0:T(8,128)S(1)}, f32[224,128]{1,0:T(8,128)S(1)}, u32[]{:S(2)}, u32[]{:S(2)}) collective-permute-start(f32[224,128]{1,0:T(8,128)S(1)} %copy-done.19), channel_id=1, source_target_pairs={{0,3},{1,0},{2,1},{3,2},{4,7},{5,4},{6,5},{7,6},{8,11},{9,8},{10,9... | collective-permute-start | bytes 344072 | tf_op jit(solution)/shard_map/ppermute | solution.py:705
  62.6 11.2 %copy-start.1 = (f32[5,272,256]{2,1,0:T(8,128)S(1)}, f32[5,272,256]{2,1,0:T(8,128)}, u32[]{:S(2)}) copy-start(f32[5,272,256]{2,1,0:T(8,128)} %get-tuple-element.81.refs_1_) | copy-start | bytes 4177924
  62.6 11.2 %copy-start.6 = (bf16[512,384]{1,0:T(8,128)(2,1)S(1)}, bf16[512,384]{1,0:T(8,128)(2,1)}, u32[]{:S(2)}) copy-start(bf16[512,384]{1,0:T(8,128)(2,1)} %constant.17.clone.refs_5_) | copy-start | bytes 1179652
  62.6 11.2 %copy-start.7 = (bf16[512,384]{1,0:T(8,128)(2,1)S(1)}, bf16[512,384]{1,0:T(8,128)(2,1)}, u32[]{:S(2)}) copy-start(bf16[512,384]{1,0:T(8,128)(2,1)} %constant.16.clone.refs_4_) | copy-start | bytes 1179652
  62.6 11.1 %collective-permute-start.10 = (f32[272,128]{1,0:T(8,128)S(1)}, f32[272,128]{1,0:T(8,128)S(1)}, u32[]{:S(2)}, u32[]{:S(2)}) collective-permute-start(f32[272,128]{1,0:T(8,128)S(1)} %get-tuple-element.82), channel_id=1, source_target_pairs={{0,1},{1,2},{2,3},{3,0},{4,5},{5,6},{6,7},{7,4},{8,9},{9,10},{10,1... | collective-permute-start | bytes 417800 | tf_op jit(solution)/shard_map/ppermute | solution.py:705
  62.7 5.9 %copy-start.15 = (f32[224,128]{1,0:T(8,128)}, f32[224,128]{1,0:T(8,128)S(1)}, u32[]{:S(2)}) copy-start(f32[224,128]{1,0:T(8,128)S(1)} %collective-permute-done.4.a0) | copy-start | bytes 344068
  62.7 11.0 %collective-permute-start.11 = (f32[272,128]{1,0:T(8,128)S(1)}, f32[272,128]{1,0:T(8,128)S(1)}, u32[]{:S(2)}, u32[]{:S(2)}) collective-permute-start(f32[272,128]{1,0:T(8,128)S(1)} %get-tuple-element.83), channel_id=1, source_target_pairs={{0,3},{1,0},{2,1},{3,2},{4,7},{5,4},{6,5},{7,6},{8,11},{9,8},{10,9... | collective-permute-start | bytes 417800 | tf_op jit(solution)/shard_map/ppermute | solution.py:705
  (3 other events, 2.0 us)

commit v2 on v1

--- a/solution.py
+++ b/solution.py
@@ -77,7 +77,7 @@
 HBM = "hbm"
 
 
-def call(body, outs, scratch, *args, micros, limit=20, held=()):
+def call(body, outs, scratch, *args, micros, limit=20, held=(), flags=None):
     def spec(in_hbm):
         return pl.BlockSpec(memory_space=pltpu.HBM if in_hbm else pltpu.VMEM)
 
@@ -91,7 +91,9 @@
         out_specs=[spec(len(o) == 3) for o in outs],
         out_shape=[(pltpu.HBM if len(o) == 3 else jax.ShapeDtypeStruct)(o[0], o[1]) for o in outs],
         scratch_shapes=[pltpu.VMEM(*x) if isinstance(x, tuple) else x for x in scratch],
-        compiler_params=pltpu.CompilerParams(vmem_limit_bytes=limit * 2**20),
+        compiler_params=pltpu.CompilerParams(
+            vmem_limit_bytes=limit * 2**20, **({"flags": flags} if flags else {})
+        ),
         cost_estimate=pl.CostEstimate(
             flops=micros * 10**8, bytes_accessed=micros * 3 * 10**6, transcendentals=0
         ),
@@ -241,18 +243,36 @@
             )
 
 
-def send_gather(own_ref, send_ref, left_ref, outs):
+def is_even(axis):
+    return lax.axis_index(axis) % 2 == 0
+
+
+def send_gather(axes, own_ref, send_ref, left_ref, outs):
     rows, faces = own_ref.shape
     hi, lo = split(own_ref[...])
     left_ref[0:rows] = hi
     left_ref[rows : 2 * rows] = lo
     slots = send_ref.shape[3]
-    for k in range(0, 4, 2):
-        picks = jnp.concatenate([send_ref[0, 0, k : k + 1], send_ref[0, 0, k + 1 : k + 2]], axis=1)
+    for k, axis in enumerate(axes):
+        even = is_even(axis)
+        to_low = send_ref[0, 0, 2 * k : 2 * k + 1]
+        to_high = send_ref[0, 0, 2 * k + 1 : 2 * k + 2]
+        picks = jnp.concatenate(
+            [jnp.where(even, to_low, to_high), jnp.where(even, to_high, to_low)], axis=1
+        )
         res = mm(left_ref[...], hot(iota((faces, 2 * slots), 0) == picks))
         res = res[:rows] + res[rows:]
-        outs[k][0:rows] = res[:, :slots]
-        outs[k + 1][0:rows] = res[:, slots:]
+        outs[2 * k][0:rows] = res[:, :slots]
+        outs[2 * k + 1][0:rows] = res[:, slots:]
+
+
+def by_direction(axes, arrived):
+    ordered = []
+    for k, axis in enumerate(axes):
+        even = is_even(axis)
+        odd_one, even_one = arrived[2 * k], arrived[2 * k + 1]
+        ordered += [jnp.where(even, odd_one, even_one), jnp.where(even, even_one, odd_one)]
+    return ordered
 
 
 def row_of(ref):
@@ -276,10 +296,9 @@
         jump_ref[:, at] = own_refs[0][:, at] - (res[:rows] + res[rows:])
 
 
-def surface(arrived, slot_turn, codes, jump_ref, flux_m_ref, perm_ref, wl_ref, base_ref, scratch, out_ref):
-    left_ref, part_ref, flux_ref = scratch
+def full_jump(arrived, slot_turn, codes, jump_ref, perm_ref, left_ref, part_ref):
     rows, faces = jump_ref.shape
-    variables, basis, elems = base_ref.shape
+    elems = faces // 4
     value = jnp.concatenate(arrived, axis=1)
     slots = value.shape[1]
     hi, lo = split(value)
@@ -295,6 +314,10 @@
         at = slice(q * elems, (q + 1) * elems)
         res = mm(left_ref[...], hot(iota((slots, elems), 0) + faces == codes[:, at]))
         part_ref[:, at] = jump_ref[:, at] - (res[:rows] + res[rows:])
+
+
+def correct(part_ref, flux_m_ref, wl_ref, base_ref, flux_ref, out_ref):
+    variables, basis, elems = base_ref.shape
     np_ = flux_ref.shape[1] // 4
 
     group = 3
@@ -321,6 +344,7 @@
 
 
 def first_kernel(
+    axes,
     state_hbm, star_hbm, deriv_hbm, trace_hbm, place_hbm, send_hbm, sea_hbm, depth_hbm, wet_hbm,
     w_ref, wt_ref, integ_ref, lifted_ref, o0, o1, o2, o3,
     star_ref, deriv_ref, trace_ref, place_ref, send_ref, own_ref,
@@ -347,30 +371,25 @@
     finish(later)
     prep_trace(trace_ref, place_ref, stage_ref, wt_ref)
     traces(integ_ref, wt_ref, (own_ref,))
-    send_gather(own_ref, send_ref, left_ref, (o0, o1, o2, o3))
+    send_gather(axes, own_ref, send_ref, left_ref, (o0, o1, o2, o3))
     rows = own_ref.shape[0]
     np_ = lifted_ref.shape[0]
     lifted_ref[...] = own_ref[2 * np_ : 3 * np_, :]
-    for side, (out, at) in enumerate(((o0, 0), (o1, EDGE - STEPS))):
-        for j in range(5):
-            if j < 3:
-                edge = sea_edge[side, j]
-            else:
-                edge = depth_edge[side] if j == 3 else wet_edge[side].astype(F32)
+    even = is_even(axes[0])
+    for j in range(5):
+        if j < 3:
+            low, high = sea_edge[0, j], sea_edge[1, j]
+        else:
+            ref = depth_edge if j == 3 else wet_edge
+            low, high = ref[0].astype(F32), ref[1].astype(F32)
+        low, high = low[:STEPS], high[EDGE - STEPS :]
+        for out, edge in ((o0, jnp.where(even, low, high)), (o1, jnp.where(even, high, low))):
             for h in range(edge.shape[1] // LANES):
                 begin = rows + h * SEA_ROWS + j * STEPS
-                out[begin : begin + STEPS] = edge[
-                    at : at + STEPS, h * LANES : (h + 1) * LANES
-                ]
-
-
-def local_work(
-    integ_ref, field_ref, star_ref, w_ref, wt_ref, turn, codes, jump_ref, base_ref,
-    own_refs, left_ref, moved_ref, total_ref,
-):
-    traces(integ_ref, wt_ref, own_refs)
-    local_jump(own_refs, turn, codes, left_ref, jump_ref)
-
+                out[begin : begin + STEPS] = edge[:, h * LANES : (h + 1) * LANES]
+
+
+def own_derivative(integ_ref, field_ref, star_ref, w_ref, base_ref, moved_ref, total_ref):
     def emit(u, at, acc):
         base_ref[u, :, at] = field_ref[u, :, at] - acc
 
@@ -400,35 +419,36 @@
         [(turn_ref, turn_out), (slot_ref, slot_out), (wl_ref, wl_out), (w_ref, w_out),
          (wt_ref, wt_out)], sem_ref,
     )
-    local_work(
-        integ_ref, field_ref, star_ref, w_ref, wt_ref, turn_ref[0:1, :], codes, jump_ref, base_ref,
-        (own0, own1, own2), left_ref, moved_ref, total_ref,
-    )
+    own_refs = (own0, own1, own2)
+    traces(integ_ref, wt_ref, own_refs)
+    local_jump(own_refs, turn_ref[0:1, :], codes, left_ref, jump_ref)
+    own_derivative(integ_ref, field_ref, star_ref, w_ref, base_ref, moved_ref, total_ref)
     finish(copies)
 
 
 def second_kernel(
-    capacity, nodes,
+    axes, capacity, nodes,
     a0, a1, a2, a3, slot_ref, codes_ref, jump_ref, flux_m_ref, perm_ref, wl_ref, base_ref,
     star_ref, w_ref, wt_ref, send_ref, lifted_ref, faces_ref, owner_ref, blocks_ref, weights_ref,
-    pay_ref, field_out, integ_out, edge_low, edge_high, s0, s1, s2, s3,
+    pay_ref, field_out, integ_out, edge_odd, edge_even, s0, s1, s2, s3,
     field_ref, integ_ref, own_ref, o0, o1, o2, o3,
     arr_left_ref, part_ref, flux_ref, moved_ref, term_ref, total_ref, left_ref,
     disp_ref, rows_ref, sem_ref,
 ):
     rows = jump_ref.shape[0]
     tail = pl.ds(rows, a0.shape[0] - rows)
-    copies = start([(a0.at[tail], edge_low), (a1.at[tail], edge_high)], sem_ref)
-    surface(
-        [a[0:rows] for a in (a0, a1, a2, a3)], slot_ref[0:1, :], row_of(codes_ref), jump_ref,
-        flux_m_ref, perm_ref, wl_ref, base_ref, (arr_left_ref, part_ref, flux_ref), field_ref,
-    )
+    copies = start([(a0.at[tail], edge_odd), (a1.at[tail], edge_even)], sem_ref)
+    full_jump(
+        by_direction(axes, [a[0:rows] for a in (a0, a1, a2, a3)]), slot_ref[0:1, :], row_of(codes_ref), jump_ref,
+        perm_ref, arr_left_ref, part_ref,
+    )
+    correct(part_ref, flux_m_ref, wl_ref, base_ref, flux_ref, field_ref)
     copies += start([(field_ref, field_out)], sem_ref, 2)
     term_ref[...] = field_ref[...]
     predict(star_ref, w_ref, moved_ref, term_ref, integ_ref, total_ref)
     copies += start([(integ_ref, integ_out)], sem_ref, 3)
     traces(integ_ref, wt_ref, (own_ref,))
-    send_gather(own_ref, send_ref, left_ref, (o0, o1, o2, o3))
+    send_gather(axes, own_ref, send_ref, left_ref, (o0, o1, o2, o3))
     copies += start([(o0, s0), (o1, s1), (o2, s2), (o3, s3)], sem_ref, 4)
     np_ = lifted_ref.shape[0]
     project(
@@ -438,40 +458,67 @@
     finish(copies)
 
 
-def local_second_kernel(
+def window_kernel(
+    axes,
+    sea_hbm, depth_hbm, wet_hbm, low_hbm, high_hbm,
     integ_hbm, field_hbm, star_hbm, w_hbm, wt_hbm, turn_hbm, codes_hbm,
-    jump_out, base_out,
+    ext_out, right_out, left_out, jump_out, base_out,
+    ext_ref, wet_ref, low_ref, high_ref, right_ref, left_ref,
     integ_ref, field_ref, star_ref, w_ref, wt_ref, turn_ref, codes_ref, jump_ref, base_ref,
-    own0, own1, own2, left_ref, moved_ref, total_ref, sem_ref,
+    own0, own1, own2, left_rows, moved_ref, total_ref, sem_ref,
 ):
     copies = start(
-        [(integ_hbm, integ_ref), (wt_hbm, wt_ref), (turn_hbm, turn_ref), (codes_hbm, codes_ref),
-         (star_hbm, star_ref), (w_hbm, w_ref), (field_hbm, field_ref)], sem_ref,
-    )
+        [(wt_hbm, wt_ref), (integ_hbm, integ_ref), (turn_hbm, turn_ref), (codes_hbm, codes_ref),
+         (w_hbm, w_ref), (star_hbm, star_ref), (field_hbm, field_ref)], sem_ref,
+    )
+    body = pl.ds(0, depth_hbm.shape[0])
+    sea = start(
+        [(sea_hbm.at[j], ext_ref.at[j, body]) for j in range(3)]
+        + [(depth_hbm, ext_ref.at[3, body]), (wet_hbm, wet_ref), (low_hbm, low_ref),
+           (high_hbm, high_ref)], sem_ref, 7,
+    )
+    finish(copies[:2])
+    own_refs = (own0, own1, own2)
+    traces(integ_ref, wt_ref, own_refs)
+    finish(copies[2:4])
+    local_jump(own_refs, turn_ref[0:1, :], row_of(codes_ref), left_rows, jump_ref)
+    written = start([(jump_ref, jump_out)], sem_ref, 14)
+    finish(copies[4:])
+    own_derivative(integ_ref, field_ref, star_ref, w_ref, base_ref, moved_ref, total_ref)
+    written += start([(base_ref, base_out)], sem_ref, 15)
+    finish(sea)
+    shore(axes, ext_ref, wet_ref, low_ref, high_ref, right_ref, left_ref)
+    written += start(
+        [(ext_ref, ext_out), (right_ref, right_out), (left_ref, left_out)], sem_ref, 16
+    )
+    finish(written)
+
+
+def last_jump_kernel(
+    axes,
+    a0, a1, a2, a3, slot_hbm, codes_hbm, jump_hbm, perm_hbm,
+    part_ref,
+    b0, b1, b2, b3, slot_ref, codes_ref, jump_ref, perm_ref, arr_left_ref, sem_ref,
+):
+    finish(
+        start(
+            [(a0, b0), (a1, b1), (a2, b2), (a3, b3), (slot_hbm, slot_ref), (perm_hbm, perm_ref),
+             (codes_hbm, codes_ref), (jump_hbm, jump_ref)], sem_ref,
+        )
+    )
+    full_jump(
+        by_direction(axes, [b0[...], b1[...], b2[...], b3[...]]), slot_ref[0:1, :], row_of(codes_ref), jump_ref,
+        perm_ref, arr_left_ref, part_ref,
+    )
+
+
+def last_kernel(
+    part_ref, flux_m_hbm, wl_hbm, base_hbm, field_out,
+    flux_m_ref, wl_ref, base_ref, field_ref, flux_ref, sem_ref,
+):
+    copies = start([(flux_m_hbm, flux_m_ref), (wl_hbm, wl_ref), (base_hbm, base_ref)], sem_ref)
     finish(copies)
-    local_work(
-        integ_ref, field_ref, star_ref, w_ref, wt_ref, turn_ref[0:1, :], row_of(codes_ref),
-        jump_ref, base_ref, (own0, own1, own2), left_ref, moved_ref, total_ref,
-    )
-    finish(start([(jump_ref, jump_out), (base_ref, base_out)], sem_ref, 7))
-
-
-def last_kernel(
-    a0, a1, a2, a3, slot_hbm, codes_hbm, jump_hbm, flux_m_hbm, perm_hbm, wl_hbm, base_hbm,
-    field_out,
-    b0, b1, b2, b3, slot_ref, codes_ref, jump_ref, flux_m_ref, perm_ref, wl_ref, base_ref,
-    field_ref, arr_left_ref, part_ref, flux_ref, sem_ref,
-):
-    copies = start(
-        [(a0, b0), (a1, b1), (a2, b2), (a3, b3), (slot_hbm, slot_ref), (perm_hbm, perm_ref),
-         (codes_hbm, codes_ref), (jump_hbm, jump_ref), (flux_m_hbm, flux_m_ref),
-         (wl_hbm, wl_ref), (base_hbm, base_ref)], sem_ref,
-    )
-    finish(copies)
-    surface(
-        [b0[...], b1[...], b2[...], b3[...]], slot_ref[0:1, :], row_of(codes_ref), jump_ref,
-        flux_m_ref, perm_ref, wl_ref, base_ref, (arr_left_ref, part_ref, flux_ref), field_ref,
-    )
+    correct(part_ref, flux_m_ref, wl_ref, base_ref, flux_ref, field_ref)
     finish(start([(field_ref, field_out)], sem_ref))
 
 
@@ -523,9 +570,10 @@
 
 
 def raster_kernel(
-    pay_ref, b_hi_hbm, b_lo_hbm, right_hbm, left_hbm,
-    uplift_ref, up_ref, down_ref, b_hi, b_lo, right_ref, left_ref, got_ref, sem_ref,
-):
+    axis, pay_ref, b_hi_hbm, b_lo_hbm, right_hbm, left_hbm,
+    uplift_ref, odd_ref, even_ref, b_hi, b_lo, right_ref, left_ref, got_ref, sem_ref,
+):
+    even = is_even(axis)
     later = start(
         [(b_hi_hbm, b_hi), (b_lo_hbm, b_lo), (right_hbm, right_ref), (left_hbm, left_ref)],
         sem_ref,
@@ -555,43 +603,35 @@
             x = jnp.where(low_row == low_col, x, jnp.where(low_row, from_above, from_below))
             step *= 2
         uplift_ref[t] = x
-        up_ref[t * HALO_X : (t + 1) * HALO_X] = x[tile_x - HALO_X :, :]
-        down_ref[t * HALO_X : (t + 1) * HALO_X] = x[:HALO_X, :]
+        up, down = x[tile_x - HALO_X :, :], x[:HALO_X, :]
+        even_ref[t * HALO_X : (t + 1) * HALO_X] = jnp.where(even, up, down)
+        odd_ref[t * HALO_X : (t + 1) * HALO_X] = jnp.where(even, down, up)
     finish(later)
 
 
-def shore_kernel(
-    axes, sea_hbm, depth_hbm, wet_hbm, low_hbm, high_hbm,
-    ext_out, right_out, left_out,
-    ext_ref, wet_ref, low_ref, high_ref, right_ref, left_ref, sem_ref,
-):
-    tile_x, tile_y = depth_hbm.shape
-    body = pl.ds(0, tile_x)
-    finish(
-        start(
-            [(sea_hbm.at[j], ext_ref.at[j, body]) for j in range(3)]
-            + [(depth_hbm, ext_ref.at[3, body]), (wet_hbm, wet_ref), (low_hbm, low_ref),
-               (high_hbm, high_ref)], sem_ref,
-        )
-    )
+def shore(axes, ext_ref, wet_ref, odd_ref, even_ref, right_ref, left_ref):
+    tile_x, tile_y = wet_ref.shape
     ext_ref[4, 0:tile_x, :] = wet_ref[...].astype(F32)
     at_x = lax.axis_index(axes[0])
     has_low = at_x > 0
     has_high = at_x < lax.axis_size(axes[0]) - 1
 
-    def edge_of(ref, present, j, before):
+    even = is_even(axes[0])
+    low = jnp.where(even, odd_ref[...], even_ref[...])
+    high = jnp.where(even, even_ref[...], odd_ref[...])
+
+    def edge_of(edges, present, j, before):
         halves = []
         for h in range(tile_y // LANES):
             begin = h * SEA_ROWS + j * STEPS
-            halves.append(ref[begin : begin + STEPS, :])
+            halves.append(edges[begin : begin + STEPS, :])
         value = jnp.where(present, jnp.concatenate(halves, axis=1), 0.0)
         blank = jnp.zeros((EDGE - STEPS, tile_y), F32)
         return jnp.concatenate([blank, value] if before else [value, blank], axis=0)
 
     for j in range(5):
-        ext_ref[j, tile_x : tile_x + EDGE, :] = edge_of(high_ref, has_high, j, False)
-        ext_ref[j, tile_x + EDGE : tile_x + 2 * EDGE, :] = edge_of(low_ref, has_low, j, True)
-    copies = start([(ext_ref, ext_out)], sem_ref)
+        ext_ref[j, tile_x : tile_x + EDGE, :] = edge_of(high, has_high, j, False)
+        ext_ref[j, tile_x + EDGE : tile_x + 2 * EDGE, :] = edge_of(low, has_low, j, True)
     lane = iota(right_ref.shape, 1)
     right = jnp.zeros(right_ref.shape, F32)
     left = right
@@ -605,26 +645,24 @@
         left = jnp.where(lane < moved, left, pltpu.roll(first, moved, 1))
     right_ref[...] = right
     left_ref[...] = left
-    finish(copies + start([(right_ref, right_out), (left_ref, left_out)], sem_ref, 1))
 
 
 def along_x_kernel(
-    axes, uplift_ref, low_ref, high_ref, b_hi, b_lo, sea_right, sea_left,
-    along_ref, right_ref, left_ref,
+    axes, uplift_ref, odd_ref, even_ref, b_hi, b_lo, sea_right, sea_left,
+    along_ref, odd_out, even_out,
 ):
     _, tile_y = uplift_ref.shape[1:]
     at_x = lax.axis_index(axes[0])
+    even_x = is_even(axes[0])
+    even_y = is_even(axes[1])
     has_low = at_x > 0
     has_high = at_x < lax.axis_size(axes[0]) - 1
     for t in range(STEPS):
         at = slice(t * HALO_X, (t + 1) * HALO_X)
+        high = jnp.where(even_x, even_ref[at, :], odd_ref[at, :])
+        low = jnp.where(even_x, odd_ref[at, :], even_ref[at, :])
         value = jnp.concatenate(
-            [
-                uplift_ref[t],
-                jnp.where(has_high, high_ref[at, :], 0.0),
-                jnp.where(has_low, low_ref[at, :], 0.0),
-            ],
-            axis=0,
+            [uplift_ref[t], jnp.where(has_high, high, 0.0), jnp.where(has_low, low, 0.0)], axis=0
         )
         hi, lo = split(value)
         along_ref[t] = mm(b_hi[...], hi) + mm(b_hi[...], lo) + mm(b_lo[...], hi)
@@ -641,16 +679,21 @@
             tail, head = pltpu.roll(tail, LANES - moved, 1), pltpu.roll(head, moved, 1)
         right = jnp.where(lane >= LANES - moved - HALO_Y, tail, right)
         left = jnp.where(lane < moved + HALO_Y, head, left)
-    right_ref[...] = right
-    left_ref[...] = left
-
-
-def ocean_kernel(axes, along_ref, ext_ref, low_ref, high_ref, b_hi, b_lo, out_ref):
+    even_out[...] = jnp.where(even_y, right, left)
+    odd_out[...] = jnp.where(even_y, left, right)
+
+
+def ocean_kernel(
+    axes, along_ref, ext_ref, odd_ref, even_ref, b_hi, b_lo, out_hbm, out_ref, sem_ref
+):
     tall, tile_y = along_ref.shape[1:]
     tile_x = out_ref.shape[1]
     at_y = lax.axis_index(axes[1])
-    low = jnp.where(at_y > 0, low_ref[...], 0.0)
-    high = jnp.where(at_y < lax.axis_size(axes[1]) - 1, high_ref[...], 0.0)
+    even = is_even(axes[1])
+    low = jnp.where(even, odd_ref[...], even_ref[...])
+    high = jnp.where(even, even_ref[...], odd_ref[...])
+    low = jnp.where(at_y > 0, low, 0.0)
+    high = jnp.where(at_y < lax.axis_size(axes[1]) - 1, high, 0.0)
     lane = iota((tall, LANES), 1)
     forces = []
     for t in range(STEPS):
@@ -695,14 +738,29 @@
         east_new = mean[1] - factor * (east * east_x + north * east_y + eta_x)
         north_new = mean[2] - factor * (east * north_x + north * north_y + eta_y)
         eta, east, north = eta_new * wet, east_new * wet, north_new * wet
-    out_ref[0] = eta[:tile_x, :tile_y]
-    out_ref[1] = east[:tile_x, :tile_y]
-    out_ref[2] = north[:tile_x, :tile_y]
-
-
-def shift(value, axis, step):
-    count = lax.axis_size(axis)
-    return lax.ppermute(value, axis, [(i, (i + step) % count) for i in range(count)])
+    copies = []
+    for j, value in enumerate((eta, east, north)):
+        out_ref[j] = value[:tile_x, :tile_y]
+        copies += start([(out_ref.at[j], out_hbm.at[j])], sem_ref, j)
+    finish(copies)
+
+
+def swap(value, axes, along, odd):
+    counts = [lax.axis_size(axis) for axis in axes]
+    other = 1 - along
+    pairs = []
+    for x in range(counts[0]):
+        for y in range(counts[1]):
+            at = [x, y]
+            to = list(at)
+            to[along] = ((at[along] - odd) ^ 1) + odd
+            if not 0 <= to[along] < counts[along]:
+                to = list(at)
+                to[other] = at[other] ^ 1
+                if to[other] >= counts[other]:
+                    to = list(at)
+            pairs.append((x * counts[1] + y, to[0] * counts[1] + to[1]))
+    return lax.ppermute(value, axes, pairs)
 
 
 def on_device(
@@ -744,11 +802,14 @@
     flux = ((variables, 4 * np_, elems), F32)
     stage = ((4 * nodes, basis), F32)
 
+    axes = ("gx", "gy")
+
     def sent(outgoing):
-        return [
-            shift(outgoing[1], "gx", 1), shift(outgoing[0], "gx", -1),
-            shift(outgoing[3], "gy", 1), shift(outgoing[2], "gy", -1),
-        ]
+        moved = []
+        for k in (0, 1):
+            for odd in (1, 0):
+                moved.append(swap(outgoing[len(moved)], axes, k, odd))
+        return moved
 
     w_of = ((3 * basis, 3 * kb), BF16)
     wt_of = ((12 * np_, 3 * kb), BF16)
@@ -765,7 +826,7 @@
         return (*array, HBM)
 
     w, wt, integ, lifted_a, *outgoing = call(
-        first_kernel,
+        lambda *refs: first_kernel(axes, *refs),
         [w_of, wt_of, field_of, lifted_of] + [(out_x, F32)] * 2 + [out_of] * 2,
         [star_of, (deriv.shape, F32), (trace_ops.shape, F32), (place.shape, BF16),
          (send_faces.shape, send_faces.dtype), wide_of, moved, field_of, field_of, left, stage,
@@ -787,8 +848,8 @@
     devs = lax.axis_size("gx") * lax.axis_size("gy")
     capacity = max(2, (sea_rows + devs - 1) // devs)
     message = (devs, capacity, STEPS * cells + LANES)
-    payload, field_h, integ_h, edge_low, edge_high, *outgoing = call(
-        lambda *refs: second_kernel(capacity, nodes, *refs),
+    payload, field_h, integ_h, edge_odd, edge_even, *outgoing = call(
+        lambda *refs: second_kernel(axes, capacity, nodes, *refs),
         [(message, F32), hbm(field_of), hbm(field_of)]
         + [((out_x[0] - rows, slots), F32, HBM)] * 2 + [hbm(out_of)] * 4,
         [field_of, field_of, wide_of] + [out_of] * 4
@@ -804,26 +865,27 @@
     axes = ("gx", "gy")
     ext_of = ((5, tall, tile_y), F32)
     strip_of = ((tall, LANES), F32)
-    edge_of = (edge_low.shape, F32)
-    ext_h, right_h, left_h = call(
-        lambda *refs: shore_kernel(axes, *refs),
-        [hbm(ext_of), hbm(strip_of), hbm(strip_of)],
-        [ext_of, (wet.shape, wet.dtype), edge_of, edge_of, strip_of, strip_of, sems(7)],
-        sea_state, depth, wet, edge_low, edge_high, micros=2, held=range(5),
-    )
-    jump_h, base_h = call(
-        local_second_kernel, [hbm(wide_of), hbm(field_of)],
-        [field_of, field_of, star_of, w_of, wt_of, turn_of, codes_of, wide_of, field_of,
-         wide_of, wide_of, wide_of, left, moved, field_of, sems(9)],
+    edge_of = (edge_odd.shape, F32)
+    ext_h, right_h, left_h, jump_h, base_h = call(
+        lambda *refs: window_kernel(axes, *refs),
+        [hbm(ext_of), hbm(strip_of), hbm(strip_of), hbm(wide_of), hbm(field_of)],
+        [ext_of, (wet.shape, wet.dtype), edge_of, edge_of, strip_of, strip_of,
+         field_of, field_of, star_of, w_of, wt_of, turn_of, codes_of, wide_of, field_of,
+         wide_of, wide_of, wide_of, left, moved, field_of, sems(19)],
+        sea_state, depth, wet, edge_odd, edge_even,
         integ_h, field_h, star, w_h, wt_h, turn_h, neighbours,
-        micros=5, held=range(7),
+        micros=6, held=range(12),
+    )
+    part, = call(
+        lambda *refs: last_jump_kernel(axes, *refs), [wide_of],
+        [out_of] * 4 + [slot_of, codes_of, wide_of, perm_of, arr_left, sems(8)],
+        *arrived, slot_h, neighbours, jump_h, perm,
+        micros=2, held=range(8),
     )
     elastic, = call(
         last_kernel, [hbm(field_of)],
-        [out_of] * 4 + [slot_of, codes_of, wide_of, flux_m_of, perm_of, wl_of, field_of, field_of,
-         arr_left, wide_of, flux, sems(11)],
-        *arrived, slot_h, neighbours, jump_h, face_flux, perm, wl_h, base_h,
-        micros=4, held=range(11),
+        [flux_m_of, wl_of, field_of, field_of, flux, sems(3)],
+        part, face_flux, wl_h, base_h, micros=2, held=range(1, 4),
     )
 
     halo = ((STEPS * HALO_X, tile_y), F32)
@@ -833,23 +895,26 @@
     read_y = np.concatenate([np.arange(tile_y + LANES), np.arange(-LANES, 0)])
     bx = [jnp.asarray(b) for b in band(cell_x, read_x)]
     by = [jnp.asarray(b.T) for b in band(cell_y, read_y)]
-    uplift, up, down, bx_hi, bx_lo, sea_right, sea_left = call(
-        raster_kernel,
+    uplift, odd, even, bx_hi, bx_lo, sea_right, sea_left = call(
+        lambda *refs: raster_kernel("gx", *refs),
         [((STEPS, tile_x, tile_y), F32), halo, halo]
         + [(b.shape, BF16) for b in bx] + [strip_of, strip_of],
         [((devs * capacity, message[2]), F32), sems(4)],
         got, *bx, right_h, left_h, micros=2, held=range(1, 5),
     )
-    x_low, x_high = shift(up, "gx", 1), shift(down, "gx", -1)
-    along, right, left_going = call(
+    odd = swap(odd, axes, 0, 1)
+    even = swap(even, axes, 0, 0)
+    along, odd_y, even_y = call(
         lambda *refs: along_x_kernel(axes, *refs),
         [((STEPS, tall, tile_y), F32), strip_of, strip_of], [],
-        uplift, x_low, x_high, bx_hi, bx_lo, sea_right, sea_left, micros=1,
-    )
-    y_low, y_high = shift(right, "gy", 1), shift(left_going, "gy", -1)
+        uplift, odd, even, bx_hi, bx_lo, sea_right, sea_left, micros=1,
+    )
+    odd_y = swap(odd_y, axes, 1, 1)
+    even_y = swap(even_y, axes, 1, 0)
+    ocean_of = ((3, tile_x, tile_y), F32)
     ocean, = call(
-        lambda *refs: ocean_kernel(axes, *refs), [((3, tile_x, tile_y), F32)], [],
-        along, ext_h, y_low, y_high, *by, micros=4,
+        lambda *refs: ocean_kernel(axes, *refs), [hbm(ocean_of)], [ocean_of, sems(3)],
+        along, ext_h, odd_y, even_y, *by, micros=4,
     )
     return elastic, ocean
 

time: 79.1 us -> 72 us (0.910); the launches traced: 77.7 us -> 71.7 us
  waiting for transfers between devices: 11.4 us -> 4.62 us
  starting transfers between devices: 19.7 us -> 21.9 us
  Pallas kernels: 44.7 us -> 43.3 us
    all_to_all x1, waiting for transfers between devices: 9.14 us -> 4.59 us  [on_device(): lax.all_to_all(payload, ('gx', 'gy'), split_axis=0, concat_axis=0, tiled=...]
    all_to_all x1, starting transfers between devices: 3.54 us -> 6.28 us  [on_device(): lax.all_to_all(payload, ('gx', 'gy'), split_axis=0, concat_axis=0, tiled=...]
    ppermute x12, waiting for transfers between devices: 2.25 us -> 0.03 us  [swap(): return lax.ppermute(value, axes, pairs)]
    pallas_call x9, Pallas kernels: 44.7 us -> 43.3 us  [call(): pl.pallas_call(body, in_specs=[spec(i in held) for i in range(len(args))]...]
  transfers between devices with their start and end apart: 13 -> 13, of which waited for: 3 -> 1; matrix products, arithmetic and copies ran while one was open for 0% -> 0% of each run, Pallas kernels for 25% -> 25%
where the time goes in v2:
time: 72 us; the launch traced here: 71.7 us
  Pallas kernels  43.3 us (60%)
  starting transfers between devices  21.9 us (30%)
  waiting for transfers between devices  4.62 us (6%)
  between operations  1.21 us (2%)
  local copies, waits for them, and re-layouts  0.76 us (1%)
    pallas_call x9, Pallas kernels, call(): pl.pallas_call(body, in_specs=[spec(i in held) for i in range(len(args))]...  43.3 us
    ppermute x12, starting transfers between devices, swap(): return lax.ppermute(value, axes, pairs)  15.6 us
    all_to_all x1, starting transfers between devices, on_device(): lax.all_to_all(payload, ('gx', 'gy'), split_axis=0, concat_axis=0, tiled=...  6.28 us
    all_to_all x1, waiting for transfers between devices, on_device(): lax.all_to_all(payload, ('gx', 'gy'), split_axis=0, concat_axis=0, tiled=...  4.59 us
  transfers between devices with their start and end apart: 13, of which 1 were waited for; matrix products, arithmetic and copies ran while one was open for 0% of the time, Pallas kernels for 25%

profile of v2, /device:TPU:1, one launch (start us, length us, event | category | flops | bytes accessed | tf_op | source)
XLA Modules:
  0.0 71.7 jit_solution(12755230148897546920)
XLA Ops:
  0.6 0.0 copy-start.4
  0.7 0.0 copy-start
  0.7 0.0 copy-start.8
  0.8 0.0 copy-start.3
  0.8 9.5 %shard_map.221 = (bf16[168,192]{1,0:T(8,128)(2,1)S(1)}, bf16[288,192]{1,0:T(8,128)(2,1)S(1)}, f32[9,56,256]{2,1,0:T(8,128)S(1)}, f32[24,1024]{1,0:T(8,128)S(1)},...) custom-call(f32[9,56,256]{2,1,0:T(8,128)} %field_ref.1, ...), custom_call_target="tpu_custom_call" | custom-call | flops 1000000000 | bytes 30000000 | tf_op jit(solution)/shard_map/pallas_call | solution.py:88
  10.3 0.1 collective-permute-start
  10.4 3.3 %collective-permute-start.1 = (f32[256,128]{1,0:T(8,128)S(1)}, f32[256,128]{1,0:T(8,128)S(1)}, u32[]{:S(2)}, u32[]{:S(2)}) collective-permute-start(f32[256,128]{1,0:T(8,128)S(1)} %get-tuple-element.44), channel_id=1, source_target_pairs={{0,4},{1,5},{2,6},{3,7},{4,0},{5,1},{6,2},{7,3},{8,12},{9,13},{10,... | collective-permute-start | bytes 393224 | tf_op jit(solution)/shard_map/ppermute | solution.py:763
  13.7 2.4 %collective-permute-start.2 = (f32[224,128]{1,0:T(8,128)S(1)}, f32[224,128]{1,0:T(8,128)S(1)}, u32[]{:S(2)}, u32[]{:S(2)}) collective-permute-start(f32[224,128]{1,0:T(8,128)S(1)} %get-tuple-element.45), channel_id=1, source_target_pairs={{0,4},{1,2},{2,1},{3,7},{4,0},{5,6},{6,5},{7,3},{8,12},{9,10},{10,... | collective-permute-start | bytes 344072 | tf_op jit(solution)/shard_map/ppermute | solution.py:763
  16.1 0.0 collective-permute-start.3
  16.1 3.7 %shard_map.222 = (f32[224,1024]{1,0:T(8,128)S(1)}, f32[9,56,256]{2,1,0:T(8,128)S(1)}, f32[8,512]{1,0:T(8,128)S(1)}, bf16[112,192]{1,0:T(8,128)(2,1)S(1)}, f32[8,...) custom-call(f32[9,56,256]{2,1,0:T(8,128)S(1)} %get-tuple-element.47., ...), custom_call_target="tpu_custom_call" | custom-call | flops 400000000 | bytes 12000000 | tf_op jit(solution)/shard_map/pallas_call | solution.py:88
  19.9 11.6 %shard_map.223 = (f32[32,4,640]{2,1,0:T(4,128)}, f32[9,56,256]{2,1,0:T(8,128)}, f32[9,56,256]{2,1,0:T(8,128)}, f32[32,128]{1,0:T(8,128)}, f32[32,128]{1,0:T(8,12...) custom-call(f32[256,128]{1,0:T(8,128)S(1)} %collective-permute-done.refs_0_, ...), custom_call_target="tpu_custom_call" | custom-call | flops 1200000000 | bytes 36000000 | tf_op jit(solution)/shard_map/pallas_call | solution.py:88
  31.6 6.3 %all-to-all-start = ((f32[32,4,640]{2,1,0:T(4,128)}), f32[32,4,640]{2,1,0:T(4,128)S(1)}, u32[]{:S(2)}, u32[]{:S(2)}) async-start(f32[32,4,640]{2,1,0:T(4,128)} %get-tuple-element.70), calls=%async_computation | async-start | bytes 655360 | tf_op jit(solution)/shard_map/all_to_all | solution.py:862
  37.9 0.5 collective-permute-start.4
  38.4 6.2 %shard_map.224 = (f32[5,272,256]{2,1,0:T(8,128)}, f32[272,128]{1,0:T(8,128)}, f32[272,128]{1,0:T(8,128)}, f32[224,1024]{1,0:T(8,128)}, f32[9,56,256]{2,1,0:T(8,128)}) custom-call(f32[3,256,256]{2,1,0:T(8,128)} %refs_0_.3, f32[256,256]{1,0:T(8,128)} %refs_1_.2, s32[256,256]{1,0:T(8,128)} %refs_2_.4, f32[32,128]{1,0:T(8,128)} %get-tuple-element.60.refs_3_, ...), custom_call_target="tpu_custom_call" | custom-call | flops 600000000 | bytes 18000000 | tf_op jit(solution)/shard_map/pallas_call | solution.py:88
  44.6 4.6 %all-to-all-done.refs_0_ = f32[32,4,640]{2,1,0:T(4,128)S(1)} async-done(((f32[32,4,640]{2,1,0:T(4,128)}), f32[32,4,640]{2,1,0:T(4,128)S(1)}, u32[]{:S(2)}, u32[]{:S(2)}) %all-to-all-start) | async-done | bytes 327712 | tf_op jit(solution)/shard_map/all_to_all | solution.py:862
  49.2 2.1 %shard_map.227 = (f32[2,256,256]{2,1,0:T(8,128)S(1)}, f32[80,256]{1,0:T(8,128)S(1)}, f32[80,256]{1,0:T(8,128)S(1)}, bf16[272,336]{1,0:T(8,128)(2,1)S(1)}, bf16[2...) custom-call(f32[32,4,640]{2,1,0:T(4,128)S(1)} %all-to-all-done.refs_0_, ...), custom_call_target="tpu_custom_call" | custom-call | flops 200000000 | bytes 6000000 | tf_op jit(solution)/shard_map/pallas_call | solution.py:88
  51.3 1.1 %collective-permute-start.8 = (f32[80,256]{1,0:T(8,128)S(1)}, f32[80,256]{1,0:T(8,128)S(1)}, u32[]{:S(2)}, u32[]{:S(2)}) collective-permute-start(f32[80,256]{1,0:T(8,128)S(1)} %get-tuple-element.74), channel_id=1, source_target_pairs={{0,1},{1,0},{2,3},{3,2},{4,8},{5,9},{6,10},{7,11},{8,4},{9,5},{10,... | collective-permute-start | bytes 245768 | tf_op jit(solution)/shard_map/ppermute | solution.py:763
  52.4 0.7 collective-permute-start.9
  53.1 0.8 %collective-permute-start.5 = (f32[224,128]{1,0:T(8,128)S(1)}, f32[224,128]{1,0:T(8,128)S(1)}, u32[]{:S(2)}, u32[]{:S(2)}) collective-permute-start(f32[224,128]{1,0:T(8,128)S(1)} %copy-done.21), channel_id=1, source_target_pairs={{0,4},{1,5},{2,6},{3,7},{4,0},{5,1},{6,2},{7,3},{8,12},{9,13},{10,... | collective-permute-start | bytes 344072 | tf_op jit(solution)/shard_map/ppermute | solution.py:763
  53.9 1.0 %collective-permute-start.6 = (f32[224,128]{1,0:T(8,128)S(1)}, f32[224,128]{1,0:T(8,128)S(1)}, u32[]{:S(2)}, u32[]{:S(2)}) collective-permute-start(f32[224,128]{1,0:T(8,128)S(1)} %copy-done.20), channel_id=1, source_target_pairs={{0,4},{1,2},{2,1},{3,7},{4,0},{5,6},{6,5},{7,3},{8,12},{9,10},{10,... | collective-permute-start | bytes 344072 | tf_op jit(solution)/shard_map/ppermute | solution.py:763
  54.9 2.1 %collective-permute-start.7 = (f32[224,128]{1,0:T(8,128)S(1)}, f32[224,128]{1,0:T(8,128)S(1)}, u32[]{:S(2)}, u32[]{:S(2)}) collective-permute-start(f32[224,128]{1,0:T(8,128)S(1)} %copy-done.19), channel_id=1, source_target_pairs={{0,1},{1,0},{2,3},{3,2},{4,5},{5,4},{6,7},{7,6},{8,9},{9,8},{10,11... | collective-permute-start | bytes 344072 | tf_op jit(solution)/shard_map/ppermute | solution.py:763
  57.0 0.7 shard_map.228
  57.7 0.0 copy-start.6
  57.7 0.0 copy-start.7
  57.7 1.5 %collective-permute-start.10 = (f32[272,128]{1,0:T(8,128)S(1)}, f32[272,128]{1,0:T(8,128)S(1)}, u32[]{:S(2)}, u32[]{:S(2)}) collective-permute-start(f32[272,128]{1,0:T(8,128)S(1)} %get-tuple-element.82), channel_id=1, source_target_pairs={{0,4},{1,2},{2,1},{3,7},{4,0},{5,6},{6,5},{7,3},{8,12},{9,10},{10,... | collective-permute-start | bytes 417800 | tf_op jit(solution)/shard_map/ppermute | solution.py:763
  59.2 2.2 %collective-permute-start.11 = (f32[272,128]{1,0:T(8,128)S(1)}, f32[272,128]{1,0:T(8,128)S(1)}, u32[]{:S(2)}, u32[]{:S(2)}) collective-permute-start(f32[272,128]{1,0:T(8,128)S(1)} %get-tuple-element.83), channel_id=1, source_target_pairs={{0,1},{1,0},{2,3},{3,2},{4,5},{5,4},{6,7},{7,6},{8,9},{9,8},{10,11... | collective-permute-start | bytes 417800 | tf_op jit(solution)/shard_map/ppermute | solution.py:763
  61.5 0.6 copy-done.16
  62.1 0.0 copy-done.17
  62.1 0.0 copy-done.18
  62.1 2.5 %shard_map.225.part_ref = f32[224,1024]{1,0:T(8,128)S(1)} custom-call(f32[224,128]{1,0:T(8,128)} %copy-done.15, f32[224,128]{1,0:T(8,128)} %copy-done.16, f32[224,128]{1,0:T(8,128)} %copy-done.17, f32[224,128]{1,0:T(8,128)} %copy-done.18, f32[8,512]{1,0:T(8,128)} %get-tuple-element.59.refs_4_, s32[4,256]{1,0:T(4,128)} %refs_5_.6, ...), custom_call_target="tpu_custom_call" | custom-call | flops 200000000 | bytes 6000000 | tf_op jit(solution)/shard_map/pallas_call | solution.py:88
  64.7 2.9 %shard_map.226 = f32[9,56,256]{2,1,0:T(8,128)} custom-call(f32[224,1024]{1,0:T(8,128)S(1)} %shard_map.225.part_ref, f32[9,9,4,256]{3,2,1,0:T(4,128)} %bitcast.11, bf16[112,192]{1,0:T(8,128)(2,1)} %get-tuple-element.68.wl_hbm, f32[9,56,256]{2,1,0:T(8,128)} %get-tuple-element.69.base_hbm), custom_call_target="tpu_custom_call" | custom-call | flops 200000000 | bytes 6000000 | tf_op jit(solution)/shard_map/pallas_call | solution.py:88
  67.6 4.0 %shard_map.229 = f32[3,256,256]{2,1,0:T(8,128)} custom-call(f32[2,272,256]{2,1,0:T(8,128)S(1)} %get-tuple-element.80.refs_0_, f32[5,272,256]{2,1,0:T(8,128)S(1)} %copy-done.2, f32[272,128]{1,0:T(8,128)S(1)} %collective-permute-done.10.refs_2_, f32[272,128]{1,0:T(8,128)S(1)} %collective-permute-done.11.refs_3_, bf16[512,384]{1,0:T(8,128)(2,1)S(1)} %copy-done.7, ...), custom_call_target="tpu_custom_call" | custom-call | flops 400000000 | bytes 12000000 | tf_op jit(solution)/shard_map/pallas_call | solution.py:88
  (47 shorter events, 0.1 us)
Async XLA Ops:
  0.6 19.2 %copy-start.4 = (bf16[448,224]{1,0:T(8,128)(2,1)S(1)}, bf16[448,224]{1,0:T(8,128)(2,1)}, u32[]{:S(2)}) copy-start(bf16[448,224]{1,0:T(8,128)(2,1)} %constant.13.clone.refs_8_.refs_7_) | copy-start | bytes 602116
  0.6 19.2 %copy-start.11 = (s32[1,1,4,128]{3,2,1,0:T(4,128)S(1)}, s32[1,1,4,128]{3,2,1,0:T(4,128)}, u32[]{:S(2)}) copy-start(s32[1,1,4,128]{3,2,1,0:T(4,128)} %refs_14_.1) | copy-start | bytes 6148
  0.7 15.4 %copy-start.5 = (f32[9,56,256]{2,1,0:T(8,128)S(1)}, f32[9,56,256]{2,1,0:T(8,128)}, u32[]{:S(2)}) copy-start(f32[9,56,256]{2,1,0:T(8,128)} %field_ref.1) | copy-start | bytes 1548292
  0.7 15.4 %copy-start = (f32[3,9,9,256]{3,0,2,1:T(4,128)S(1)}, f32[3,9,9,256]{3,0,2,1:T(4,128)}, u32[]{:S(2)}) copy-start(f32[3,9,9,256]{3,0,2,1:T(4,128)} %param.23) | copy-start | bytes 746500
  0.7 15.4 %copy-start.8 = (s32[4,256]{1,0:T(4,128)S(1)}, s32[4,256]{1,0:T(4,128)}, u32[]{:S(2)}) copy-start(s32[4,256]{1,0:T(4,128)} %refs_5_.6) | copy-start | bytes 12292
  0.7 15.4 %copy-start.10 = (s32[4,256]{1,0:T(4,128)S(1)}, s32[4,256]{1,0:T(4,128)}, u32[]{:S(2)}) copy-start(s32[4,256]{1,0:T(4,128)} %orient_ref.1) | copy-start | bytes 12292
  0.7 15.4 %copy-start.9 = (f32[4,21,56]{2,0,1:T(4,128)S(1)}, f32[4,21,56]{2,0,1:T(4,128)}, u32[]{:S(2)}) copy-start(f32[4,21,56]{2,0,1:T(4,128)} %param.26) | copy-start | bytes 56452
  0.7 19.2 %copy-start.1 = (f32[21,128,256]{2,1,0:T(8,128)S(1)}, f32[21,128,256]{2,1,0:T(8,128)}, u32[]{:S(2)}) copy-start(f32[21,128,256]{2,1,0:T(8,128)} %refs_19_.1) | copy-start | bytes 8257540
  0.7 19.2 %copy-start.14 = (s32[128]{0:T(128)S(1)}, s32[128]{0:T(128)}, u32[]{:S(2)}) copy-start(s32[128]{0:T(128)} %param.33) | copy-start | bytes 1540
  0.7 19.2 %copy-start.13 = (s32[128,1]{0,1:T(1,128)S(1)}, s32[128,1]{0,1:T(1,128)}, u32[]{:S(2)}) copy-start(s32[128,1]{0,1:T(1,128)} %param.32) | copy-start | bytes 1540
  0.7 19.2 %copy-start.12 = (s32[128]{0:T(128)S(1)}, s32[128]{0:T(128)}, u32[]{:S(2)}) copy-start(s32[128]{0:T(128)} %param.31) | copy-start | bytes 1540
  0.8 19.2 %copy-start.3 = (f32[4,9,9,256]{3,0,2,1:T(4,128)S(1)}, f32[4,9,9,256]{3,0,2,1:T(4,128)}, u32[]{:S(2)}) copy-start(f32[4,9,9,256]{3,0,2,1:T(4,128)} %param.27) | copy-start | bytes 995332
  10.3 9.5 %collective-permute-start = (f32[256,128]{1,0:T(8,128)S(1)}, f32[256,128]{1,0:T(8,128)S(1)}, u32[]{:S(2)}, u32[]{:S(2)}) collective-permute-start(f32[256,128]{1,0:T(8,128)S(1)} %get-tuple-element.43), channel_id=1, source_target_pairs={{0,1},{1,0},{2,3},{3,2},{4,8},{5,9},{6,10},{7,11},{8,4},{9,5},{10,... | collective-permute-start | bytes 393224 | tf_op jit(solution)/shard_map/ppermute | solution.py:763
  10.4 9.4 %collective-permute-start.1 = (f32[256,128]{1,0:T(8,128)S(1)}, f32[256,128]{1,0:T(8,128)S(1)}, u32[]{:S(2)}, u32[]{:S(2)}) collective-permute-start(f32[256,128]{1,0:T(8,128)S(1)} %get-tuple-element.44), channel_id=1, source_target_pairs={{0,4},{1,5},{2,6},{3,7},{4,0},{5,1},{6,2},{7,3},{8,12},{9,13},{10,... | collective-permute-start | bytes 393224 | tf_op jit(solution)/shard_map/ppermute | solution.py:763
  13.7 6.1 %collective-permute-start.2 = (f32[224,128]{1,0:T(8,128)S(1)}, f32[224,128]{1,0:T(8,128)S(1)}, u32[]{:S(2)}, u32[]{:S(2)}) collective-permute-start(f32[224,128]{1,0:T(8,128)S(1)} %get-tuple-element.45), channel_id=1, source_target_pairs={{0,4},{1,2},{2,1},{3,7},{4,0},{5,6},{6,5},{7,3},{8,12},{9,10},{10,... | collective-permute-start | bytes 344072 | tf_op jit(solution)/shard_map/ppermute | solution.py:763
  16.1 3.8 %collective-permute-start.3 = (f32[224,128]{1,0:T(8,128)S(1)}, f32[224,128]{1,0:T(8,128)S(1)}, u32[]{:S(2)}, u32[]{:S(2)}) collective-permute-start(f32[224,128]{1,0:T(8,128)S(1)} %get-tuple-element.46), channel_id=1, source_target_pairs={{0,1},{1,0},{2,3},{3,2},{4,5},{5,4},{6,7},{7,6},{8,9},{9,8},{10,11... | collective-permute-start | bytes 344072 | tf_op jit(solution)/shard_map/ppermute | solution.py:763
  31.6 21.5 %copy-start.21 = (f32[224,128]{1,0:T(8,128)S(1)}, f32[224,128]{1,0:T(8,128)}, u32[]{:S(2)}) copy-start(f32[224,128]{1,0:T(8,128)} %get-tuple-element.56) | copy-start | bytes 344068
  31.6 22.3 %copy-start.20 = (f32[224,128]{1,0:T(8,128)S(1)}, f32[224,128]{1,0:T(8,128)}, u32[]{:S(2)}) copy-start(f32[224,128]{1,0:T(8,128)} %get-tuple-element.57) | copy-start | bytes 344068
  31.6 23.3 %copy-start.19 = (f32[224,128]{1,0:T(8,128)S(1)}, f32[224,128]{1,0:T(8,128)}, u32[]{:S(2)}) copy-start(f32[224,128]{1,0:T(8,128)} %get-tuple-element.58) | copy-start | bytes 344068
  31.6 17.6 %all-to-all-start = ((f32[32,4,640]{2,1,0:T(4,128)}), f32[32,4,640]{2,1,0:T(4,128)S(1)}, u32[]{:S(2)}, u32[]{:S(2)}) async-start(f32[32,4,640]{2,1,0:T(4,128)} %get-tuple-element.70), calls=%async_computation | async-start | bytes 655360 | tf_op jit(solution)/shard_map/all_to_all | solution.py:862
  37.9 21.3 %collective-permute-start.4 = (f32[224,128]{1,0:T(8,128)}, f32[224,128]{1,0:T(8,128)S(1)}, u32[]{:S(2)}, u32[]{:S(2)}) collective-permute-start(f32[224,128]{1,0:T(8,128)} %get-tuple-element.55), channel_id=1, source_target_pairs={{0,1},{1,0},{2,3},{3,2},{4,8},{5,9},{6,10},{7,11},{8,4},{9,5},{10,... | collective-permute-start | bytes 344072 | tf_op jit(solution)/shard_map/ppermute | solution.py:763
  51.3 3.6 %collective-permute-start.8 = (f32[80,256]{1,0:T(8,128)S(1)}, f32[80,256]{1,0:T(8,128)S(1)}, u32[]{:S(2)}, u32[]{:S(2)}) collective-permute-start(f32[80,256]{1,0:T(8,128)S(1)} %get-tuple-element.74), channel_id=1, source_target_pairs={{0,1},{1,0},{2,3},{3,2},{4,8},{5,9},{6,10},{7,11},{8,4},{9,5},{10,... | collective-permute-start | bytes 245768 | tf_op jit(solution)/shard_map/ppermute | solution.py:763
  52.4 4.6 %collective-permute-start.9 = (f32[80,256]{1,0:T(8,128)S(1)}, f32[80,256]{1,0:T(8,128)S(1)}, u32[]{:S(2)}, u32[]{:S(2)}) collective-permute-start(f32[80,256]{1,0:T(8,128)S(1)} %get-tuple-element.75), channel_id=1, source_target_pairs={{0,4},{1,5},{2,6},{3,7},{4,0},{5,1},{6,2},{7,3},{8,12},{9,13},{10,... | collective-permute-start | bytes 245768 | tf_op jit(solution)/shard_map/ppermute | solution.py:763
  53.1 8.3 %collective-permute-start.5 = (f32[224,128]{1,0:T(8,128)S(1)}, f32[224,128]{1,0:T(8,128)S(1)}, u32[]{:S(2)}, u32[]{:S(2)}) collective-permute-start(f32[224,128]{1,0:T(8,128)S(1)} %copy-done.21), channel_id=1, source_target_pairs={{0,4},{1,5},{2,6},{3,7},{4,0},{5,1},{6,2},{7,3},{8,12},{9,13},{10,... | collective-permute-start | bytes 344072 | tf_op jit(solution)/shard_map/ppermute | solution.py:763
  53.9 7.5 %collective-permute-start.6 = (f32[224,128]{1,0:T(8,128)S(1)}, f32[224,128]{1,0:T(8,128)S(1)}, u32[]{:S(2)}, u32[]{:S(2)}) collective-permute-start(f32[224,128]{1,0:T(8,128)S(1)} %copy-done.20), channel_id=1, source_target_pairs={{0,4},{1,2},{2,1},{3,7},{4,0},{5,6},{6,5},{7,3},{8,12},{9,10},{10,... | collective-permute-start | bytes 344072 | tf_op jit(solution)/shard_map/ppermute | solution.py:763
  54.9 6.5 %collective-permute-start.7 = (f32[224,128]{1,0:T(8,128)S(1)}, f32[224,128]{1,0:T(8,128)S(1)}, u32[]{:S(2)}, u32[]{:S(2)}) collective-permute-start(f32[224,128]{1,0:T(8,128)S(1)} %copy-done.19), channel_id=1, source_target_pairs={{0,1},{1,0},{2,3},{3,2},{4,5},{5,4},{6,7},{7,6},{8,9},{9,8},{10,11... | collective-permute-start | bytes 344072 | tf_op jit(solution)/shard_map/ppermute | solution.py:763
  57.7 9.9 %copy-start.2 = (f32[5,272,256]{2,1,0:T(8,128)S(1)}, f32[5,272,256]{2,1,0:T(8,128)}, u32[]{:S(2)}) copy-start(f32[5,272,256]{2,1,0:T(8,128)} %get-tuple-element.81.refs_1_) | copy-start | bytes 4177924
  57.7 9.9 %copy-start.6 = (bf16[512,384]{1,0:T(8,128)(2,1)S(1)}, bf16[512,384]{1,0:T(8,128)(2,1)}, u32[]{:S(2)}) copy-start(bf16[512,384]{1,0:T(8,128)(2,1)} %constant.17.clone.refs_5_) | copy-start | bytes 1179652
  57.7 9.9 %copy-start.7 = (bf16[512,384]{1,0:T(8,128)(2,1)S(1)}, bf16[512,384]{1,0:T(8,128)(2,1)}, u32[]{:S(2)}) copy-start(bf16[512,384]{1,0:T(8,128)(2,1)} %constant.16.clone.refs_4_) | copy-start | bytes 1179652
  57.7 9.8 %collective-permute-start.10 = (f32[272,128]{1,0:T(8,128)S(1)}, f32[272,128]{1,0:T(8,128)S(1)}, u32[]{:S(2)}, u32[]{:S(2)}) collective-permute-start(f32[272,128]{1,0:T(8,128)S(1)} %get-tuple-element.82), channel_id=1, source_target_pairs={{0,4},{1,2},{2,1},{3,7},{4,0},{5,6},{6,5},{7,3},{8,12},{9,10},{10,... | collective-permute-start | bytes 417800 | tf_op jit(solution)/shard_map/ppermute | solution.py:763
  59.2 2.2 %copy-start.15 = (f32[224,128]{1,0:T(8,128)}, f32[224,128]{1,0:T(8,128)S(1)}, u32[]{:S(2)}) copy-start(f32[224,128]{1,0:T(8,128)S(1)} %collective-permute-done.4.refs_0_) | copy-start | bytes 344068
  59.2 8.3 %collective-permute-start.11 = (f32[272,128]{1,0:T(8,128)S(1)}, f32[272,128]{1,0:T(8,128)S(1)}, u32[]{:S(2)}, u32[]{:S(2)}) collective-permute-start(f32[272,128]{1,0:T(8,128)S(1)} %get-tuple-element.83), channel_id=1, source_target_pairs={{0,1},{1,0},{2,3},{3,2},{4,5},{5,4},{6,7},{7,6},{8,9},{9,8},{10,11... | collective-permute-start | bytes 417800 | tf_op jit(solution)/shard_map/ppermute | solution.py:763
  (3 other events, 2.0 us)

commit v3 on v2

--- a/solution.py
+++ b/solution.py
@@ -224,22 +224,29 @@
     lax.fori_loop(1, ORDER, body, 0)
 
 
-def traces(integ_ref, wt_ref, own_refs):
+def traces(integ_ref, wt_ref, own_ref, turn=None, turned_ref=None):
     variables, _, elems = integ_ref.shape
     np_ = wt_ref.shape[0] // 12
-    count = len(own_refs)
+    count = 1 if turn is None else 3
     for v in range(variables):
         t = mm(wt_ref[0 : count * 4 * np_, :], stacked(integ_ref[v]))
-        for r in range(count):
-            for f in range(4):
-                own_refs[r][v * np_ : (v + 1) * np_, f * elems : (f + 1) * elems] = t[
-                    (r * 4 + f) * np_ : (r * 4 + f + 1) * np_
-                ]
-    rows = own_refs[0].shape[0]
-    for r in range(count):
-        if rows > variables * np_:
-            own_refs[r][variables * np_ :, :] = jnp.zeros(
-                (rows - variables * np_, 4 * elems), F32
+        rows = slice(v * np_, (v + 1) * np_)
+        for f in range(4):
+            at = slice(f * elems, (f + 1) * elems)
+            plain, *others = [
+                t[(r * 4 + f) * np_ : (r * 4 + f + 1) * np_] for r in range(count)
+            ]
+            own_ref[rows, at] = plain
+            if others:
+                turned_ref[rows, at] = jnp.where(
+                    turn[:, at] == 1.0,
+                    others[0],
+                    jnp.where(turn[:, at] == 2.0, others[1], plain),
+                )
+    for ref in (own_ref, turned_ref):
+        if ref is not None and ref.shape[0] > variables * np_:
+            ref[variables * np_ :, :] = jnp.zeros(
+                (ref.shape[0] - variables * np_, 4 * elems), F32
             )
 
 
@@ -279,21 +286,16 @@
     return jnp.concatenate([ref[f : f + 1, :] for f in range(ref.shape[0])], axis=1)
 
 
-def local_jump(own_refs, source_turn, codes, left_ref, jump_ref):
-    rows, faces = own_refs[0].shape
+def local_jump(own_ref, turned_ref, codes, left_ref, jump_ref):
+    rows, faces = own_ref.shape
     width = faces // 4
-    value = jnp.where(
-        source_turn == 1.0,
-        own_refs[1][...],
-        jnp.where(source_turn == 2.0, own_refs[2][...], own_refs[0][...]),
-    )
-    hi, lo = split(value)
+    hi, lo = split(turned_ref[...])
     left_ref[0:rows] = hi
     left_ref[rows : 2 * rows] = lo
     for q in range(4):
         at = slice(q * width, (q + 1) * width)
         res = mm(left_ref[...], hot(iota((faces, width), 0) == codes[:, at]))
-        jump_ref[:, at] = own_refs[0][:, at] - (res[:rows] + res[rows:])
+        jump_ref[:, at] = own_ref[:, at] - (res[:rows] + res[rows:])
 
 
 def full_jump(arrived, slot_turn, codes, jump_ref, perm_ref, left_ref, part_ref):
@@ -370,7 +372,7 @@
     predict(star_ref, w_ref, moved_ref, term_ref, integ_ref, total_ref)
     finish(later)
     prep_trace(trace_ref, place_ref, stage_ref, wt_ref)
-    traces(integ_ref, wt_ref, (own_ref,))
+    traces(integ_ref, wt_ref, own_ref)
     send_gather(axes, own_ref, send_ref, left_ref, (o0, o1, o2, o3))
     rows = own_ref.shape[0]
     np_ = lifted_ref.shape[0]
@@ -400,7 +402,7 @@
 def local_first_kernel(
     integ_ref, field_ref, star_ref, w_ref, wt_ref, codes_ref, orient_ref, lift_ref,
     jump_ref, base_ref, slot_ref, wl_ref, turn_out, slot_out, wl_out, w_out, wt_out,
-    turn_ref, own0, own1, own2, left_ref, moved_ref, total_ref, stage_ref, sem_ref,
+    turn_ref, own_ref, turned_ref, left_ref, moved_ref, total_ref, stage_ref, sem_ref,
 ):
     prep_lift(lift_ref, stage_ref, wl_ref)
     codes = row_of(codes_ref)
@@ -419,9 +421,8 @@
         [(turn_ref, turn_out), (slot_ref, slot_out), (wl_ref, wl_out), (w_ref, w_out),
          (wt_ref, wt_out)], sem_ref,
     )
-    own_refs = (own0, own1, own2)
-    traces(integ_ref, wt_ref, own_refs)
-    local_jump(own_refs, turn_ref[0:1, :], codes, left_ref, jump_ref)
+    traces(integ_ref, wt_ref, own_ref, turn_ref[0:1, :], turned_ref)
+    local_jump(own_ref, turned_ref, codes, left_ref, jump_ref)
     own_derivative(integ_ref, field_ref, star_ref, w_ref, base_ref, moved_ref, total_ref)
     finish(copies)
 
@@ -447,7 +448,7 @@
     term_ref[...] = field_ref[...]
     predict(star_ref, w_ref, moved_ref, term_ref, integ_ref, total_ref)
     copies += start([(integ_ref, integ_out)], sem_ref, 3)
-    traces(integ_ref, wt_ref, (own_ref,))
+    traces(integ_ref, wt_ref, own_ref)
     send_gather(axes, own_ref, send_ref, left_ref, (o0, o1, o2, o3))
     copies += start([(o0, s0), (o1, s1), (o2, s2), (o3, s3)], sem_ref, 4)
     np_ = lifted_ref.shape[0]
@@ -465,7 +466,7 @@
     ext_out, right_out, left_out, jump_out, base_out,
     ext_ref, wet_ref, low_ref, high_ref, right_ref, left_ref,
     integ_ref, field_ref, star_ref, w_ref, wt_ref, turn_ref, codes_ref, jump_ref, base_ref,
-    own0, own1, own2, left_rows, moved_ref, total_ref, sem_ref,
+    own_ref, turned_ref, left_rows, moved_ref, total_ref, sem_ref,
 ):
     copies = start(
         [(wt_hbm, wt_ref), (integ_hbm, integ_ref), (turn_hbm, turn_ref), (codes_hbm, codes_ref),
@@ -477,11 +478,10 @@
         + [(depth_hbm, ext_ref.at[3, body]), (wet_hbm, wet_ref), (low_hbm, low_ref),
            (high_hbm, high_ref)], sem_ref, 7,
     )
-    finish(copies[:2])
-    own_refs = (own0, own1, own2)
-    traces(integ_ref, wt_ref, own_refs)
-    finish(copies[2:4])
-    local_jump(own_refs, turn_ref[0:1, :], row_of(codes_ref), left_rows, jump_ref)
+    finish(copies[:3])
+    traces(integ_ref, wt_ref, own_ref, turn_ref[0:1, :], turned_ref)
+    finish(copies[3:4])
+    local_jump(own_ref, turned_ref, row_of(codes_ref), left_rows, jump_ref)
     written = start([(jump_ref, jump_out)], sem_ref, 14)
     finish(copies[4:])
     own_derivative(integ_ref, field_ref, star_ref, w_ref, base_ref, moved_ref, total_ref)
@@ -497,17 +497,16 @@
 def last_jump_kernel(
     axes,
     a0, a1, a2, a3, slot_hbm, codes_hbm, jump_hbm, perm_hbm,
-    part_ref,
-    b0, b1, b2, b3, slot_ref, codes_ref, jump_ref, perm_ref, arr_left_ref, sem_ref,
+    part_ref, slot_ref, codes_ref, jump_ref, perm_ref, arr_left_ref, sem_ref,
 ):
     finish(
         start(
-            [(a0, b0), (a1, b1), (a2, b2), (a3, b3), (slot_hbm, slot_ref), (perm_hbm, perm_ref),
-             (codes_hbm, codes_ref), (jump_hbm, jump_ref)], sem_ref,
+            [(slot_hbm, slot_ref), (perm_hbm, perm_ref), (codes_hbm, codes_ref),
+             (jump_hbm, jump_ref)], sem_ref,
         )
     )
     full_jump(
-        by_direction(axes, [b0[...], b1[...], b2[...], b3[...]]), slot_ref[0:1, :], row_of(codes_ref), jump_ref,
+        by_direction(axes, [a0[...], a1[...], a2[...], a3[...]]), slot_ref[0:1, :], row_of(codes_ref), jump_ref,
         perm_ref, arr_left_ref, part_ref,
     )
 
@@ -544,7 +543,7 @@
     devs = pay_ref.shape[0]
     total = devs * capacity
     put = hot(iota((total, sea_rows), 0) == place)
-    chunk = 32
+    chunk = 64
 
     def body(c, carry):
         here = pl.ds(pl.multiple_of(c * chunk, chunk), chunk)
@@ -695,13 +694,20 @@
     low = jnp.where(at_y > 0, low, 0.0)
     high = jnp.where(at_y < lax.axis_size(axes[1]) - 1, high, 0.0)
     lane = iota((tall, LANES), 1)
+    his, los = [], []
+    for t in range(STEPS):
+        right = pltpu.roll(high, LANES - t * HALO_Y, 1) if t else high
+        left = pltpu.roll(low, t * HALO_Y, 1) if t else low
+        edge = jnp.where(lane < LANES // 2, right, left)
+        hi, lo = split(jnp.concatenate([along_ref[t], edge], axis=1))
+        his.append(hi)
+        los.append(lo)
+    coarse = mm(jnp.concatenate(his + los, axis=0), b_hi[...])
+    fine = mm(jnp.concatenate(his, axis=0), b_lo[...])
     forces = []
     for t in range(STEPS):
-        right = pltpu.roll(high, LANES - HALO_Y, 1) if t else high
-        left = pltpu.roll(low, HALO_Y, 1) if t else low
-        value = jnp.concatenate([along_ref[t], right, left], axis=1)
-        hi, lo = split(value)
-        forces.append(mm(hi, b_hi[...]) + mm(lo, b_hi[...]) + mm(hi, b_lo[...]))
+        at, more = slice(t * tall, (t + 1) * tall), slice((t + STEPS) * tall, (t + STEPS + 1) * tall)
+        forces.append(coarse[at] + coarse[more] + fine[at])
     fields = []
     for j in range(5):
         moved = 2 * HALO_Y + 2 * j
@@ -840,7 +846,7 @@
         local_first_kernel,
         [wide_of, field_of, slot_of, wl_of, hbm(turn_of), hbm(slot_of), hbm(wl_of), hbm(w_of),
          hbm(wt_of)],
-        [turn_of, wide_of, wide_of, wide_of, left, moved, field_of, stage, sems(5)],
+        [turn_of, wide_of, wide_of, left, moved, field_of, stage, sems(5)],
         integ, state, star, w, wt, neighbours, orient, lift,
         micros=4,
     )
@@ -871,16 +877,16 @@
         [hbm(ext_of), hbm(strip_of), hbm(strip_of), hbm(wide_of), hbm(field_of)],
         [ext_of, (wet.shape, wet.dtype), edge_of, edge_of, strip_of, strip_of,
          field_of, field_of, star_of, w_of, wt_of, turn_of, codes_of, wide_of, field_of,
-         wide_of, wide_of, wide_of, left, moved, field_of, sems(19)],
+         wide_of, wide_of, left, moved, field_of, sems(19)],
         sea_state, depth, wet, edge_odd, edge_even,
         integ_h, field_h, star, w_h, wt_h, turn_h, neighbours,
         micros=6, held=range(12),
     )
     part, = call(
         lambda *refs: last_jump_kernel(axes, *refs), [wide_of],
-        [out_of] * 4 + [slot_of, codes_of, wide_of, perm_of, arr_left, sems(8)],
+        [slot_of, codes_of, wide_of, perm_of, arr_left, sems(4)],
         *arrived, slot_h, neighbours, jump_h, perm,
-        micros=2, held=range(8),
+        micros=2, held=range(4, 8),
     )
     elastic, = call(
         last_kernel, [hbm(field_of)],
@@ -892,7 +898,7 @@
     cell_x = np.concatenate([np.arange(tile_x + EDGE), np.arange(-EDGE, 0)])
     read_x = np.concatenate([np.arange(tile_x + HALO_X), np.arange(-HALO_X, 0)])
     cell_y = np.concatenate([np.arange(tile_y + LANES // 2), np.arange(-LANES // 2, 0)])
-    read_y = np.concatenate([np.arange(tile_y + LANES), np.arange(-LANES, 0)])
+    read_y = cell_y
     bx = [jnp.asarray(b) for b in band(cell_x, read_x)]
     by = [jnp.asarray(b.T) for b in band(cell_y, read_y)]
     uplift, odd, even, bx_hi, bx_lo, sea_right, sea_left = call(

time: 72 us -> 70.9 us (0.985)
  no operation moved by 1% of the time
where the time goes in v3:
time: 70.9 us; the launch traced here: 70.6 us
  Pallas kernels  42.8 us (60%)
  starting transfers between devices  21.9 us (31%)
  waiting for transfers between devices  4.71 us (7%)
  between operations  1.18 us (2%)
    pallas_call x9, Pallas kernels, call(): pl.pallas_call(body, in_specs=[spec(i in held) for i in range(len(args))]...  42.8 us
    ppermute x12, starting transfers between devices, swap(): return lax.ppermute(value, axes, pairs)  15.6 us
    all_to_all x1, starting transfers between devices, on_device(): lax.all_to_all(payload, ('gx', 'gy'), split_axis=0, concat_axis=0, tiled=...  6.29 us
    all_to_all x1, waiting for transfers between devices, on_device(): lax.all_to_all(payload, ('gx', 'gy'), split_axis=0, concat_axis=0, tiled=...  4.68 us
  transfers between devices with their start and end apart: 13, of which 1 were waited for; matrix products, arithmetic and copies ran while one was open for 0% of the time, Pallas kernels for 25%

profile of v3, /device:TPU:1, one launch (start us, length us, event | category | flops | bytes accessed | tf_op | source)
XLA Modules:
  0.0 70.6 jit_solution(1710451807862140220)
XLA Ops:
  0.6 0.0 copy-start.4
  0.7 0.0 copy-start
  0.7 0.0 copy-start.8
  0.8 0.0 copy-start.3
  0.8 9.5 %shard_map.221 = (bf16[168,192]{1,0:T(8,128)(2,1)S(1)}, bf16[288,192]{1,0:T(8,128)(2,1)S(1)}, f32[9,56,256]{2,1,0:T(8,128)S(1)}, f32[24,1024]{1,0:T(8,128)S(1)},...) custom-call(f32[9,56,256]{2,1,0:T(8,128)} %field_ref.1, ...), custom_call_target="tpu_custom_call" | custom-call | flops 1000000000 | bytes 30000000 | tf_op jit(solution)/shard_map/pallas_call | solution.py:88
  10.3 0.1 collective-permute-start
  10.4 3.3 %collective-permute-start.1 = (f32[256,128]{1,0:T(8,128)S(1)}, f32[256,128]{1,0:T(8,128)S(1)}, u32[]{:S(2)}, u32[]{:S(2)}) collective-permute-start(f32[256,128]{1,0:T(8,128)S(1)} %get-tuple-element.44), channel_id=1, source_target_pairs={{0,4},{1,5},{2,6},{3,7},{4,0},{5,1},{6,2},{7,3},{8,12},{9,13},{10,... | collective-permute-start | bytes 393224 | tf_op jit(solution)/shard_map/ppermute | solution.py:769
  13.7 2.4 %collective-permute-start.2 = (f32[224,128]{1,0:T(8,128)S(1)}, f32[224,128]{1,0:T(8,128)S(1)}, u32[]{:S(2)}, u32[]{:S(2)}) collective-permute-start(f32[224,128]{1,0:T(8,128)S(1)} %get-tuple-element.45), channel_id=1, source_target_pairs={{0,4},{1,2},{2,1},{3,7},{4,0},{5,6},{6,5},{7,3},{8,12},{9,10},{10,... | collective-permute-start | bytes 344072 | tf_op jit(solution)/shard_map/ppermute | solution.py:769
  16.1 0.0 collective-permute-start.3
  16.1 3.7 %shard_map.222 = (f32[224,1024]{1,0:T(8,128)S(1)}, f32[9,56,256]{2,1,0:T(8,128)S(1)}, f32[8,512]{1,0:T(8,128)S(1)}, bf16[112,192]{1,0:T(8,128)(2,1)S(1)}, f32[8,...) custom-call(f32[9,56,256]{2,1,0:T(8,128)S(1)} %get-tuple-element.47., ...), custom_call_target="tpu_custom_call" | custom-call | flops 400000000 | bytes 12000000 | tf_op jit(solution)/shard_map/pallas_call | solution.py:88
  19.8 0.0 collective-permute-done.2.refs_2_
  19.8 0.0 collective-permute-done.3.refs_3_
  19.9 11.4 %shard_map.223 = (f32[32,4,640]{2,1,0:T(4,128)}, f32[9,56,256]{2,1,0:T(8,128)}, f32[9,56,256]{2,1,0:T(8,128)}, f32[32,128]{1,0:T(8,128)}, f32[32,128]{1,0:T(8,12...) custom-call(f32[256,128]{1,0:T(8,128)S(1)} %collective-permute-done.refs_0_, ...), custom_call_target="tpu_custom_call" | custom-call | flops 1200000000 | bytes 36000000 | tf_op jit(solution)/shard_map/pallas_call | solution.py:88
  31.3 6.3 %all-to-all-start = ((f32[32,4,640]{2,1,0:T(4,128)}), f32[32,4,640]{2,1,0:T(4,128)S(1)}, u32[]{:S(2)}, u32[]{:S(2)}) async-start(f32[32,4,640]{2,1,0:T(4,128)} %get-tuple-element.70), calls=%async_computation | async-start | bytes 655360 | tf_op jit(solution)/shard_map/all_to_all | solution.py:868
  37.6 0.5 collective-permute-start.4
  38.1 6.1 %shard_map.224 = (f32[5,272,256]{2,1,0:T(8,128)}, f32[272,128]{1,0:T(8,128)}, f32[272,128]{1,0:T(8,128)}, f32[224,1024]{1,0:T(8,128)}, f32[9,56,256]{2,1,0:T(8,128)}) custom-call(f32[3,256,256]{2,1,0:T(8,128)} %refs_0_.3, f32[256,256]{1,0:T(8,128)} %refs_1_.2, s32[256,256]{1,0:T(8,128)} %refs_2_.4, f32[32,128]{1,0:T(8,128)} %get-tuple-element.60.refs_3_, ...), custom_call_target="tpu_custom_call" | custom-call | flops 600000000 | bytes 18000000 | tf_op jit(solution)/shard_map/pallas_call | solution.py:88
  44.2 4.7 %all-to-all-done.refs_0_ = f32[32,4,640]{2,1,0:T(4,128)S(1)} async-done(((f32[32,4,640]{2,1,0:T(4,128)}), f32[32,4,640]{2,1,0:T(4,128)S(1)}, u32[]{:S(2)}, u32[]{:S(2)}) %all-to-all-start) | async-done | bytes 327712 | tf_op jit(solution)/shard_map/all_to_all | solution.py:868
  48.9 2.1 %shard_map.227 = (f32[2,256,256]{2,1,0:T(8,128)S(1)}, f32[80,256]{1,0:T(8,128)S(1)}, f32[80,256]{1,0:T(8,128)S(1)}, bf16[272,336]{1,0:T(8,128)(2,1)S(1)}, bf16[2...) custom-call(f32[32,4,640]{2,1,0:T(4,128)S(1)} %all-to-all-done.refs_0_, ...), custom_call_target="tpu_custom_call" | custom-call | flops 200000000 | bytes 6000000 | tf_op jit(solution)/shard_map/pallas_call | solution.py:88
  51.1 1.1 %collective-permute-start.8 = (f32[80,256]{1,0:T(8,128)S(1)}, f32[80,256]{1,0:T(8,128)S(1)}, u32[]{:S(2)}, u32[]{:S(2)}) collective-permute-start(f32[80,256]{1,0:T(8,128)S(1)} %get-tuple-element.74), channel_id=1, source_target_pairs={{0,1},{1,0},{2,3},{3,2},{4,8},{5,9},{6,10},{7,11},{8,4},{9,5},{10,... | collective-permute-start | bytes 245768 | tf_op jit(solution)/shard_map/ppermute | solution.py:769
  52.2 0.7 collective-permute-start.9
  52.8 0.8 %collective-permute-start.5 = (f32[224,128]{1,0:T(8,128)S(1)}, f32[224,128]{1,0:T(8,128)S(1)}, u32[]{:S(2)}, u32[]{:S(2)}) collective-permute-start(f32[224,128]{1,0:T(8,128)S(1)} %copy-done.17), channel_id=1, source_target_pairs={{0,4},{1,5},{2,6},{3,7},{4,0},{5,1},{6,2},{7,3},{8,12},{9,13},{10,... | collective-permute-start | bytes 344072 | tf_op jit(solution)/shard_map/ppermute | solution.py:769
  53.6 1.0 %collective-permute-start.6 = (f32[224,128]{1,0:T(8,128)S(1)}, f32[224,128]{1,0:T(8,128)S(1)}, u32[]{:S(2)}, u32[]{:S(2)}) collective-permute-start(f32[224,128]{1,0:T(8,128)S(1)} %copy-done.16), channel_id=1, source_target_pairs={{0,4},{1,2},{2,1},{3,7},{4,0},{5,6},{6,5},{7,3},{8,12},{9,10},{10,... | collective-permute-start | bytes 344072 | tf_op jit(solution)/shard_map/ppermute | solution.py:769
  54.6 2.1 %collective-permute-start.7 = (f32[224,128]{1,0:T(8,128)S(1)}, f32[224,128]{1,0:T(8,128)S(1)}, u32[]{:S(2)}, u32[]{:S(2)}) collective-permute-start(f32[224,128]{1,0:T(8,128)S(1)} %copy-done.15), channel_id=1, source_target_pairs={{0,1},{1,0},{2,3},{3,2},{4,5},{5,4},{6,7},{7,6},{8,9},{9,8},{10,11... | collective-permute-start | bytes 344072 | tf_op jit(solution)/shard_map/ppermute | solution.py:769
  56.7 0.0 collective-permute-done.9.refs_2_
  56.7 0.7 shard_map.228
  57.4 0.0 copy-start.6
  57.4 0.0 copy-start.7
  57.5 1.5 %collective-permute-start.10 = (f32[272,128]{1,0:T(8,128)S(1)}, f32[272,128]{1,0:T(8,128)S(1)}, u32[]{:S(2)}, u32[]{:S(2)}) collective-permute-start(f32[272,128]{1,0:T(8,128)S(1)} %get-tuple-element.82), channel_id=1, source_target_pairs={{0,4},{1,2},{2,1},{3,7},{4,0},{5,6},{6,5},{7,3},{8,12},{9,10},{10,... | collective-permute-start | bytes 417800 | tf_op jit(solution)/shard_map/ppermute | solution.py:769
  59.0 2.2 %collective-permute-start.11 = (f32[272,128]{1,0:T(8,128)S(1)}, f32[272,128]{1,0:T(8,128)S(1)}, u32[]{:S(2)}, u32[]{:S(2)}) collective-permute-start(f32[272,128]{1,0:T(8,128)S(1)} %get-tuple-element.83), channel_id=1, source_target_pairs={{0,1},{1,0},{2,3},{3,2},{4,5},{5,4},{6,7},{7,6},{8,9},{9,8},{10,11... | collective-permute-start | bytes 417800 | tf_op jit(solution)/shard_map/ppermute | solution.py:769
  61.2 2.3 %shard_map.225.part_ref = f32[224,1024]{1,0:T(8,128)S(1)} custom-call(f32[224,128]{1,0:T(8,128)S(1)} %collective-permute-done.4.refs_0_, f32[224,128]{1,0:T(8,128)S(1)} %collective-permute-done.5.refs_1_, f32[224,128]{1,0:T(8,128)S(1)} %collective-permute-done.6.refs_2_, f32[224,128]{1,0:T(8,128)S(1)} %collective-permute-done.7.refs_3_, ...), custom_call_target="tpu_custom_call" | custom-call | flops 200000000 | bytes 6000000 | tf_op jit(solution)/shard_map/pallas_call | solution.py:88
  63.5 2.9 %shard_map.226 = f32[9,56,256]{2,1,0:T(8,128)} custom-call(f32[224,1024]{1,0:T(8,128)S(1)} %shard_map.225.part_ref, f32[9,9,4,256]{3,2,1,0:T(4,128)} %bitcast.11, bf16[112,192]{1,0:T(8,128)(2,1)} %get-tuple-element.68.wl_hbm, f32[9,56,256]{2,1,0:T(8,128)} %get-tuple-element.69.base_hbm), custom_call_target="tpu_custom_call" | custom-call | flops 200000000 | bytes 6000000 | tf_op jit(solution)/shard_map/pallas_call | solution.py:88
  66.4 4.1 %shard_map.229 = f32[3,256,256]{2,1,0:T(8,128)} custom-call(f32[2,272,256]{2,1,0:T(8,128)S(1)} %get-tuple-element.80.refs_0_, f32[5,272,256]{2,1,0:T(8,128)S(1)} %copy-done.2, f32[272,128]{1,0:T(8,128)S(1)} %collective-permute-done.10.refs_2_, f32[272,128]{1,0:T(8,128)S(1)} %collective-permute-done.11.refs_3_, bf16[384,384]{1,0:T(8,128)(2,1)S(1)} %copy-done.7, ...), custom_call_target="tpu_custom_call" | custom-call | flops 400000000 | bytes 12000000 | tf_op jit(solution)/shard_map/pallas_call | solution.py:88
  (39 shorter events, 0.1 us)
Async XLA Ops:
  0.6 19.2 %copy-start.4 = (bf16[448,224]{1,0:T(8,128)(2,1)S(1)}, bf16[448,224]{1,0:T(8,128)(2,1)}, u32[]{:S(2)}) copy-start(bf16[448,224]{1,0:T(8,128)(2,1)} %constant.13.clone.refs_8_.refs_7_) | copy-start | bytes 602116
  0.6 19.2 %copy-start.11 = (s32[1,1,4,128]{3,2,1,0:T(4,128)S(1)}, s32[1,1,4,128]{3,2,1,0:T(4,128)}, u32[]{:S(2)}) copy-start(s32[1,1,4,128]{3,2,1,0:T(4,128)} %refs_14_.1) | copy-start | bytes 6148
  0.7 15.4 %copy-start.5 = (f32[9,56,256]{2,1,0:T(8,128)S(1)}, f32[9,56,256]{2,1,0:T(8,128)}, u32[]{:S(2)}) copy-start(f32[9,56,256]{2,1,0:T(8,128)} %field_ref.1) | copy-start | bytes 1548292
  0.7 15.4 %copy-start = (f32[3,9,9,256]{3,0,2,1:T(4,128)S(1)}, f32[3,9,9,256]{3,0,2,1:T(4,128)}, u32[]{:S(2)}) copy-start(f32[3,9,9,256]{3,0,2,1:T(4,128)} %param.23) | copy-start | bytes 746500
  0.7 15.4 %copy-start.8 = (s32[4,256]{1,0:T(4,128)S(1)}, s32[4,256]{1,0:T(4,128)}, u32[]{:S(2)}) copy-start(s32[4,256]{1,0:T(4,128)} %refs_5_.6) | copy-start | bytes 12292
  0.7 15.4 %copy-start.10 = (s32[4,256]{1,0:T(4,128)S(1)}, s32[4,256]{1,0:T(4,128)}, u32[]{:S(2)}) copy-start(s32[4,256]{1,0:T(4,128)} %orient_ref.1) | copy-start | bytes 12292
  0.7 15.4 %copy-start.9 = (f32[4,21,56]{2,0,1:T(4,128)S(1)}, f32[4,21,56]{2,0,1:T(4,128)}, u32[]{:S(2)}) copy-start(f32[4,21,56]{2,0,1:T(4,128)} %param.26) | copy-start | bytes 56452
  0.7 19.2 %copy-start.1 = (f32[21,128,256]{2,1,0:T(8,128)S(1)}, f32[21,128,256]{2,1,0:T(8,128)}, u32[]{:S(2)}) copy-start(f32[21,128,256]{2,1,0:T(8,128)} %refs_19_.1) | copy-start | bytes 8257540
  0.7 19.2 %copy-start.14 = (s32[128]{0:T(128)S(1)}, s32[128]{0:T(128)}, u32[]{:S(2)}) copy-start(s32[128]{0:T(128)} %param.33) | copy-start | bytes 1540
  0.7 19.2 %copy-start.13 = (s32[128,1]{0,1:T(1,128)S(1)}, s32[128,1]{0,1:T(1,128)}, u32[]{:S(2)}) copy-start(s32[128,1]{0,1:T(1,128)} %param.32) | copy-start | bytes 1540
  0.7 19.2 %copy-start.12 = (s32[128]{0:T(128)S(1)}, s32[128]{0:T(128)}, u32[]{:S(2)}) copy-start(s32[128]{0:T(128)} %param.31) | copy-start | bytes 1540
  0.8 19.2 %copy-start.3 = (f32[4,9,9,256]{3,0,2,1:T(4,128)S(1)}, f32[4,9,9,256]{3,0,2,1:T(4,128)}, u32[]{:S(2)}) copy-start(f32[4,9,9,256]{3,0,2,1:T(4,128)} %param.27) | copy-start | bytes 995332
  10.3 9.5 %collective-permute-start = (f32[256,128]{1,0:T(8,128)S(1)}, f32[256,128]{1,0:T(8,128)S(1)}, u32[]{:S(2)}, u32[]{:S(2)}) collective-permute-start(f32[256,128]{1,0:T(8,128)S(1)} %get-tuple-element.43), channel_id=1, source_target_pairs={{0,1},{1,0},{2,3},{3,2},{4,8},{5,9},{6,10},{7,11},{8,4},{9,5},{10,... | collective-permute-start | bytes 393224 | tf_op jit(solution)/shard_map/ppermute | solution.py:769
  10.4 9.4 %collective-permute-start.1 = (f32[256,128]{1,0:T(8,128)S(1)}, f32[256,128]{1,0:T(8,128)S(1)}, u32[]{:S(2)}, u32[]{:S(2)}) collective-permute-start(f32[256,128]{1,0:T(8,128)S(1)} %get-tuple-element.44), channel_id=1, source_target_pairs={{0,4},{1,5},{2,6},{3,7},{4,0},{5,1},{6,2},{7,3},{8,12},{9,13},{10,... | collective-permute-start | bytes 393224 | tf_op jit(solution)/shard_map/ppermute | solution.py:769
  13.7 6.1 %collective-permute-start.2 = (f32[224,128]{1,0:T(8,128)S(1)}, f32[224,128]{1,0:T(8,128)S(1)}, u32[]{:S(2)}, u32[]{:S(2)}) collective-permute-start(f32[224,128]{1,0:T(8,128)S(1)} %get-tuple-element.45), channel_id=1, source_target_pairs={{0,4},{1,2},{2,1},{3,7},{4,0},{5,6},{6,5},{7,3},{8,12},{9,10},{10,... | collective-permute-start | bytes 344072 | tf_op jit(solution)/shard_map/ppermute | solution.py:769
  16.1 3.8 %collective-permute-start.3 = (f32[224,128]{1,0:T(8,128)S(1)}, f32[224,128]{1,0:T(8,128)S(1)}, u32[]{:S(2)}, u32[]{:S(2)}) collective-permute-start(f32[224,128]{1,0:T(8,128)S(1)} %get-tuple-element.46), channel_id=1, source_target_pairs={{0,1},{1,0},{2,3},{3,2},{4,5},{5,4},{6,7},{7,6},{8,9},{9,8},{10,11... | collective-permute-start | bytes 344072 | tf_op jit(solution)/shard_map/ppermute | solution.py:769
  31.3 21.5 %copy-start.17 = (f32[224,128]{1,0:T(8,128)S(1)}, f32[224,128]{1,0:T(8,128)}, u32[]{:S(2)}) copy-start(f32[224,128]{1,0:T(8,128)} %get-tuple-element.56) | copy-start | bytes 344068
  31.3 22.3 %copy-start.16 = (f32[224,128]{1,0:T(8,128)S(1)}, f32[224,128]{1,0:T(8,128)}, u32[]{:S(2)}) copy-start(f32[224,128]{1,0:T(8,128)} %get-tuple-element.57) | copy-start | bytes 344068
  31.3 23.3 %copy-start.15 = (f32[224,128]{1,0:T(8,128)S(1)}, f32[224,128]{1,0:T(8,128)}, u32[]{:S(2)}) copy-start(f32[224,128]{1,0:T(8,128)} %get-tuple-element.58) | copy-start | bytes 344068
  31.3 17.6 %all-to-all-start = ((f32[32,4,640]{2,1,0:T(4,128)}), f32[32,4,640]{2,1,0:T(4,128)S(1)}, u32[]{:S(2)}, u32[]{:S(2)}) async-start(f32[32,4,640]{2,1,0:T(4,128)} %get-tuple-element.70), calls=%async_computation | async-start | bytes 655360 | tf_op jit(solution)/shard_map/all_to_all | solution.py:868
  37.6 21.3 %collective-permute-start.4 = (f32[224,128]{1,0:T(8,128)}, f32[224,128]{1,0:T(8,128)S(1)}, u32[]{:S(2)}, u32[]{:S(2)}) collective-permute-start(f32[224,128]{1,0:T(8,128)} %get-tuple-element.55), channel_id=1, source_target_pairs={{0,1},{1,0},{2,3},{3,2},{4,8},{5,9},{6,10},{7,11},{8,4},{9,5},{10,... | collective-permute-start | bytes 344072 | tf_op jit(solution)/shard_map/ppermute | solution.py:769
  51.1 3.6 %collective-permute-start.8 = (f32[80,256]{1,0:T(8,128)S(1)}, f32[80,256]{1,0:T(8,128)S(1)}, u32[]{:S(2)}, u32[]{:S(2)}) collective-permute-start(f32[80,256]{1,0:T(8,128)S(1)} %get-tuple-element.74), channel_id=1, source_target_pairs={{0,1},{1,0},{2,3},{3,2},{4,8},{5,9},{6,10},{7,11},{8,4},{9,5},{10,... | collective-permute-start | bytes 245768 | tf_op jit(solution)/shard_map/ppermute | solution.py:769
  52.2 4.6 %collective-permute-start.9 = (f32[80,256]{1,0:T(8,128)S(1)}, f32[80,256]{1,0:T(8,128)S(1)}, u32[]{:S(2)}, u32[]{:S(2)}) collective-permute-start(f32[80,256]{1,0:T(8,128)S(1)} %get-tuple-element.75), channel_id=1, source_target_pairs={{0,4},{1,5},{2,6},{3,7},{4,0},{5,1},{6,2},{7,3},{8,12},{9,13},{10,... | collective-permute-start | bytes 245768 | tf_op jit(solution)/shard_map/ppermute | solution.py:769
  52.8 8.3 %collective-permute-start.5 = (f32[224,128]{1,0:T(8,128)S(1)}, f32[224,128]{1,0:T(8,128)S(1)}, u32[]{:S(2)}, u32[]{:S(2)}) collective-permute-start(f32[224,128]{1,0:T(8,128)S(1)} %copy-done.17), channel_id=1, source_target_pairs={{0,4},{1,5},{2,6},{3,7},{4,0},{5,1},{6,2},{7,3},{8,12},{9,13},{10,... | collective-permute-start | bytes 344072 | tf_op jit(solution)/shard_map/ppermute | solution.py:769
  53.6 7.5 %collective-permute-start.6 = (f32[224,128]{1,0:T(8,128)S(1)}, f32[224,128]{1,0:T(8,128)S(1)}, u32[]{:S(2)}, u32[]{:S(2)}) collective-permute-start(f32[224,128]{1,0:T(8,128)S(1)} %copy-done.16), channel_id=1, source_target_pairs={{0,4},{1,2},{2,1},{3,7},{4,0},{5,6},{6,5},{7,3},{8,12},{9,10},{10,... | collective-permute-start | bytes 344072 | tf_op jit(solution)/shard_map/ppermute | solution.py:769
  54.6 6.5 %collective-permute-start.7 = (f32[224,128]{1,0:T(8,128)S(1)}, f32[224,128]{1,0:T(8,128)S(1)}, u32[]{:S(2)}, u32[]{:S(2)}) collective-permute-start(f32[224,128]{1,0:T(8,128)S(1)} %copy-done.15), channel_id=1, source_target_pairs={{0,1},{1,0},{2,3},{3,2},{4,5},{5,4},{6,7},{7,6},{8,9},{9,8},{10,11... | collective-permute-start | bytes 344072 | tf_op jit(solution)/shard_map/ppermute | solution.py:769
  57.4 8.9 %copy-start.2 = (f32[5,272,256]{2,1,0:T(8,128)S(1)}, f32[5,272,256]{2,1,0:T(8,128)}, u32[]{:S(2)}) copy-start(f32[5,272,256]{2,1,0:T(8,128)} %get-tuple-element.81.refs_1_) | copy-start | bytes 4177924
  57.4 8.9 %copy-start.6 = (bf16[384,384]{1,0:T(8,128)(2,1)S(1)}, bf16[384,384]{1,0:T(8,128)(2,1)}, u32[]{:S(2)}) copy-start(bf16[384,384]{1,0:T(8,128)(2,1)} %constant.17.clone.refs_5_) | copy-start | bytes 884740
  57.4 8.9 %copy-start.7 = (bf16[384,384]{1,0:T(8,128)(2,1)S(1)}, bf16[384,384]{1,0:T(8,128)(2,1)}, u32[]{:S(2)}) copy-start(bf16[384,384]{1,0:T(8,128)(2,1)} %constant.16.clone.refs_4_) | copy-start | bytes 884740
  57.5 8.9 %collective-permute-start.10 = (f32[272,128]{1,0:T(8,128)S(1)}, f32[272,128]{1,0:T(8,128)S(1)}, u32[]{:S(2)}, u32[]{:S(2)}) collective-permute-start(f32[272,128]{1,0:T(8,128)S(1)} %get-tuple-element.82), channel_id=1, source_target_pairs={{0,4},{1,2},{2,1},{3,7},{4,0},{5,6},{6,5},{7,3},{8,12},{9,10},{10,... | collective-permute-start | bytes 417800 | tf_op jit(solution)/shard_map/ppermute | solution.py:769
  59.0 7.4 %collective-permute-start.11 = (f32[272,128]{1,0:T(8,128)S(1)}, f32[272,128]{1,0:T(8,128)S(1)}, u32[]{:S(2)}, u32[]{:S(2)}) collective-permute-start(f32[272,128]{1,0:T(8,128)S(1)} %get-tuple-element.83), channel_id=1, source_target_pairs={{0,1},{1,0},{2,3},{3,2},{4,5},{5,4},{6,7},{7,6},{8,9},{9,8},{10,11... | collective-permute-start | bytes 417800 | tf_op jit(solution)/shard_map/ppermute | solution.py:769

commit v4 on v3

--- a/solution.py
+++ b/solution.py
@@ -203,9 +203,10 @@
         combine(first, star_ref, moved_ref, total_ref, emit)
 
 
-def predict(star_ref, w_ref, moved_ref, term_ref, integ_ref, total_ref):
+def predict(star_ref, w_ref, moved_ref, term_ref, integ_ref, total_ref, awaited=()):
     integ_ref[...] = term_ref[...]
     mix(term_ref, 0, w_ref, moved_ref)
+    finish(awaited)
 
     def body(k, carry):
         scale = F32(-1.0 / ORDER)
@@ -368,8 +369,8 @@
     later = later + start(pairs, sem_ref, 6)
     finish(urgent[:1])
     prep_deriv(deriv_ref, w_ref)
-    finish(urgent[1:])
-    predict(star_ref, w_ref, moved_ref, term_ref, integ_ref, total_ref)
+    finish(urgent[1:2])
+    predict(star_ref, w_ref, moved_ref, term_ref, integ_ref, total_ref, urgent[2:])
     finish(later)
     prep_trace(trace_ref, place_ref, stage_ref, wt_ref)
     traces(integ_ref, wt_ref, own_ref)

time: 70.9 us -> 70.9 us (level)
  no operation moved by 1% of the time
where the time goes in v4:
time: 70.9 us; the launch traced here: 70.6 us
  Pallas kernels  42.7 us (60%)
  starting transfers between devices  21.9 us (31%)
  waiting for transfers between devices  4.71 us (7%)
  between operations  1.18 us (2%)
    pallas_call x9, Pallas kernels, call(): pl.pallas_call(body, in_specs=[spec(i in held) for i in range(len(args))]...  42.7 us
    ppermute x12, starting transfers between devices, swap(): return lax.ppermute(value, axes, pairs)  15.5 us
    all_to_all x1, starting transfers between devices, on_device(): lax.all_to_all(payload, ('gx', 'gy'), split_axis=0, concat_axis=0, tiled=...  6.34 us
    all_to_all x1, waiting for transfers between devices, on_device(): lax.all_to_all(payload, ('gx', 'gy'), split_axis=0, concat_axis=0, tiled=...  4.68 us
  transfers between devices with their start and end apart: 13, of which 1 were waited for; matrix products, arithmetic and copies ran while one was open for 0% of the time, Pallas kernels for 25%

profile of v4, /device:TPU:1, one launch (start us, length us, event | category | flops | bytes accessed | tf_op | source)
XLA Modules:
  0.0 70.6 jit_solution(17588862409437655831)
XLA Ops:
  0.6 0.0 copy-start.4
  0.7 0.0 copy-start
  0.7 0.0 copy-start.8
  0.8 0.0 copy-start.3
  0.8 9.5 %shard_map.221 = (bf16[168,192]{1,0:T(8,128)(2,1)S(1)}, bf16[288,192]{1,0:T(8,128)(2,1)S(1)}, f32[9,56,256]{2,1,0:T(8,128)S(1)}, f32[24,1024]{1,0:T(8,128)S(1)},...) custom-call(f32[9,56,256]{2,1,0:T(8,128)} %field_ref.1, ...), custom_call_target="tpu_custom_call" | custom-call | flops 1000000000 | bytes 30000000 | tf_op jit(solution)/shard_map/pallas_call | solution.py:88
  10.3 0.1 collective-permute-start
  10.4 3.3 %collective-permute-start.1 = (f32[256,128]{1,0:T(8,128)S(1)}, f32[256,128]{1,0:T(8,128)S(1)}, u32[]{:S(2)}, u32[]{:S(2)}) collective-permute-start(f32[256,128]{1,0:T(8,128)S(1)} %get-tuple-element.44), channel_id=1, source_target_pairs={{0,4},{1,5},{2,6},{3,7},{4,0},{5,1},{6,2},{7,3},{8,12},{9,13},{10,... | collective-permute-start | bytes 393224 | tf_op jit(solution)/shard_map/ppermute | solution.py:770
  13.6 2.3 %collective-permute-start.2 = (f32[224,128]{1,0:T(8,128)S(1)}, f32[224,128]{1,0:T(8,128)S(1)}, u32[]{:S(2)}, u32[]{:S(2)}) collective-permute-start(f32[224,128]{1,0:T(8,128)S(1)} %get-tuple-element.45), channel_id=1, source_target_pairs={{0,4},{1,2},{2,1},{3,7},{4,0},{5,6},{6,5},{7,3},{8,12},{9,10},{10,... | collective-permute-start | bytes 344072 | tf_op jit(solution)/shard_map/ppermute | solution.py:770
  16.0 3.7 %shard_map.222 = (f32[224,1024]{1,0:T(8,128)S(1)}, f32[9,56,256]{2,1,0:T(8,128)S(1)}, f32[8,512]{1,0:T(8,128)S(1)}, bf16[112,192]{1,0:T(8,128)(2,1)S(1)}, f32[8,...) custom-call(f32[9,56,256]{2,1,0:T(8,128)S(1)} %get-tuple-element.47., ...), custom_call_target="tpu_custom_call" | custom-call | flops 400000000 | bytes 12000000 | tf_op jit(solution)/shard_map/pallas_call | solution.py:88
  19.8 0.0 collective-permute-done.2.refs_2_
  19.8 0.0 collective-permute-done.1.refs_1_
  19.9 11.4 %shard_map.223 = (f32[32,4,640]{2,1,0:T(4,128)}, f32[9,56,256]{2,1,0:T(8,128)}, f32[9,56,256]{2,1,0:T(8,128)}, f32[32,128]{1,0:T(8,128)}, f32[32,128]{1,0:T(8,12...) custom-call(f32[256,128]{1,0:T(8,128)S(1)} %collective-permute-done.refs_0_, ...), custom_call_target="tpu_custom_call" | custom-call | flops 1200000000 | bytes 36000000 | tf_op jit(solution)/shard_map/pallas_call | solution.py:88
  31.3 6.3 %all-to-all-start = ((f32[32,4,640]{2,1,0:T(4,128)}), f32[32,4,640]{2,1,0:T(4,128)S(1)}, u32[]{:S(2)}, u32[]{:S(2)}) async-start(f32[32,4,640]{2,1,0:T(4,128)} %get-tuple-element.70), calls=%async_computation | async-start | bytes 655360 | tf_op jit(solution)/shard_map/all_to_all | solution.py:869
  37.6 0.5 collective-permute-start.4
  38.1 6.1 %shard_map.224 = (f32[5,272,256]{2,1,0:T(8,128)}, f32[272,128]{1,0:T(8,128)}, f32[272,128]{1,0:T(8,128)}, f32[224,1024]{1,0:T(8,128)}, f32[9,56,256]{2,1,0:T(8,128)}) custom-call(f32[3,256,256]{2,1,0:T(8,128)} %refs_0_.3, f32[256,256]{1,0:T(8,128)} %refs_1_.2, s32[256,256]{1,0:T(8,128)} %refs_2_.4, f32[32,128]{1,0:T(8,128)} %get-tuple-element.60.refs_3_, ...), custom_call_target="tpu_custom_call" | custom-call | flops 600000000 | bytes 18000000 | tf_op jit(solution)/shard_map/pallas_call | solution.py:88
  44.2 4.7 %all-to-all-done.refs_0_ = f32[32,4,640]{2,1,0:T(4,128)S(1)} async-done(((f32[32,4,640]{2,1,0:T(4,128)}), f32[32,4,640]{2,1,0:T(4,128)S(1)}, u32[]{:S(2)}, u32[]{:S(2)}) %all-to-all-start) | async-done | bytes 327712 | tf_op jit(solution)/shard_map/all_to_all | solution.py:869
  48.9 2.1 %shard_map.227 = (f32[2,256,256]{2,1,0:T(8,128)S(1)}, f32[80,256]{1,0:T(8,128)S(1)}, f32[80,256]{1,0:T(8,128)S(1)}, bf16[272,336]{1,0:T(8,128)(2,1)S(1)}, bf16[2...) custom-call(f32[32,4,640]{2,1,0:T(4,128)S(1)} %all-to-all-done.refs_0_, ...), custom_call_target="tpu_custom_call" | custom-call | flops 200000000 | bytes 6000000 | tf_op jit(solution)/shard_map/pallas_call | solution.py:88
  51.0 1.1 %collective-permute-start.8 = (f32[80,256]{1,0:T(8,128)S(1)}, f32[80,256]{1,0:T(8,128)S(1)}, u32[]{:S(2)}, u32[]{:S(2)}) collective-permute-start(f32[80,256]{1,0:T(8,128)S(1)} %get-tuple-element.74), channel_id=1, source_target_pairs={{0,1},{1,0},{2,3},{3,2},{4,8},{5,9},{6,10},{7,11},{8,4},{9,5},{10,... | collective-permute-start | bytes 245768 | tf_op jit(solution)/shard_map/ppermute | solution.py:770
  52.1 0.7 collective-permute-start.9
  52.8 0.8 %collective-permute-start.5 = (f32[224,128]{1,0:T(8,128)S(1)}, f32[224,128]{1,0:T(8,128)S(1)}, u32[]{:S(2)}, u32[]{:S(2)}) collective-permute-start(f32[224,128]{1,0:T(8,128)S(1)} %copy-done.17), channel_id=1, source_target_pairs={{0,4},{1,5},{2,6},{3,7},{4,0},{5,1},{6,2},{7,3},{8,12},{9,13},{10,... | collective-permute-start | bytes 344072 | tf_op jit(solution)/shard_map/ppermute | solution.py:770
  53.6 1.0 %collective-permute-start.6 = (f32[224,128]{1,0:T(8,128)S(1)}, f32[224,128]{1,0:T(8,128)S(1)}, u32[]{:S(2)}, u32[]{:S(2)}) collective-permute-start(f32[224,128]{1,0:T(8,128)S(1)} %copy-done.16), channel_id=1, source_target_pairs={{0,4},{1,2},{2,1},{3,7},{4,0},{5,6},{6,5},{7,3},{8,12},{9,10},{10,... | collective-permute-start | bytes 344072 | tf_op jit(solution)/shard_map/ppermute | solution.py:770
  54.6 2.1 %collective-permute-start.7 = (f32[224,128]{1,0:T(8,128)S(1)}, f32[224,128]{1,0:T(8,128)S(1)}, u32[]{:S(2)}, u32[]{:S(2)}) collective-permute-start(f32[224,128]{1,0:T(8,128)S(1)} %copy-done.15), channel_id=1, source_target_pairs={{0,1},{1,0},{2,3},{3,2},{4,5},{5,4},{6,7},{7,6},{8,9},{9,8},{10,11... | collective-permute-start | bytes 344072 | tf_op jit(solution)/shard_map/ppermute | solution.py:770
  56.7 0.0 collective-permute-done.9.refs_2_
  56.7 0.7 shard_map.228
  57.4 0.0 copy-start.6
  57.4 0.0 copy-start.7
  57.4 1.5 %collective-permute-start.10 = (f32[272,128]{1,0:T(8,128)S(1)}, f32[272,128]{1,0:T(8,128)S(1)}, u32[]{:S(2)}, u32[]{:S(2)}) collective-permute-start(f32[272,128]{1,0:T(8,128)S(1)} %get-tuple-element.82), channel_id=1, source_target_pairs={{0,4},{1,2},{2,1},{3,7},{4,0},{5,6},{6,5},{7,3},{8,12},{9,10},{10,... | collective-permute-start | bytes 417800 | tf_op jit(solution)/shard_map/ppermute | solution.py:770
  58.9 0.0 collective-permute-done.4.refs_0_
  58.9 2.2 %collective-permute-start.11 = (f32[272,128]{1,0:T(8,128)S(1)}, f32[272,128]{1,0:T(8,128)S(1)}, u32[]{:S(2)}, u32[]{:S(2)}) collective-permute-start(f32[272,128]{1,0:T(8,128)S(1)} %get-tuple-element.83), channel_id=1, source_target_pairs={{0,1},{1,0},{2,3},{3,2},{4,5},{5,4},{6,7},{7,6},{8,9},{9,8},{10,11... | collective-permute-start | bytes 417800 | tf_op jit(solution)/shard_map/ppermute | solution.py:770
  61.1 2.3 %shard_map.225.part_ref = f32[224,1024]{1,0:T(8,128)S(1)} custom-call(f32[224,128]{1,0:T(8,128)S(1)} %collective-permute-done.4.refs_0_, f32[224,128]{1,0:T(8,128)S(1)} %collective-permute-done.5.refs_1_, f32[224,128]{1,0:T(8,128)S(1)} %collective-permute-done.6.refs_2_, f32[224,128]{1,0:T(8,128)S(1)} %collective-permute-done.7.refs_3_, ...), custom_call_target="tpu_custom_call" | custom-call | flops 200000000 | bytes 6000000 | tf_op jit(solution)/shard_map/pallas_call | solution.py:88
  63.4 2.9 %shard_map.226 = f32[9,56,256]{2,1,0:T(8,128)} custom-call(f32[224,1024]{1,0:T(8,128)S(1)} %shard_map.225.part_ref, f32[9,9,4,256]{3,2,1,0:T(4,128)} %bitcast.11, bf16[112,192]{1,0:T(8,128)(2,1)} %get-tuple-element.68.wl_hbm, f32[9,56,256]{2,1,0:T(8,128)} %get-tuple-element.69.base_hbm), custom_call_target="tpu_custom_call" | custom-call | flops 200000000 | bytes 6000000 | tf_op jit(solution)/shard_map/pallas_call | solution.py:88
  66.3 4.1 %shard_map.229 = f32[3,256,256]{2,1,0:T(8,128)} custom-call(f32[2,272,256]{2,1,0:T(8,128)S(1)} %get-tuple-element.80.refs_0_, f32[5,272,256]{2,1,0:T(8,128)S(1)} %copy-done.2, f32[272,128]{1,0:T(8,128)S(1)} %collective-permute-done.10.refs_2_, f32[272,128]{1,0:T(8,128)S(1)} %collective-permute-done.11.refs_3_, bf16[384,384]{1,0:T(8,128)(2,1)S(1)} %copy-done.7, ...), custom_call_target="tpu_custom_call" | custom-call | flops 400000000 | bytes 12000000 | tf_op jit(solution)/shard_map/pallas_call | solution.py:88
  (39 shorter events, 0.1 us)
Async XLA Ops:
  0.6 19.2 %copy-start.4 = (bf16[448,224]{1,0:T(8,128)(2,1)S(1)}, bf16[448,224]{1,0:T(8,128)(2,1)}, u32[]{:S(2)}) copy-start(bf16[448,224]{1,0:T(8,128)(2,1)} %constant.13.clone.refs_8_.refs_7_) | copy-start | bytes 602116
  0.6 19.2 %copy-start.11 = (s32[1,1,4,128]{3,2,1,0:T(4,128)S(1)}, s32[1,1,4,128]{3,2,1,0:T(4,128)}, u32[]{:S(2)}) copy-start(s32[1,1,4,128]{3,2,1,0:T(4,128)} %refs_14_.1) | copy-start | bytes 6148
  0.7 15.3 %copy-start.5 = (f32[9,56,256]{2,1,0:T(8,128)S(1)}, f32[9,56,256]{2,1,0:T(8,128)}, u32[]{:S(2)}) copy-start(f32[9,56,256]{2,1,0:T(8,128)} %field_ref.1) | copy-start | bytes 1548292
  0.7 15.3 %copy-start = (f32[3,9,9,256]{3,0,2,1:T(4,128)S(1)}, f32[3,9,9,256]{3,0,2,1:T(4,128)}, u32[]{:S(2)}) copy-start(f32[3,9,9,256]{3,0,2,1:T(4,128)} %param.23) | copy-start | bytes 746500
  0.7 15.3 %copy-start.8 = (s32[4,256]{1,0:T(4,128)S(1)}, s32[4,256]{1,0:T(4,128)}, u32[]{:S(2)}) copy-start(s32[4,256]{1,0:T(4,128)} %refs_5_.6) | copy-start | bytes 12292
  0.7 15.3 %copy-start.10 = (s32[4,256]{1,0:T(4,128)S(1)}, s32[4,256]{1,0:T(4,128)}, u32[]{:S(2)}) copy-start(s32[4,256]{1,0:T(4,128)} %orient_ref.1) | copy-start | bytes 12292
  0.7 15.3 %copy-start.9 = (f32[4,21,56]{2,0,1:T(4,128)S(1)}, f32[4,21,56]{2,0,1:T(4,128)}, u32[]{:S(2)}) copy-start(f32[4,21,56]{2,0,1:T(4,128)} %param.26) | copy-start | bytes 56452
  0.7 19.1 %copy-start.1 = (f32[21,128,256]{2,1,0:T(8,128)S(1)}, f32[21,128,256]{2,1,0:T(8,128)}, u32[]{:S(2)}) copy-start(f32[21,128,256]{2,1,0:T(8,128)} %refs_19_.1) | copy-start | bytes 8257540
  0.7 19.1 %copy-start.14 = (s32[128]{0:T(128)S(1)}, s32[128]{0:T(128)}, u32[]{:S(2)}) copy-start(s32[128]{0:T(128)} %param.33) | copy-start | bytes 1540
  0.7 19.1 %copy-start.13 = (s32[128,1]{0,1:T(1,128)S(1)}, s32[128,1]{0,1:T(1,128)}, u32[]{:S(2)}) copy-start(s32[128,1]{0,1:T(1,128)} %param.32) | copy-start | bytes 1540
  0.7 19.1 %copy-start.12 = (s32[128]{0:T(128)S(1)}, s32[128]{0:T(128)}, u32[]{:S(2)}) copy-start(s32[128]{0:T(128)} %param.31) | copy-start | bytes 1540
  0.8 19.1 %copy-start.3 = (f32[4,9,9,256]{3,0,2,1:T(4,128)S(1)}, f32[4,9,9,256]{3,0,2,1:T(4,128)}, u32[]{:S(2)}) copy-start(f32[4,9,9,256]{3,0,2,1:T(4,128)} %param.27) | copy-start | bytes 995332
  10.3 9.5 %collective-permute-start = (f32[256,128]{1,0:T(8,128)S(1)}, f32[256,128]{1,0:T(8,128)S(1)}, u32[]{:S(2)}, u32[]{:S(2)}) collective-permute-start(f32[256,128]{1,0:T(8,128)S(1)} %get-tuple-element.43), channel_id=1, source_target_pairs={{0,1},{1,0},{2,3},{3,2},{4,8},{5,9},{6,10},{7,11},{8,4},{9,5},{10,... | collective-permute-start | bytes 393224 | tf_op jit(solution)/shard_map/ppermute | solution.py:770
  10.4 9.4 %collective-permute-start.1 = (f32[256,128]{1,0:T(8,128)S(1)}, f32[256,128]{1,0:T(8,128)S(1)}, u32[]{:S(2)}, u32[]{:S(2)}) collective-permute-start(f32[256,128]{1,0:T(8,128)S(1)} %get-tuple-element.44), channel_id=1, source_target_pairs={{0,4},{1,5},{2,6},{3,7},{4,0},{5,1},{6,2},{7,3},{8,12},{9,13},{10,... | collective-permute-start | bytes 393224 | tf_op jit(solution)/shard_map/ppermute | solution.py:770
  13.6 6.1 %collective-permute-start.2 = (f32[224,128]{1,0:T(8,128)S(1)}, f32[224,128]{1,0:T(8,128)S(1)}, u32[]{:S(2)}, u32[]{:S(2)}) collective-permute-start(f32[224,128]{1,0:T(8,128)S(1)} %get-tuple-element.45), channel_id=1, source_target_pairs={{0,4},{1,2},{2,1},{3,7},{4,0},{5,6},{6,5},{7,3},{8,12},{9,10},{10,... | collective-permute-start | bytes 344072 | tf_op jit(solution)/shard_map/ppermute | solution.py:770
  16.0 3.8 %collective-permute-start.3 = (f32[224,128]{1,0:T(8,128)S(1)}, f32[224,128]{1,0:T(8,128)S(1)}, u32[]{:S(2)}, u32[]{:S(2)}) collective-permute-start(f32[224,128]{1,0:T(8,128)S(1)} %get-tuple-element.46), channel_id=1, source_target_pairs={{0,1},{1,0},{2,3},{3,2},{4,5},{5,4},{6,7},{7,6},{8,9},{9,8},{10,11... | collective-permute-start | bytes 344072 | tf_op jit(solution)/shard_map/ppermute | solution.py:770
  31.2 21.6 %copy-start.17 = (f32[224,128]{1,0:T(8,128)S(1)}, f32[224,128]{1,0:T(8,128)}, u32[]{:S(2)}) copy-start(f32[224,128]{1,0:T(8,128)} %get-tuple-element.56) | copy-start | bytes 344068
  31.3 22.3 %copy-start.16 = (f32[224,128]{1,0:T(8,128)S(1)}, f32[224,128]{1,0:T(8,128)}, u32[]{:S(2)}) copy-start(f32[224,128]{1,0:T(8,128)} %get-tuple-element.57) | copy-start | bytes 344068
  31.3 23.4 %copy-start.15 = (f32[224,128]{1,0:T(8,128)S(1)}, f32[224,128]{1,0:T(8,128)}, u32[]{:S(2)}) copy-start(f32[224,128]{1,0:T(8,128)} %get-tuple-element.58) | copy-start | bytes 344068
  31.3 17.6 %all-to-all-start = ((f32[32,4,640]{2,1,0:T(4,128)}), f32[32,4,640]{2,1,0:T(4,128)S(1)}, u32[]{:S(2)}, u32[]{:S(2)}) async-start(f32[32,4,640]{2,1,0:T(4,128)} %get-tuple-element.70), calls=%async_computation | async-start | bytes 655360 | tf_op jit(solution)/shard_map/all_to_all | solution.py:869
  37.6 21.3 %collective-permute-start.4 = (f32[224,128]{1,0:T(8,128)}, f32[224,128]{1,0:T(8,128)S(1)}, u32[]{:S(2)}, u32[]{:S(2)}) collective-permute-start(f32[224,128]{1,0:T(8,128)} %get-tuple-element.55), channel_id=1, source_target_pairs={{0,1},{1,0},{2,3},{3,2},{4,8},{5,9},{6,10},{7,11},{8,4},{9,5},{10,... | collective-permute-start | bytes 344072 | tf_op jit(solution)/shard_map/ppermute | solution.py:770
  51.0 3.6 %collective-permute-start.8 = (f32[80,256]{1,0:T(8,128)S(1)}, f32[80,256]{1,0:T(8,128)S(1)}, u32[]{:S(2)}, u32[]{:S(2)}) collective-permute-start(f32[80,256]{1,0:T(8,128)S(1)} %get-tuple-element.74), channel_id=1, source_target_pairs={{0,1},{1,0},{2,3},{3,2},{4,8},{5,9},{6,10},{7,11},{8,4},{9,5},{10,... | collective-permute-start | bytes 245768 | tf_op jit(solution)/shard_map/ppermute | solution.py:770
  52.1 4.6 %collective-permute-start.9 = (f32[80,256]{1,0:T(8,128)S(1)}, f32[80,256]{1,0:T(8,128)S(1)}, u32[]{:S(2)}, u32[]{:S(2)}) collective-permute-start(f32[80,256]{1,0:T(8,128)S(1)} %get-tuple-element.75), channel_id=1, source_target_pairs={{0,4},{1,5},{2,6},{3,7},{4,0},{5,1},{6,2},{7,3},{8,12},{9,13},{10,... | collective-permute-start | bytes 245768 | tf_op jit(solution)/shard_map/ppermute | solution.py:770
  52.8 8.3 %collective-permute-start.5 = (f32[224,128]{1,0:T(8,128)S(1)}, f32[224,128]{1,0:T(8,128)S(1)}, u32[]{:S(2)}, u32[]{:S(2)}) collective-permute-start(f32[224,128]{1,0:T(8,128)S(1)} %copy-done.17), channel_id=1, source_target_pairs={{0,4},{1,5},{2,6},{3,7},{4,0},{5,1},{6,2},{7,3},{8,12},{9,13},{10,... | collective-permute-start | bytes 344072 | tf_op jit(solution)/shard_map/ppermute | solution.py:770
  53.6 7.5 %collective-permute-start.6 = (f32[224,128]{1,0:T(8,128)S(1)}, f32[224,128]{1,0:T(8,128)S(1)}, u32[]{:S(2)}, u32[]{:S(2)}) collective-permute-start(f32[224,128]{1,0:T(8,128)S(1)} %copy-done.16), channel_id=1, source_target_pairs={{0,4},{1,2},{2,1},{3,7},{4,0},{5,6},{6,5},{7,3},{8,12},{9,10},{10,... | collective-permute-start | bytes 344072 | tf_op jit(solution)/shard_map/ppermute | solution.py:770
  54.6 6.5 %collective-permute-start.7 = (f32[224,128]{1,0:T(8,128)S(1)}, f32[224,128]{1,0:T(8,128)S(1)}, u32[]{:S(2)}, u32[]{:S(2)}) collective-permute-start(f32[224,128]{1,0:T(8,128)S(1)} %copy-done.15), channel_id=1, source_target_pairs={{0,1},{1,0},{2,3},{3,2},{4,5},{5,4},{6,7},{7,6},{8,9},{9,8},{10,11... | collective-permute-start | bytes 344072 | tf_op jit(solution)/shard_map/ppermute | solution.py:770
  57.4 8.9 %copy-start.2 = (f32[5,272,256]{2,1,0:T(8,128)S(1)}, f32[5,272,256]{2,1,0:T(8,128)}, u32[]{:S(2)}) copy-start(f32[5,272,256]{2,1,0:T(8,128)} %get-tuple-element.81.refs_1_) | copy-start | bytes 4177924
  57.4 8.9 %copy-start.6 = (bf16[384,384]{1,0:T(8,128)(2,1)S(1)}, bf16[384,384]{1,0:T(8,128)(2,1)}, u32[]{:S(2)}) copy-start(bf16[384,384]{1,0:T(8,128)(2,1)} %constant.17.clone.refs_5_) | copy-start | bytes 884740
  57.4 8.9 %copy-start.7 = (bf16[384,384]{1,0:T(8,128)(2,1)S(1)}, bf16[384,384]{1,0:T(8,128)(2,1)}, u32[]{:S(2)}) copy-start(bf16[384,384]{1,0:T(8,128)(2,1)} %constant.16.clone.refs_4_) | copy-start | bytes 884740
  57.4 8.9 %collective-permute-start.10 = (f32[272,128]{1,0:T(8,128)S(1)}, f32[272,128]{1,0:T(8,128)S(1)}, u32[]{:S(2)}, u32[]{:S(2)}) collective-permute-start(f32[272,128]{1,0:T(8,128)S(1)} %get-tuple-element.82), channel_id=1, source_target_pairs={{0,4},{1,2},{2,1},{3,7},{4,0},{5,6},{6,5},{7,3},{8,12},{9,10},{10,... | collective-permute-start | bytes 417800 | tf_op jit(solution)/shard_map/ppermute | solution.py:770
  58.9 7.4 %collective-permute-start.11 = (f32[272,128]{1,0:T(8,128)S(1)}, f32[272,128]{1,0:T(8,128)S(1)}, u32[]{:S(2)}, u32[]{:S(2)}) collective-permute-start(f32[272,128]{1,0:T(8,128)S(1)} %get-tuple-element.83), channel_id=1, source_target_pairs={{0,1},{1,0},{2,3},{3,2},{4,5},{5,4},{6,7},{7,6},{8,9},{9,8},{10,11... | collective-permute-start | bytes 417800 | tf_op jit(solution)/shard_map/ppermute | solution.py:770
